TPU v7x, 256 devices: a whole 4x4x8 slice. The times are simulated.
256 devices in a mesh: slab: 32 (over z_lo, y, core), grp: 8 (over z_hi, x).
Axes of the slice: x: 4, y: 4, z: 8 (z_hi: 2, z_lo: 4; z = z_hi * 4 + z_lo), core: 2. Of those that a mesh axis runs over, the one named last changes fastest.
Arguments:
- volume: float32 [64, 128, 32, 128], P(None, 'slab', 'grp'), may hold values from -6 to 6
- conv_fine: float32 [3, 3, 3, 64, 64], replicated, may hold values from -0.15625 to 0.15625
- down_first: float32 [2, 2, 2, 64, 128], replicated, may hold values from -0.25 to 0.25
- conv_middle: float32 [3, 3, 3, 128, 128], replicated, may hold values from -0.109375 to 0.109375
- down_second: float32 [2, 2, 2, 128, 256], P(None, None, None, None, 'grp'), may hold values from -0.1875 to 0.1875
- conv_coarse: float32 [3, 3, 3, 256, 512], P(None, None, None, None, 'grp'), may hold values from -0.078125 to 0.078125
Outputs:
- features: float32 [512, 32, 256], P('grp', 'slab')
All inputs are finite; a program needn't handle non-finite values.
Results may differ from a plain program's by a relative error of at most 0.000082.
Values sent between devices are 32-bit elements; how exact they have to be, the bound alone decides.
No kernel may reach another device: no remote copies, remote signals or barrier semaphores. Data moves between devices by JAX's collectives and lax.ppermute only.
A program may use at most 64 MiB of HBM per device.

v0:
```python
import functools

import jax
import jax.numpy as jnp
from jax import lax
from jax.experimental import pallas as pl
from jax.experimental.pallas import tpu as pltpu
from jax.sharding import PartitionSpec as P

F32 = jnp.float32
BF16 = jnp.bfloat16
XORS = (0, 4, 1, 5, 2, 6, 3, 7)


def split(x):
    hi = x.astype(BF16)
    return hi, (x - hi.astype(F32)).astype(BF16)


def mm(a, b):
    return lax.dot_general(a, b, (((1,), (0,)), ((), ())), preferred_element_type=F32)


def mm_t(a, b):
    return lax.dot_general(a, b, (((1,), (1,)), ((), ())), preferred_element_type=F32)


def gelu(v):
    return v * (1.0 + lax.erf(v * 0.7071067811865476)) * 0.5


def call(kernel, outs, args, scratch=(), flops=0):
    vmem = pl.BlockSpec(memory_space=pltpu.VMEM)
    size = sum(a.size * a.dtype.itemsize for a in args)
    return pl.pallas_call(
        kernel,
        out_shape=[jax.ShapeDtypeStruct(s, t) for s, t in outs],
        in_specs=[vmem] * len(args),
        out_specs=[vmem] * len(outs),
        scratch_shapes=list(scratch),
        compiler_params=pltpu.CompilerParams(vmem_limit_bytes=16 * 2**20),
        cost_estimate=pl.CostEstimate(flops=flops, bytes_accessed=size, transcendentals=0),
        name=kernel.__name__,
    )(*args)


def edges(vol, w2, low, high, half):
    for d in range(4):
        low[d * 64 : d * 64 + 64, :] = vol[pl.ds(d * 4, 64, stride=16), :]
        high[d * 64 : d * 64 + 64, :] = vol[pl.ds(d * 4 + 3, 64, stride=16), :]
    part = lax.rem(lax.axis_index("slab"), 2)
    half[...] = w2[pl.ds(pl.multiple_of(part * 128, 128), 128), :]


def put_shifted(x, high, low, lead, row, lane):
    column = lax.broadcasted_iota(jnp.int32, x.shape, 1)
    for k in range(3):
        if k == 0:
            y = jnp.where(column == 0, 0.0, pltpu.roll(x, 1, 1))
        elif k == 1:
            y = x
        else:
            y = jnp.where(column == 127, 0.0, pltpu.roll(x, 127, 1))
        hi, lo = split(y)
        high[lead, row + 64 * k : row + 64 * k + 64, lane : lane + 128] = hi
        low[lead, row + 64 * k : row + 64 * k + 64, lane : lane + 128] = lo


def taps(weights, high, low):
    both = mm(weights, high)
    return both[:192] + both[192:] + mm(weights[:192], low)


def planes(first, second):
    by_depth = [first[:, :128], first[:, 128:], second[:, :128], second[:, 128:]]
    sums = []
    for out in range(-1, 5):
        terms = [by_depth[out + a - 1][a * 64 : a * 64 + 64] for a in range(3) if 0 <= out + a - 1 < 4]
        sums.append(functools.reduce(jnp.add, terms))
    return sums


def fine_own(vol, w1, acc, wt, high, low):
    zeros = jnp.zeros((64, 256), BF16)
    for lead in range(2):
        for h in range(4):
            high[lead, h * 256 + 192 : h * 256 + 256, :] = zeros
            low[lead, h * 256 + 192 : h * 256 + 256, :] = zeros
    for b in range(3):
        wt[:, b * 256 + 192 : b * 256 + 256] = jnp.zeros((384, 64), BF16)
    for a in range(3):
        for b in range(3):
            x = w1[a * 576 + b * 192 : a * 576 + b * 192 + 192, :]
            x = jnp.concatenate([x, jnp.zeros((64, 64), F32)], axis=0)
            hi, lo = split(x.T)
            wt[a * 64 : a * 64 + 64, b * 256 : b * 256 + 256] = hi
            wt[192 + a * 64 : 192 + a * 64 + 64, b * 256 : b * 256 + 256] = lo
    for d in range(4):
        for h in range(4):
            put_shifted(vol[pl.ds(d * 4 + h, 64, stride=16), :], high, low, d // 2, h * 256, d % 2 * 128)
    for h in range(4):
        first, last = max(h - 1, 0), min(h + 1, 3)
        rows = slice(first * 256, last * 256 + 256)
        lanes = slice((first - h + 1) * 256, (last - h + 2) * 256)
        weights = wt[:, lanes]
        parts = [taps(weights, high[lead, rows, :], low[lead, rows, :]) for lead in range(2)]
        for i, value in enumerate(planes(*parts)):
            acc[i * 256 + h * 64 : i * 256 + h * 64 + 64, :] = value


def fine_rim(acc, wt, below, above, inner, down, up, high, low):
    grp = lax.axis_index("grp")
    zeros = jnp.zeros((64, 256), BF16)
    for side in range(2):
        ref = (below, above)[side]
        h = (0, 3)[side]
        inside = (grp > 0, grp < lax.axis_size("grp") - 1)[side]
        for lead in range(2):
            high[lead, 192:256, :] = zeros
            low[lead, 192:256, :] = zeros
        for d in range(4):
            x = jnp.where(inside, ref[d * 64 : d * 64 + 64, :], 0.0)
            put_shifted(x, high, low, d // 2, 0, d % 2 * 128)
        weights = wt[:, side * 512 : side * 512 + 256]
        parts = [taps(weights, high[lead], low[lead]) for lead in range(2)]
        for i, value in enumerate(planes(*parts)):
            total = value + acc[i * 256 + h * 64 : i * 256 + h * 64 + 64, :]
            if i == 0:
                down[h * 64 : h * 64 + 64, :] = total
            elif i == 5:
                up[h * 64 : h * 64 + 64, :] = total
            else:
                at = (i - 1) * 128 + side * 64
                inner[at : at + 64, :] = total
    for h in (1, 2):
        down[h * 64 : h * 64 + 64, :] = acc[h * 64 : h * 64 + 64, :]
        up[h * 64 : h * 64 + 64, :] = acc[5 * 256 + h * 64 : 5 * 256 + h * 64 + 64, :]


def first_down(acc, inner, before, after, w, out_low, out_high, cells, whi, wlo):
    slab = lax.axis_index("slab")
    for a in range(2):
        for bk in range(4):
            hi, lo = split(w[(a * 4 + bk) * 64 : (a * 4 + bk) * 64 + 64, :])
            whi[(bk * 2 + a) * 64 : (bk * 2 + a) * 64 + 64, :] = hi
            wlo[(bk * 2 + a) * 64 : (bk * 2 + a) * 64 + 64, :] = lo
    for h in range(4):
        level = []
        for d in range(4):
            if h in (0, 3):
                at = d * 128 + (h == 3) * 64
                v = inner[at : at + 64, :]
            else:
                at = (d + 1) * 256 + h * 64
                v = acc[at : at + 64, :]
            if d == 0:
                v = v + jnp.where(slab > 0, before[h * 64 : h * 64 + 64, :], 0.0)
            if d == 3:
                v = v + jnp.where(slab < lax.axis_size("slab") - 1, after[h * 64 : h * 64 + 64, :], 0.0)
            level.append(gelu(v))
        for d2 in range(2):
            cells[h * 2 + d2] = jnp.concatenate(level[2 * d2 : 2 * d2 + 2], axis=0).T
    for h2 in range(2):
        rows = []
        for d2 in range(2):
            rows.append(jnp.concatenate(
                [cells[(2 * h2 + b) * 2 + d2, pl.ds(k, 64, stride=2), :] for b in range(2) for k in range(2)], axis=1))
        hi, lo = split(jnp.concatenate(rows, axis=0))
        both = mm(jnp.concatenate([hi, lo], axis=0), whi[...])
        (out_low, out_high)[h2][...] = both[:128] + both[128:] + mm(hi, wlo[...])


def filters(wm, wc, mid, coarse):
    for a in range(3):
        for i in range(9):
            x = wm[(a * 9 + i) * 128 : (a * 9 + i) * 128 + 128, :]
            hi, lo = split(x)
            mid[i * 128 : i * 128 + 128, a * 128 : a * 128 + 128] = hi
            mid[1152 + i * 128 : 1152 + i * 128 + 128, a * 128 : a * 128 + 128] = lo
            hi, lo = split(wc[(a * 9 + i) * 64 : (a * 9 + i) * 64 + 64, :])
            coarse[a * 64 : a * 64 + 64, i * 256 : i * 256 + 256] = hi
            coarse[192 + a * 64 : 192 + a * 64 + 64, i * 256 : i * 256 + 256] = lo


def gathered_filters(mine, other, whi, wlo):
    grp = lax.axis_index("grp")
    part = lax.rem(lax.axis_index("slab"), 2)
    for ref, half in ((mine, part), (other, 1 - part)):
        for j, mask in enumerate(XORS):
            at = pl.multiple_of((grp ^ mask) * 32, 32)
            for i in range(4):
                hi, lo = split(ref[j * 128 + i * 32 : j * 128 + i * 32 + 32, :])
                whi[half, pl.ds(at, 32), i * 128 : i * 128 + 128] = hi
                wlo[half, pl.ds(at, 32), i * 128 : i * 128 + 128] = lo


def shifted_rows(x, k, width):
    row = lax.rem(lax.broadcasted_iota(jnp.int32, x.shape, 0), width)
    if k == 0:
        return jnp.where(row == 0, 0.0, pltpu.roll(x, 1, 0))
    if k == 2:
        return jnp.where(row == width - 1, 0.0, pltpu.roll(x, x.shape[0] - 1, 0))
    return x


def middle(d_low, d_high, below, above, w, inner, down, up, high, low):
    grp = lax.axis_index("grp")
    for i, ref in enumerate((below, d_low, d_high, above)):
        for d in range(2):
            x = ref[d * 64 : d * 64 + 64, :]
            if i == 0:
                x = jnp.where(grp > 0, x, 0.0)
            if i == 3:
                x = jnp.where(grp < lax.axis_size("grp") - 1, x, 0.0)
            for k in range(3):
                hi, lo = split(shifted_rows(x, k, 64))
                high[d, i * 64 : i * 64 + 64, k * 128 : k * 128 + 128] = hi
                low[d, i * 64 : i * 64 + 64, k * 128 : k * 128 + 128] = lo
    total = jnp.zeros((256, 384), F32)
    for b in range(3):
        rows = slice(b * 64, b * 64 + 128)
        hi = [high[d, rows, :] for d in range(2)]
        lo = [low[d, rows, :] for d in range(2)]
        both = mm(jnp.concatenate(hi + lo, axis=0), w[b * 384 : b * 384 + 384, :])
        rest = mm(jnp.concatenate(hi, axis=0), w[1152 + b * 384 : 1152 + b * 384 + 384, :])
        total = total + (both[:256] + both[256:] + rest)
    inner[:128, :] = total[:128, 128:256] + total[128:, 256:]
    inner[128:, :] = total[:128, :128] + total[128:, 128:256]
    down[...] = total[:128, 256:]
    up[...] = total[128:, :128]


def second_down(inner, before, after, whi, wlo, out, cells):
    slab = lax.axis_index("slab")
    first = inner[:128, :] + jnp.where(slab > 0, before[...], 0.0)
    second = inner[128:, :] + jnp.where(slab < lax.axis_size("slab") - 1, after[...], 0.0)
    cells[:128, :] = gelu(first)
    cells[128:, :] = gelu(second)
    total = jnp.zeros((32, 256), F32)
    for a in range(2):
        x = jnp.concatenate(
            [cells[pl.ds(a * 128 + b * 64 + k, 32, stride=2), :] for b in range(2) for k in range(2)], axis=1)
        hi, lo = split(x)
        both = mm_t(jnp.concatenate([hi, lo], axis=0), whi[a])
        total = total + (both[:32] + both[32:] + mm_t(hi, wlo[a]))
    out[...] = total


def coarse_conv(own, one, two, three, w, down, mid, up, grid, high, low):
    grp = lax.axis_index("grp")
    base, x = grp & 4, grp & 3
    for r, ref in enumerate((own, one, two, three)):
        source = base + ((x - r) & 3)
        for j in range(2):
            at = pl.multiple_of((source ^ (4 * j)) * 32, 32)
            grid[pl.ds(at, 32), :] = ref[j * 32 : j * 32 + 32, :]
    zeros = jnp.zeros((32, 768), BF16)
    for ref in (high, low):
        ref[:32, :] = zeros
        ref[288:, :] = zeros
    for k in range(3):
        hi, lo = split(shifted_rows(grid[...], k, 32))
        high[32:288, k * 256 : k * 256 + 256] = hi
        low[32:288, k * 256 : k * 256 + 256] = lo
    total = jnp.zeros((192, 256), F32)
    for b in range(3):
        rows, lanes = slice(b * 32, b * 32 + 256), slice(b * 768, b * 768 + 768)
        both = mm_t(w[:, lanes], high[rows, :])
        total = total + (both[:192] + both[192:] + mm_t(w[:192, lanes], low[rows, :]))
    up[...] = total[:64]
    mid[...] = total[64:128]
    down[...] = total[128:]


def finish(mid, before, after, out):
    slab = lax.axis_index("slab")
    v = mid[...] + jnp.where(slab > 0, before[...], 0.0)
    v = v + jnp.where(slab < lax.axis_size("slab") - 1, after[...], 0.0)
    out[...] = gelu(v)


def per_device(volume, conv_fine, down_first, conv_middle, down_second, conv_coarse):
    slabs, grps = lax.axis_size("slab"), lax.axis_size("grp")

    def turn(x, axis, by):
        n = lax.axis_size(axis)
        return lax.ppermute(x, axis, [(i, (i + by) % n) for i in range(n)])

    def swap(x, axis, mask):
        n = lax.axis_size(axis)
        return lax.ppermute(x, axis, [(i, i ^ mask) for i in range(n)])

    def turn_x(x, by):
        return lax.ppermute(x, "grp", [(i, (i & 4) | ((i + by) & 3)) for i in range(grps)])

    vol = volume.reshape(1024, 128)
    w1 = conv_fine.reshape(1728, 64)
    wd1 = down_first.reshape(512, 128)
    wm = conv_middle.reshape(3456, 128)
    w2 = jnp.swapaxes(down_second, 3, 4).reshape(256, 128)
    wc = jnp.swapaxes(conv_coarse, 3, 4).reshape(1728, 256)

    low, high, half = call(edges, [((256, 128), F32), ((256, 128), F32), ((128, 128), F32)], (vol, w2))
    below, above = turn(high, "grp", 1), turn(low, "grp", -1)
    taken = [pltpu.VMEM((2, 1024, 256), BF16)] * 2
    acc, wt = call(fine_own, [((1536, 128), F32), ((384, 768), BF16)], (vol, w1), taken, flops=10**9)
    mid_w, coarse_w = call(filters, [((2304, 384), BF16), ((384, 2304), BF16)], (wm, wc), flops=10**8)

    two = jnp.concatenate([half, swap(half, "grp", 4)], axis=0)
    four = jnp.concatenate([two, swap(two, "grp", 1)], axis=0)
    mine = jnp.concatenate([four, swap(four, "grp", 2)], axis=0)
    other = swap(mine, "slab", 1)
    whi, wlo = call(gathered_filters, [((2, 256, 512), BF16)] * 2, (mine, other))

    inner, down, up = call(
        fine_rim, [((512, 128), F32), ((256, 128), F32), ((256, 128), F32)], (acc, wt, below, above),
        [pltpu.VMEM((2, 256, 256), BF16)] * 2, flops=10**8)
    before, after = turn(up, "slab", 1), turn(down, "slab", -1)
    d_low, d_high = call(
        first_down, [((128, 128), F32)] * 2, (acc, inner, before, after, wd1),
        [pltpu.VMEM((8, 128, 128), F32), pltpu.VMEM((512, 128), BF16), pltpu.VMEM((512, 128), BF16)], flops=10**8)
    below, above = turn(d_high, "grp", 1), turn(d_low, "grp", -1)
    inner, down, up = call(
        middle, [((256, 128), F32), ((128, 128), F32), ((128, 128), F32)], (d_low, d_high, below, above, mid_w),
        [pltpu.VMEM((2, 256, 384), BF16)] * 2, flops=10**8)
    before, after = turn(up, "slab", 1), turn(down, "slab", -1)
    (row,) = call(
        second_down, [((32, 256), F32)], (inner, before, after, whi, wlo), [pltpu.VMEM((256, 128), F32)], flops=10**8)
    pair = jnp.concatenate([row, swap(row, "grp", 4)], axis=0)
    others = [turn_x(pair, by) for by in (1, 2, 3)]
    down, mid, up = call(
        coarse_conv, [((64, 256), F32)] * 3, (pair, *others, coarse_w),
        [pltpu.VMEM((256, 256), F32), pltpu.VMEM((320, 768), BF16), pltpu.VMEM((320, 768), BF16)], flops=10**8)
    before, after = turn(up, "slab", 1), turn(down, "slab", -1)
    (out,) = call(finish, [((64, 256), F32)], (mid, before, after))
    return out.reshape(64, 1, 256)


def solution(mesh):
    placed = (
        P(None, "slab", "grp", None),
        P(),
        P(),
        P(),
        P(None, None, None, None, "grp"),
        P(None, None, None, None, "grp"),
    )
    return jax.shard_map(
        per_device, mesh=mesh, in_specs=placed, out_specs=P("grp", "slab", None), check_vma=False
    )
```

profile of v0, /device:TPU:4, one launch (start us, length us, event | category | flops | bytes accessed | tf_op | source)
XLA Modules:
  0.0 97.2 jit_solution(16201383150923527081)
XLA Ops:
  0.0 1.0 %copy-done.2 = f32[64,4,4,128]{3,2,1,0:T(4,128)S(1)} copy-done((f32[64,4,4,128]{3,2,1,0:T(4,128)S(1)}, f32[64,4,4,128]{3,2,1,0:T(4,128)}, u32[]{:S(2)}) %copy-start.2) | copy-done | bytes 524312
  1.0 0.9 copy-done.4
  1.9 0.1 edges.1
  2.0 7.3 %collective-permute-start.8 = (f32[128,128]{1,0:T(8,128)S(1)}, f32[128,128]{1,0:T(8,128)S(1)}, u32[]{:S(2)}, u32[]{:S(2)}) collective-permute-start(f32[128,128]{1,0:T(8,128)S(1)} %get-tuple-element.38), channel_id=1, source_target_pairs={{0,4},{1,5},{2,6},{3,7},{4,0},{5,1},{6,2},{7,3},{8,12},{9,13},{10,... | collective-permute-start | bytes 196616 | tf_op jit(solution)/shard_map/ppermute | solution.py:291
  9.3 2.4 %collective-permute-done.8 = f32[128,128]{1,0:T(8,128)S(1)} collective-permute-done((f32[128,128]{1,0:T(8,128)S(1)}, f32[128,128]{1,0:T(8,128)S(1)}, u32[]{:S(2)}, u32[]{:S(2)}) %collective-permute-start.8) | collective-permute-done | bytes 65568 | tf_op jit(solution)/shard_map/ppermute | solution.py:291
  11.8 1.3 %collective-permute-start.9 = (f32[256,128]{1,0:T(8,128)S(1)}, f32[256,128]{1,0:T(8,128)S(1)}, u32[]{:S(2)}, u32[]{:S(2)}) collective-permute-start(f32[256,128]{1,0:T(8,128)S(1)} %pad_maximum_fusion.1), channel_id=1, source_target_pairs={{0,1},{1,0},{2,3},{3,2},{4,5},{5,4},{6,7},{7,6},{8,9},{9,8},{10,11... | collective-permute-start | bytes 393224 | tf_op jit(solution)/shard_map/ppermute | solution.py:291
  13.1 3.8 %collective-permute-done.9 = f32[256,128]{1,0:T(8,128)S(1)} collective-permute-done((f32[256,128]{1,0:T(8,128)S(1)}, f32[256,128]{1,0:T(8,128)S(1)}, u32[]{:S(2)}, u32[]{:S(2)}) %collective-permute-start.9) | collective-permute-done | bytes 131104 | tf_op jit(solution)/shard_map/ppermute | solution.py:291
  16.8 1.0 %collective-permute-start.10 = (f32[512,128]{1,0:T(8,128)S(1)}, f32[512,128]{1,0:T(8,128)S(1)}, u32[]{:S(2)}, u32[]{:S(2)}) collective-permute-start(f32[512,128]{1,0:T(8,128)S(1)} %pad_maximum_fusion), channel_id=1, source_target_pairs={{0,2},{1,3},{2,0},{3,1},{4,6},{5,7},{6,4},{7,5},{8,10},{9,11},{10,... | collective-permute-start | bytes 786440 | tf_op jit(solution)/shard_map/ppermute | solution.py:291
  17.9 6.9 %collective-permute-done.10 = f32[512,128]{1,0:T(8,128)S(1)} collective-permute-done((f32[512,128]{1,0:T(8,128)S(1)}, f32[512,128]{1,0:T(8,128)S(1)}, u32[]{:S(2)}, u32[]{:S(2)}) %collective-permute-start.10) | collective-permute-done | bytes 262176 | tf_op jit(solution)/shard_map/ppermute | solution.py:291
  24.8 0.1 collective-permute-start.11
  24.9 1.5 %collective-permute-start = (f32[256,128]{1,0:T(8,128)S(1)}, f32[256,128]{1,0:T(8,128)S(1)}, u32[]{:S(2)}, u32[]{:S(2)}) collective-permute-start(f32[256,128]{1,0:T(8,128)S(1)} %get-tuple-element.27), channel_id=1, source_target_pairs={{0,1},{1,2},{2,3},{3,4},{4,5},{5,6},{6,7},{7,0},{8,9},{9,10},{10,1... | collective-permute-start | bytes 393224 | tf_op jit(solution)/shard_map/ppermute | solution.py:287
  26.4 0.6 collective-permute-start.1
  27.0 2.0 %fine_own.1 = (f32[1536,128]{1,0:T(8,128)S(1)}, bf16[384,768]{1,0:T(8,128)(2,1)S(1)}) custom-call(f32[1024,128]{1,0:T(8,128)S(1)} %bitcast.14, f32[1728,64]{1,0:T(8,128)S(1)} %bitcast.18), custom_call_target="tpu_custom_call" | custom-call | flops 1000000000 | bytes 966656 | tf_op jit(solution)/shard_map/fine_own/pallas_call | solution.py:35
  29.0 0.0 copy-start
  29.0 1.8 %collective-permute-done.below = f32[256,128]{1,0:T(8,128)S(1)} collective-permute-done((f32[256,128]{1,0:T(8,128)S(1)}, f32[256,128]{1,0:T(8,128)S(1)}, u32[]{:S(2)}, u32[]{:S(2)}) %collective-permute-start) | collective-permute-done | bytes 131104 | tf_op jit(solution)/shard_map/ppermute | solution.py:287
  30.8 5.3 %collective-permute-done.1.above = f32[256,128]{1,0:T(8,128)S(1)} collective-permute-done((f32[256,128]{1,0:T(8,128)S(1)}, f32[256,128]{1,0:T(8,128)S(1)}, u32[]{:S(2)}, u32[]{:S(2)}) %collective-permute-start.1) | collective-permute-done | bytes 131104 | tf_op jit(solution)/shard_map/ppermute | solution.py:287
  36.1 0.6 fine_rim.1
  36.8 0.1 collective-permute-start.2
  36.8 5.6 %collective-permute-start.3 = (f32[256,128]{1,0:T(8,128)S(1)}, f32[256,128]{1,0:T(8,128)S(1)}, u32[]{:S(2)}, u32[]{:S(2)}) collective-permute-start(f32[256,128]{1,0:T(8,128)S(1)} %get-tuple-element.31), channel_id=1, source_target_pairs={{0,248},{8,0},{16,8},{24,16},{32,24},{40,32},{48,40},{56,48},{64,5... | collective-permute-start | bytes 393224 | tf_op jit(solution)/shard_map/ppermute | solution.py:287
  42.5 2.6 %collective-permute-done.2.before = f32[256,128]{1,0:T(8,128)S(1)} collective-permute-done((f32[256,128]{1,0:T(8,128)S(1)}, f32[256,128]{1,0:T(8,128)S(1)}, u32[]{:S(2)}, u32[]{:S(2)}) %collective-permute-start.2) | collective-permute-done | bytes 131104 | tf_op jit(solution)/shard_map/ppermute | solution.py:287
  45.1 0.0 collective-permute-done.3.after
  45.1 0.5 first_down.1
  45.6 7.9 %collective-permute-start.4 = (f32[128,128]{1,0:T(8,128)S(1)}, f32[128,128]{1,0:T(8,128)S(1)}, u32[]{:S(2)}, u32[]{:S(2)}) collective-permute-start(f32[128,128]{1,0:T(8,128)S(1)} %get-tuple-element.33.d_high), channel_id=1, source_target_pairs={{0,1},{1,2},{2,3},{3,4},{4,5},{5,6},{6,7},{7,0},{8,9},{9,10},{10,1... | collective-permute-start | bytes 196616 | tf_op jit(solution)/shard_map/ppermute | solution.py:287
  53.6 0.0 collective-permute-start.5
  53.6 0.5 filters.1
  54.1 1.4 %collective-permute-done.4.below = f32[128,128]{1,0:T(8,128)S(1)} collective-permute-done((f32[128,128]{1,0:T(8,128)S(1)}, f32[128,128]{1,0:T(8,128)S(1)}, u32[]{:S(2)}, u32[]{:S(2)}) %collective-permute-start.4) | collective-permute-done | bytes 65568 | tf_op jit(solution)/shard_map/ppermute | solution.py:287
  55.5 2.4 %collective-permute-done.5.above = f32[128,128]{1,0:T(8,128)S(1)} collective-permute-done((f32[128,128]{1,0:T(8,128)S(1)}, f32[128,128]{1,0:T(8,128)S(1)}, u32[]{:S(2)}, u32[]{:S(2)}) %collective-permute-start.5) | collective-permute-done | bytes 65568 | tf_op jit(solution)/shard_map/ppermute | solution.py:287
  57.9 1.2 %middle.1 = (f32[256,128]{1,0:T(8,128)S(1)}, f32[128,128]{1,0:T(8,128)S(1)}, f32[128,128]{1,0:T(8,128)S(1)}) custom-call(f32[128,128]{1,0:T(8,128)S(1)} %get-tuple-element.32.d_low, f32[128,128]{1,0:T(8,128)S(1)} %get-tuple-element.33.d_high, f32[128,128]{1,0:T(8,128)S(1)} %collective-permute-done.4.below, f32[128,128]{1,0:T(8,128)S(1)} %collective-permute-done.5.above, ...), custom_call_target="tpu_custom_call" | custom-call | flops 100000000 | bytes 2031616 | tf_op jit(solution)/shard_map/middle/pallas_call | solution.py:35
  59.1 0.1 collective-permute-start.6
  59.2 5.6 %collective-permute-start.7 = (f32[128,128]{1,0:T(8,128)S(1)}, f32[128,128]{1,0:T(8,128)S(1)}, u32[]{:S(2)}, u32[]{:S(2)}) collective-permute-start(f32[128,128]{1,0:T(8,128)S(1)} %get-tuple-element.37), channel_id=1, source_target_pairs={{0,248},{8,0},{16,8},{24,16},{32,24},{40,32},{48,40},{56,48},{64,5... | collective-permute-start | bytes 196616 | tf_op jit(solution)/shard_map/ppermute | solution.py:287
  64.8 0.0 collective-permute-done.11.other
  64.8 0.2 gathered_filters.1
  65.0 1.7 %collective-permute-done.6.before = f32[128,128]{1,0:T(8,128)S(1)} collective-permute-done((f32[128,128]{1,0:T(8,128)S(1)}, f32[128,128]{1,0:T(8,128)S(1)}, u32[]{:S(2)}, u32[]{:S(2)}) %collective-permute-start.6) | collective-permute-done | bytes 65568 | tf_op jit(solution)/shard_map/ppermute | solution.py:287
  66.8 0.0 collective-permute-done.7.after
  66.8 0.4 second_down.1
  67.2 1.5 %collective-permute-start.12 = (f32[32,256]{1,0:T(8,128)S(1)}, f32[32,256]{1,0:T(8,128)S(1)}, u32[]{:S(2)}, u32[]{:S(2)}) collective-permute-start(f32[32,256]{1,0:T(8,128)S(1)} %second_down.1), channel_id=1, source_target_pairs={{0,4},{1,5},{2,6},{3,7},{4,0},{5,1},{6,2},{7,3},{8,12},{9,13},{10,... | collective-permute-start | bytes 98312 | tf_op jit(solution)/shard_map/ppermute | solution.py:291
  68.7 6.3 %collective-permute-done.12 = f32[32,256]{1,0:T(8,128)S(1)} collective-permute-done((f32[32,256]{1,0:T(8,128)S(1)}, f32[32,256]{1,0:T(8,128)S(1)}, u32[]{:S(2)}, u32[]{:S(2)}) %collective-permute-start.12) | collective-permute-done | bytes 32800 | tf_op jit(solution)/shard_map/ppermute | solution.py:291
  75.1 6.9 %collective-permute-start.13 = (f32[64,256]{1,0:T(8,128)S(1)}, f32[64,256]{1,0:T(8,128)S(1)}, u32[]{:S(2)}, u32[]{:S(2)}) collective-permute-start(f32[64,256]{1,0:T(8,128)S(1)} %pad_maximum_fusion.2.own), channel_id=1, source_target_pairs={{0,1},{1,2},{2,3},{3,0},{4,5},{5,6},{6,7},{7,4},{8,9},{9,10},{10,1... | collective-permute-start | bytes 196616 | tf_op jit(solution)/shard_map/ppermute | solution.py:294
  82.0 0.0 collective-permute-start.14
  82.0 1.6 %collective-permute-start.15 = (f32[64,256]{1,0:T(8,128)S(1)}, f32[64,256]{1,0:T(8,128)S(1)}, u32[]{:S(2)}, u32[]{:S(2)}) collective-permute-start(f32[64,256]{1,0:T(8,128)S(1)} %pad_maximum_fusion.2.own), channel_id=1, source_target_pairs={{0,3},{1,0},{2,1},{3,2},{4,7},{5,4},{6,5},{7,6},{8,11},{9,8},{10,9... | collective-permute-start | bytes 196616 | tf_op jit(solution)/shard_map/ppermute | solution.py:294
  83.6 0.3 collective-permute-done.13.one
  83.9 3.9 %collective-permute-done.14.two = f32[64,256]{1,0:T(8,128)S(1)} collective-permute-done((f32[64,256]{1,0:T(8,128)S(1)}, f32[64,256]{1,0:T(8,128)S(1)}, u32[]{:S(2)}, u32[]{:S(2)}) %collective-permute-start.14) | collective-permute-done | bytes 65568 | tf_op jit(solution)/shard_map/ppermute | solution.py:294
  87.8 1.0 %coarse_conv.1 = (f32[64,256]{1,0:T(8,128)S(1)}, f32[64,256]{1,0:T(8,128)S(1)}, f32[64,256]{1,0:T(8,128)S(1)}) custom-call(f32[64,256]{1,0:T(8,128)S(1)} %pad_maximum_fusion.2.own, f32[64,256]{1,0:T(8,128)S(1)} %collective-permute-done.13.one, f32[64,256]{1,0:T(8,128)S(1)} %collective-permute-done.14.two, f32[64,256]{1,0:T(8,128)S(1)} %collective-permute-done.15.three, ...), custom_call_target="tpu_custom_call" | custom-call | flops 100000000 | bytes 2031616 | tf_op jit(solution)/shard_map/coarse_conv/pallas_call | solution.py:35
  88.8 0.1 collective-permute-start.16
  88.9 5.6 %collective-permute-start.17 = (f32[64,256]{1,0:T(8,128)S(1)}, f32[64,256]{1,0:T(8,128)S(1)}, u32[]{:S(2)}, u32[]{:S(2)}) collective-permute-start(f32[64,256]{1,0:T(8,128)S(1)} %get-tuple-element.44), channel_id=1, source_target_pairs={{0,248},{8,0},{16,8},{24,16},{32,24},{40,32},{48,40},{56,48},{64,5... | collective-permute-start | bytes 196616 | tf_op jit(solution)/shard_map/ppermute | solution.py:287
  94.5 1.9 %collective-permute-done.16.before = f32[64,256]{1,0:T(8,128)S(1)} collective-permute-done((f32[64,256]{1,0:T(8,128)S(1)}, f32[64,256]{1,0:T(8,128)S(1)}, u32[]{:S(2)}, u32[]{:S(2)}) %collective-permute-start.16) | collective-permute-done | bytes 65568 | tf_op jit(solution)/shard_map/ppermute | solution.py:287
  96.5 0.0 collective-permute-done.17.after
  96.5 0.7 copy.7
  (18 shorter events, 0.1 us)
Async XLA Ops:
  0.0 1.0 %copy-start.2 = (f32[64,4,4,128]{3,2,1,0:T(4,128)S(1)}, f32[64,4,4,128]{3,2,1,0:T(4,128)}, u32[]{:S(2)}) copy-start(f32[64,4,4,128]{3,2,1,0:T(4,128)} %param.6) | copy-start | bytes 1572868
  1.0 0.9 copy-start.4
  1.9 25.1 %copy-start.5 = (f32[3,3,3,64,64]{4,3,2,1,0:T(8,128)S(1)}, f32[3,3,3,64,64]{4,3,2,1,0:T(8,128)}, u32[]{:S(2)}) copy-start(f32[3,3,3,64,64]{4,3,2,1,0:T(8,128)} %param.7) | copy-start | bytes 1327108
  2.0 9.7 %collective-permute-start.8 = (f32[128,128]{1,0:T(8,128)S(1)}, f32[128,128]{1,0:T(8,128)S(1)}, u32[]{:S(2)}, u32[]{:S(2)}) collective-permute-start(f32[128,128]{1,0:T(8,128)S(1)} %get-tuple-element.38), channel_id=1, source_target_pairs={{0,4},{1,5},{2,6},{3,7},{4,0},{5,1},{6,2},{7,3},{8,12},{9,13},{10,... | collective-permute-start | bytes 196616 | tf_op jit(solution)/shard_map/ppermute | solution.py:291
  11.8 5.1 %collective-permute-start.9 = (f32[256,128]{1,0:T(8,128)S(1)}, f32[256,128]{1,0:T(8,128)S(1)}, u32[]{:S(2)}, u32[]{:S(2)}) collective-permute-start(f32[256,128]{1,0:T(8,128)S(1)} %pad_maximum_fusion.1), channel_id=1, source_target_pairs={{0,1},{1,0},{2,3},{3,2},{4,5},{5,4},{6,7},{7,6},{8,9},{9,8},{10,11... | collective-permute-start | bytes 393224 | tf_op jit(solution)/shard_map/ppermute | solution.py:291
  16.8 8.0 %collective-permute-start.10 = (f32[512,128]{1,0:T(8,128)S(1)}, f32[512,128]{1,0:T(8,128)S(1)}, u32[]{:S(2)}, u32[]{:S(2)}) collective-permute-start(f32[512,128]{1,0:T(8,128)S(1)} %pad_maximum_fusion), channel_id=1, source_target_pairs={{0,2},{1,3},{2,0},{3,1},{4,6},{5,7},{6,4},{7,5},{8,10},{9,11},{10,... | collective-permute-start | bytes 786440 | tf_op jit(solution)/shard_map/ppermute | solution.py:291
  24.8 40.0 %collective-permute-start.11 = (f32[1024,128]{1,0:T(8,128)S(1)}, f32[1024,128]{1,0:T(8,128)S(1)}, u32[]{:S(2)}, u32[]{:S(2)}) collective-permute-start(f32[1024,128]{1,0:T(8,128)S(1)} %constant_dynamic-update-slice_fusion.mine), channel_id=1, source_target_pairs={{0,8},{8,0},{16,24},{24,16},{32,40},{40,32},{48,56},{56,48},{64,72... | collective-permute-start | bytes 1572872 | tf_op jit(solution)/shard_map/ppermute | solution.py:291
  24.9 5.9 %collective-permute-start = (f32[256,128]{1,0:T(8,128)S(1)}, f32[256,128]{1,0:T(8,128)S(1)}, u32[]{:S(2)}, u32[]{:S(2)}) collective-permute-start(f32[256,128]{1,0:T(8,128)S(1)} %get-tuple-element.27), channel_id=1, source_target_pairs={{0,1},{1,2},{2,3},{3,4},{4,5},{5,6},{6,7},{7,0},{8,9},{9,10},{10,1... | collective-permute-start | bytes 393224 | tf_op jit(solution)/shard_map/ppermute | solution.py:287
  26.4 9.7 %collective-permute-start.1 = (f32[256,128]{1,0:T(8,128)S(1)}, f32[256,128]{1,0:T(8,128)S(1)}, u32[]{:S(2)}, u32[]{:S(2)}) collective-permute-start(f32[256,128]{1,0:T(8,128)S(1)} %get-tuple-element.28), channel_id=1, source_target_pairs={{0,7},{1,0},{2,1},{3,2},{4,3},{5,4},{6,5},{7,6},{8,15},{9,8},{10,9... | collective-permute-start | bytes 393224 | tf_op jit(solution)/shard_map/ppermute | solution.py:287
  27.0 18.1 %copy-start.3 = (f32[2,2,2,64,128]{4,3,2,1,0:T(8,128)S(1)}, f32[2,2,2,64,128]{4,3,2,1,0:T(8,128)}, u32[]{:S(2)}) copy-start(f32[2,2,2,64,128]{4,3,2,1,0:T(8,128)} %param.8) | copy-start | bytes 786436
  27.0 26.6 %copy-start.1 = (f32[3,3,3,256,64]{3,4,2,1,0:T(8,128)S(1)}, f32[3,3,3,256,64]{3,4,2,1,0:T(8,128)}, u32[]{:S(2)}) copy-start(f32[3,3,3,256,64]{3,4,2,1,0:T(8,128)} %param.11) | copy-start | bytes 5308420
  29.0 24.6 %copy-start = (f32[3,3,3,128,128]{4,3,2,1,0:T(8,128)S(1)}, f32[3,3,3,128,128]{4,3,2,1,0:T(8,128)}, u32[]{:S(2)}) copy-start(f32[3,3,3,128,128]{4,3,2,1,0:T(8,128)} %param.9) | copy-start | bytes 5308420
  36.8 8.4 %collective-permute-start.2 = (f32[256,128]{1,0:T(8,128)S(1)}, f32[256,128]{1,0:T(8,128)S(1)}, u32[]{:S(2)}, u32[]{:S(2)}) collective-permute-start(f32[256,128]{1,0:T(8,128)S(1)} %get-tuple-element.30), channel_id=1, source_target_pairs={{0,8},{8,16},{16,24},{24,32},{32,40},{40,48},{48,56},{56,64},{64,7... | collective-permute-start | bytes 393224 | tf_op jit(solution)/shard_map/ppermute | solution.py:287
  36.8 8.3 %collective-permute-start.3 = (f32[256,128]{1,0:T(8,128)S(1)}, f32[256,128]{1,0:T(8,128)S(1)}, u32[]{:S(2)}, u32[]{:S(2)}) collective-permute-start(f32[256,128]{1,0:T(8,128)S(1)} %get-tuple-element.31), channel_id=1, source_target_pairs={{0,248},{8,0},{16,8},{24,16},{32,24},{40,32},{48,40},{56,48},{64,5... | collective-permute-start | bytes 393224 | tf_op jit(solution)/shard_map/ppermute | solution.py:287
  45.6 9.9 %collective-permute-start.4 = (f32[128,128]{1,0:T(8,128)S(1)}, f32[128,128]{1,0:T(8,128)S(1)}, u32[]{:S(2)}, u32[]{:S(2)}) collective-permute-start(f32[128,128]{1,0:T(8,128)S(1)} %get-tuple-element.33.d_high), channel_id=1, source_target_pairs={{0,1},{1,2},{2,3},{3,4},{4,5},{5,6},{6,7},{7,0},{8,9},{9,10},{10,1... | collective-permute-start | bytes 196616 | tf_op jit(solution)/shard_map/ppermute | solution.py:287
  53.6 4.3 %collective-permute-start.5 = (f32[128,128]{1,0:T(8,128)S(1)}, f32[128,128]{1,0:T(8,128)S(1)}, u32[]{:S(2)}, u32[]{:S(2)}) collective-permute-start(f32[128,128]{1,0:T(8,128)S(1)} %get-tuple-element.32.d_low), channel_id=1, source_target_pairs={{0,7},{1,0},{2,1},{3,2},{4,3},{5,4},{6,5},{7,6},{8,15},{9,8},{10,9... | collective-permute-start | bytes 196616 | tf_op jit(solution)/shard_map/ppermute | solution.py:287
  59.1 7.7 %collective-permute-start.6 = (f32[128,128]{1,0:T(8,128)S(1)}, f32[128,128]{1,0:T(8,128)S(1)}, u32[]{:S(2)}, u32[]{:S(2)}) collective-permute-start(f32[128,128]{1,0:T(8,128)S(1)} %get-tuple-element.36), channel_id=1, source_target_pairs={{0,8},{8,16},{16,24},{24,32},{32,40},{40,48},{48,56},{56,64},{64,7... | collective-permute-start | bytes 196616 | tf_op jit(solution)/shard_map/ppermute | solution.py:287
  59.2 7.6 %collective-permute-start.7 = (f32[128,128]{1,0:T(8,128)S(1)}, f32[128,128]{1,0:T(8,128)S(1)}, u32[]{:S(2)}, u32[]{:S(2)}) collective-permute-start(f32[128,128]{1,0:T(8,128)S(1)} %get-tuple-element.37), channel_id=1, source_target_pairs={{0,248},{8,0},{16,8},{24,16},{32,24},{40,32},{48,40},{56,48},{64,5... | collective-permute-start | bytes 196616 | tf_op jit(solution)/shard_map/ppermute | solution.py:287
  67.2 7.9 %collective-permute-start.12 = (f32[32,256]{1,0:T(8,128)S(1)}, f32[32,256]{1,0:T(8,128)S(1)}, u32[]{:S(2)}, u32[]{:S(2)}) collective-permute-start(f32[32,256]{1,0:T(8,128)S(1)} %second_down.1), channel_id=1, source_target_pairs={{0,4},{1,5},{2,6},{3,7},{4,0},{5,1},{6,2},{7,3},{8,12},{9,13},{10,... | collective-permute-start | bytes 98312 | tf_op jit(solution)/shard_map/ppermute | solution.py:291
  75.1 8.9 %collective-permute-start.13 = (f32[64,256]{1,0:T(8,128)S(1)}, f32[64,256]{1,0:T(8,128)S(1)}, u32[]{:S(2)}, u32[]{:S(2)}) collective-permute-start(f32[64,256]{1,0:T(8,128)S(1)} %pad_maximum_fusion.2.own), channel_id=1, source_target_pairs={{0,1},{1,2},{2,3},{3,0},{4,5},{5,6},{6,7},{7,4},{8,9},{9,10},{10,1... | collective-permute-start | bytes 196616 | tf_op jit(solution)/shard_map/ppermute | solution.py:294
  82.0 5.8 %collective-permute-start.14 = (f32[64,256]{1,0:T(8,128)S(1)}, f32[64,256]{1,0:T(8,128)S(1)}, u32[]{:S(2)}, u32[]{:S(2)}) collective-permute-start(f32[64,256]{1,0:T(8,128)S(1)} %pad_maximum_fusion.2.own), channel_id=1, source_target_pairs={{0,2},{1,3},{2,0},{3,1},{4,6},{5,7},{6,4},{7,5},{8,10},{9,11},{10,... | collective-permute-start | bytes 196616 | tf_op jit(solution)/shard_map/ppermute | solution.py:294
  82.0 5.8 %collective-permute-start.15 = (f32[64,256]{1,0:T(8,128)S(1)}, f32[64,256]{1,0:T(8,128)S(1)}, u32[]{:S(2)}, u32[]{:S(2)}) collective-permute-start(f32[64,256]{1,0:T(8,128)S(1)} %pad_maximum_fusion.2.own), channel_id=1, source_target_pairs={{0,3},{1,0},{2,1},{3,2},{4,7},{5,4},{6,5},{7,6},{8,11},{9,8},{10,9... | collective-permute-start | bytes 196616 | tf_op jit(solution)/shard_map/ppermute | solution.py:294
  88.8 7.7 %collective-permute-start.16 = (f32[64,256]{1,0:T(8,128)S(1)}, f32[64,256]{1,0:T(8,128)S(1)}, u32[]{:S(2)}, u32[]{:S(2)}) collective-permute-start(f32[64,256]{1,0:T(8,128)S(1)} %get-tuple-element.43), channel_id=1, source_target_pairs={{0,8},{8,16},{16,24},{24,32},{32,40},{40,48},{48,56},{56,64},{64,7... | collective-permute-start | bytes 196616 | tf_op jit(solution)/shard_map/ppermute | solution.py:287
  88.9 7.6 %collective-permute-start.17 = (f32[64,256]{1,0:T(8,128)S(1)}, f32[64,256]{1,0:T(8,128)S(1)}, u32[]{:S(2)}, u32[]{:S(2)}) collective-permute-start(f32[64,256]{1,0:T(8,128)S(1)} %get-tuple-element.44), channel_id=1, source_target_pairs={{0,248},{8,0},{16,8},{24,16},{32,24},{40,32},{48,40},{56,48},{64,5... | collective-permute-start | bytes 196616 | tf_op jit(solution)/shard_map/ppermute | solution.py:287
where the time goes:
time: 98 us; the launch traced here: 97.2 us
  starting transfers between devices  46.9 us (48%)
  waiting for transfers between devices  40.9 us (42%)
  Pallas kernels  6.56 us (7%)
  local copies, waits for them, and re-layouts  2.7 us (3%)
    ppermute x10, starting transfers between devices, turn(): return lax.ppermute(x, axis, [(i, (i + by) % n) for i in range(n)])  27.2 us
    ppermute x5, waiting for transfers between devices, swap(): return lax.ppermute(x, axis, [(i, i ^ mask) for i in range(n)])  19.5 us
    ppermute x10, waiting for transfers between devices, turn(): return lax.ppermute(x, axis, [(i, (i + by) % n) for i in range(n)])  17.2 us
    ppermute x5, starting transfers between devices, swap(): return lax.ppermute(x, axis, [(i, i ^ mask) for i in range(n)])  11.2 us
    ppermute x3, starting transfers between devices, turn_x(): lax.ppermute(x, 'grp', [(i, i & 4 | i + by & 3) for i in range(grps)])  8.51 us
    pallas_call x10, Pallas kernels, call(): pl.pallas_call(kernel, out_shape=[jax.ShapeDtypeStruct(s, t) for s, t in...  6.56 us
    ppermute x3, waiting for transfers between devices, turn_x(): lax.ppermute(x, 'grp', [(i, i & 4 | i + by & 3) for i in range(grps)])  4.21 us
    unnamed x15, local copies, waits for them, and re-layouts  1.98 us
  transfers between devices with their start and end apart: 18, of which 13 were waited for; matrix products, arithmetic and copies ran while one was open for 0% of the time, Pallas kernels for 5%

commit v1 on v0

v1 whole, which is shorter than its diff:
```python
import functools

import jax
import jax.numpy as jnp
from jax import lax
from jax.experimental import pallas as pl
from jax.experimental.pallas import tpu as pltpu
from jax.sharding import PartitionSpec as P

F32 = jnp.float32
BF16 = jnp.bfloat16
XORS = (0, 4, 1, 5, 3, 7, 2, 6)


def split(x):
    hi = x.astype(BF16)
    return hi, (x - hi.astype(F32)).astype(BF16)


def mm(a, b):
    return lax.dot_general(a, b, (((1,), (0,)), ((), ())), preferred_element_type=F32)


def mm_t(a, b):
    return lax.dot_general(a, b, (((1,), (1,)), ((), ())), preferred_element_type=F32)


def gelu(v):
    return v * (1.0 + lax.erf(v * 0.7071067811865476)) * 0.5


def call(kernel, outs, args, scratch=(), flops=0, after=()):
    vmem = pl.BlockSpec(memory_space=pltpu.VMEM)
    size = sum(a.size * a.dtype.itemsize for a in args)
    return pl.pallas_call(
        kernel,
        out_shape=[jax.ShapeDtypeStruct(s, t) for s, t in outs],
        in_specs=[vmem] * len(args) + [pl.BlockSpec(memory_space=pl.ANY)] * len(after),
        out_specs=[vmem] * len(outs),
        scratch_shapes=list(scratch),
        compiler_params=pltpu.CompilerParams(vmem_limit_bytes=16 * 2**20),
        cost_estimate=pl.CostEstimate(flops=flops, bytes_accessed=size, transcendentals=0),
        name=kernel.__name__,
    )(*args, *after)


def parity(axis):
    return lax.rem(lax.axis_index(axis), 2)


def send(near, far, index, up, down, axis):
    even = parity(axis) == 0
    near[index] = jnp.where(even, up, down)
    far[index] = jnp.where(even, down, up)


def received(near, far, index, axis):
    place = lax.axis_index(axis)
    even = parity(axis) == 0
    one, two = near[index], far[index]
    before = jnp.where(place > 0, jnp.where(even, two, one), 0.0)
    after = jnp.where(place < lax.axis_size(axis) - 1, jnp.where(even, one, two), 0.0)
    return before, after


def edges(vol, near, far):
    for d in range(4):
        first = vol[pl.ds(d * 4, 64, stride=16), :]
        last = vol[pl.ds(d * 4 + 3, 64, stride=16), :]
        send(near, far, pl.ds(d * 64, 64), last, first, "grp")


def own_half(w2, after, half):
    half[...] = w2[pl.ds(pl.multiple_of(parity("slab") * 128, 128), 128), :]


def joined(first, second, after, out):
    n = first.shape[0]
    out[:n, :] = first[...]
    out[n:, :] = second[...]


def put_shifted(x, high, low, lead, row, lane):
    column = lax.broadcasted_iota(jnp.int32, x.shape, 1)
    for k in range(3):
        if k == 0:
            y = jnp.where(column == 0, 0.0, pltpu.roll(x, 1, 1))
        elif k == 1:
            y = x
        else:
            y = jnp.where(column == 127, 0.0, pltpu.roll(x, 127, 1))
        hi, lo = split(y)
        high[lead, row + 64 * k : row + 64 * k + 64, lane : lane + 128] = hi
        low[lead, row + 64 * k : row + 64 * k + 64, lane : lane + 128] = lo


def taps(weights, high, low):
    both = mm(weights, high)
    return both[:192] + both[192:] + mm(weights[:192], low)


def planes(first, second):
    by_depth = [first[:, :128], first[:, 128:], second[:, :128], second[:, 128:]]
    sums = []
    for out in range(-1, 5):
        terms = [by_depth[out + a - 1][a * 64 : a * 64 + 64] for a in range(3) if 0 <= out + a - 1 < 4]
        sums.append(functools.reduce(jnp.add, terms))
    return sums


def fine_own(vol, w1, acc, wt, high, low):
    zeros = jnp.zeros((64, 256), BF16)
    for lead in range(2):
        for h in range(4):
            high[lead, h * 256 + 192 : h * 256 + 256, :] = zeros
            low[lead, h * 256 + 192 : h * 256 + 256, :] = zeros
    for b in range(3):
        wt[:, b * 256 + 192 : b * 256 + 256] = jnp.zeros((384, 64), BF16)
    for a in range(3):
        for b in range(3):
            x = w1[a * 576 + b * 192 : a * 576 + b * 192 + 192, :]
            x = jnp.concatenate([x, jnp.zeros((64, 64), F32)], axis=0)
            hi, lo = split(x.T)
            wt[a * 64 : a * 64 + 64, b * 256 : b * 256 + 256] = hi
            wt[192 + a * 64 : 192 + a * 64 + 64, b * 256 : b * 256 + 256] = lo
    for d in range(4):
        for h in range(4):
            put_shifted(vol[pl.ds(d * 4 + h, 64, stride=16), :], high, low, d // 2, h * 256, d % 2 * 128)
    for h in range(4):
        first, last = max(h - 1, 0), min(h + 1, 3)
        rows = slice(first * 256, last * 256 + 256)
        lanes = slice((first - h + 1) * 256, (last - h + 2) * 256)
        weights = wt[:, lanes]
        parts = [taps(weights, high[lead, rows, :], low[lead, rows, :]) for lead in range(2)]
        for i, value in enumerate(planes(*parts)):
            acc[i * 256 + h * 64 : i * 256 + h * 64 + 64, :] = value


def fine_rim(acc, wt, near, far, inner, out_near, out_far, high, low):
    zeros = jnp.zeros((64, 256), BF16)
    for side in range(2):
        for lead in range(2):
            high[side * 2 + lead, 192:256, :] = zeros
            low[side * 2 + lead, 192:256, :] = zeros
    for d in range(4):
        below, above = received(near, far, pl.ds(d * 64, 64), "grp")
        put_shifted(below, high, low, d // 2, 0, d % 2 * 128)
        put_shifted(above, high, low, 2 + d // 2, 0, d % 2 * 128)
    for side in range(2):
        h = (0, 3)[side]
        weights = wt[:, side * 512 : side * 512 + 256]
        parts = [taps(weights, high[side * 2 + lead], low[side * 2 + lead]) for lead in range(2)]
        totals = planes(*parts)
        for i, value in enumerate(totals):
            totals[i] = value + acc[i * 256 + h * 64 : i * 256 + h * 64 + 64, :]
            if 0 < i < 5:
                inner[(i - 1) * 128 + side * 64 : (i - 1) * 128 + side * 64 + 64, :] = totals[i]
        send(out_near, out_far, pl.ds(h * 64, 64), totals[5], totals[0], "slab")
    for h in (1, 2):
        at = pl.ds(h * 64, 64)
        send(out_near, out_far, at, acc[5 * 256 + h * 64 : 5 * 256 + h * 64 + 64, :], acc[at, :], "slab")


def first_down(acc, inner, near, far, w, out_low, out_high, out_near, out_far, cells, whi, wlo):
    for a in range(2):
        for bk in range(4):
            hi, lo = split(w[(a * 4 + bk) * 64 : (a * 4 + bk) * 64 + 64, :])
            whi[(bk * 2 + a) * 64 : (bk * 2 + a) * 64 + 64, :] = hi
            wlo[(bk * 2 + a) * 64 : (bk * 2 + a) * 64 + 64, :] = lo
    for h in range(4):
        before, after = received(near, far, pl.ds(h * 64, 64), "slab")
        level = []
        for d in range(4):
            if h in (0, 3):
                at = d * 128 + (h == 3) * 64
                v = inner[at : at + 64, :]
            else:
                at = (d + 1) * 256 + h * 64
                v = acc[at : at + 64, :]
            if d == 0:
                v = v + before
            if d == 3:
                v = v + after
            level.append(gelu(v))
        for d2 in range(2):
            cells[h * 2 + d2] = jnp.concatenate(level[2 * d2 : 2 * d2 + 2], axis=0).T
    results = []
    for h2 in range(2):
        rows = []
        for d2 in range(2):
            rows.append(jnp.concatenate(
                [cells[(2 * h2 + b) * 2 + d2, pl.ds(k, 64, stride=2), :] for b in range(2) for k in range(2)], axis=1))
        hi, lo = split(jnp.concatenate(rows, axis=0))
        both = mm(jnp.concatenate([hi, lo], axis=0), whi[...])
        results.append(both[:128] + both[128:] + mm(hi, wlo[...]))
    out_low[...], out_high[...] = results
    send(out_near, out_far, slice(None), results[1], results[0], "grp")


def filters(wm, wc, mid, coarse):
    for a in range(3):
        for i in range(9):
            x = wm[(a * 9 + i) * 128 : (a * 9 + i) * 128 + 128, :]
            hi, lo = split(x)
            mid[i * 128 : i * 128 + 128, a * 128 : a * 128 + 128] = hi
            mid[1152 + i * 128 : 1152 + i * 128 + 128, a * 128 : a * 128 + 128] = lo
            hi, lo = split(wc[(a * 9 + i) * 64 : (a * 9 + i) * 64 + 64, :])
            coarse[a * 64 : a * 64 + 64, i * 256 : i * 256 + 256] = hi
            coarse[192 + a * 64 : 192 + a * 64 + 64, i * 256 : i * 256 + 256] = lo


def gathered_filters(mine, other, whi, wlo):
    grp = lax.axis_index("grp")
    part = lax.rem(lax.axis_index("slab"), 2)
    for ref, half in ((mine, part), (other, 1 - part)):
        for j, mask in enumerate(XORS):
            at = pl.multiple_of((grp ^ mask) * 32, 32)
            for i in range(4):
                hi, lo = split(ref[j * 128 + i * 32 : j * 128 + i * 32 + 32, :])
                whi[half, pl.ds(at, 32), i * 128 : i * 128 + 128] = hi
                wlo[half, pl.ds(at, 32), i * 128 : i * 128 + 128] = lo


def shifted_rows(x, k, width):
    row = lax.rem(lax.broadcasted_iota(jnp.int32, x.shape, 0), width)
    if k == 0:
        return jnp.where(row == 0, 0.0, pltpu.roll(x, 1, 0))
    if k == 2:
        return jnp.where(row == width - 1, 0.0, pltpu.roll(x, x.shape[0] - 1, 0))
    return x


def put_rows(x, high, low, lead, row):
    for k in range(3):
        hi, lo = split(shifted_rows(x, k, 64))
        high[lead, row : row + 64, k * 128 : k * 128 + 128] = hi
        low[lead, row : row + 64, k * 128 : k * 128 + 128] = lo


def middle_taps(high, low, leads, rows, w, b):
    hi = [high[lead, rows, :] for lead in leads]
    lo = [low[lead, rows, :] for lead in leads]
    n = sum(x.shape[0] for x in hi)
    both = mm(jnp.concatenate(hi + lo, axis=0), w[b * 384 : b * 384 + 384, :])
    return both[:n] + both[n:] + mm(jnp.concatenate(hi, axis=0), w[1152 + b * 384 : 1152 + b * 384 + 384, :])


def middle_own(d_low, d_high, w, total, high, low):
    for i, ref in enumerate((d_low, d_high)):
        for d in range(2):
            put_rows(ref[d * 64 : d * 64 + 64, :], high, low, i, d * 64)
    every = slice(0, 128)
    center = middle_taps(high, low, (0, 1), every, w, 1)
    total[:128, :] = center[:128] + middle_taps(high, low, (1,), every, w, 2)
    total[128:, :] = center[128:] + middle_taps(high, low, (0,), every, w, 0)


def middle_rim(own, near, far, w, inner, out_near, out_far, high, low):
    for d in range(2):
        below, above = received(near, far, pl.ds(d * 64, 64), "grp")
        put_rows(below, high, low, 0, d * 64)
        put_rows(above, high, low, 1, d * 64)
    every = slice(0, 128)
    for h in range(2):
        total = own[h * 128 : h * 128 + 128, :] + middle_taps(high, low, (h,), every, w, 2 * h)
        inner[h * 64 : h * 64 + 64, :] = total[:64, 128:256] + total[64:, 256:]
        inner[128 + h * 64 : 128 + h * 64 + 64, :] = total[:64, :128] + total[64:, 128:256]
        send(out_near, out_far, pl.ds(h * 64, 64), total[64:, :128], total[:64, 256:], "slab")


def second_down(inner, near, far, whi, wlo, out, cells):
    before, after = received(near, far, slice(None), "slab")
    cells[:128, :] = gelu(inner[:128, :] + before)
    cells[128:, :] = gelu(inner[128:, :] + after)
    total = jnp.zeros((32, 256), F32)
    for a in range(2):
        x = jnp.concatenate(
            [cells[pl.ds(a * 128 + b * 64 + k, 32, stride=2), :] for b in range(2) for k in range(2)], axis=1)
        hi, lo = split(x)
        both = mm_t(jnp.concatenate([hi, lo], axis=0), whi[a])
        total = total + (both[:32] + both[32:] + mm_t(hi, wlo[a]))
    out[...] = total


def coarse_conv(own, one, two, three, w, mid, out_near, out_far, grid, high, low):
    grp = lax.axis_index("grp")
    for mask, ref in enumerate((own, one, two, three)):
        for j in range(2):
            at = pl.multiple_of((grp ^ (mask + 4 * j)) * 32, 32)
            grid[pl.ds(at, 32), :] = ref[j * 32 : j * 32 + 32, :]
    zeros = jnp.zeros((32, 768), BF16)
    for ref in (high, low):
        ref[:32, :] = zeros
        ref[288:, :] = zeros
    for k in range(3):
        hi, lo = split(shifted_rows(grid[...], k, 32))
        high[32:288, k * 256 : k * 256 + 256] = hi
        low[32:288, k * 256 : k * 256 + 256] = lo
    total = jnp.zeros((192, 256), F32)
    for b in range(3):
        rows, lanes = slice(b * 32, b * 32 + 256), slice(b * 768, b * 768 + 768)
        both = mm_t(w[:, lanes], high[rows, :])
        total = total + (both[:192] + both[192:] + mm_t(w[:192, lanes], low[rows, :]))
    mid[...] = total[64:128]
    send(out_near, out_far, slice(None), total[:64], total[128:], "slab")


def finish(mid, near, far, out):
    before, after = received(near, far, slice(None), "slab")
    out[:, 0, :] = gelu(mid[...] + before + after)


def per_device(volume, conv_fine, down_first, conv_middle, down_second, conv_coarse):
    slabs, grps = lax.axis_size("slab"), lax.axis_size("grp")

    def permute(x, target):
        pairs = []
        for s in range(slabs):
            for g in range(grps):
                t, u = target(s, g)
                pairs.append((s * grps + g, t * grps + u))
        return lax.ppermute(x, ("slab", "grp"), pairs)

    def far_slab(s, g):
        if s in (0, slabs - 1):
            return slabs - 1 - s, g ^ 4
        return (s + 1 if s % 2 else s - 1), g

    def far_grp(s, g):
        if g in (0, grps - 1):
            z, rest = divmod(s, slabs // 4)
            return (3 - z) * (slabs // 4) + rest, grps - 1 - g
        return s, (g + 1 if g % 2 else g - 1)

    def over_grp(near, far):
        return swap(near, "grp", 1), permute(far, far_grp)

    def over_slab(near, far):
        return swap(near, "slab", 1), permute(far, far_slab)

    def swap(x, axis, mask):
        if axis == "slab":
            return permute(x, lambda s, g: (s ^ mask, g))
        return permute(x, lambda s, g: (s, g ^ mask))

    def join(first, second, after):
        rows, lanes = first.shape
        return call(joined, [((2 * rows, lanes), F32)], (first, second), after=(after,))[0]

    vol = volume.reshape(1024, 128)
    w1 = conv_fine.reshape(1728, 64)
    wd1 = down_first.reshape(512, 128)
    wm = conv_middle.reshape(3456, 128)
    w2 = jnp.swapaxes(down_second, 3, 4).reshape(256, 128)
    wc = jnp.swapaxes(conv_coarse, 3, 4).reshape(1728, 256)

    rim = over_grp(*call(edges, [((256, 128), F32)] * 2, (vol,)))
    taken = [pltpu.VMEM((2, 1024, 256), BF16)] * 2
    acc, wt = call(fine_own, [((1536, 128), F32), ((384, 768), BF16)], (vol, w1), taken, flops=10**9)
    (half,) = call(own_half, [((128, 128), F32)], (w2,), after=(acc,))
    second = swap(half, "grp", 4)

    taken = [pltpu.VMEM((4, 256, 256), BF16)] * 2
    inner, *out = call(fine_rim, [((512, 128), F32)] + [((256, 128), F32)] * 2, (acc, wt, *rim), taken, flops=10**8)
    rim = over_slab(*out)
    two = join(half, second, inner)
    second = swap(two, "grp", 1)
    mid_w, coarse_w = call(filters, [((2304, 384), BF16), ((384, 2304), BF16)], (wm, wc), flops=10**8)

    taken = [pltpu.VMEM((8, 128, 128), F32), pltpu.VMEM((512, 128), BF16), pltpu.VMEM((512, 128), BF16)]
    d_low, d_high, *out = call(first_down, [((128, 128), F32)] * 4, (acc, inner, *rim, wd1), taken, flops=10**8)
    rim = over_grp(*out)
    four = join(two, second, d_low)
    second = swap(four, "grp", 3)
    taken = [pltpu.VMEM((2, 128, 384), BF16)] * 2
    (own,) = call(middle_own, [((256, 384), F32)], (d_low, d_high, mid_w), taken, flops=10**8)
    inner, *out = call(
        middle_rim, [((256, 128), F32)] + [((128, 128), F32)] * 2, (own, *rim, mid_w), taken, flops=10**8)
    rim = over_slab(*out)
    mine = join(four, second, inner)
    other = swap(mine, "slab", 1)
    whi, wlo = call(gathered_filters, [((2, 256, 512), BF16)] * 2, (mine, other))
    (row,) = call(
        second_down, [((32, 256), F32)], (inner, *rim, whi, wlo), [pltpu.VMEM((256, 128), F32)], flops=10**8)

    pair = join(row, swap(row, "grp", 4), row)
    others = [swap(pair, "grp", mask) for mask in (1, 2, 3)]
    taken = [pltpu.VMEM((256, 256), F32), pltpu.VMEM((320, 768), BF16), pltpu.VMEM((320, 768), BF16)]
    mid, *out = call(coarse_conv, [((64, 256), F32)] * 3, (pair, *others, coarse_w), taken, flops=10**8)
    rim = over_slab(*out)
    return call(finish, [((64, 1, 256), F32)], (mid, *rim))[0]


def solution(mesh):
    placed = (
        P(None, "slab", "grp", None),
        P(),
        P(),
        P(),
        P(None, None, None, None, "grp"),
        P(None, None, None, None, "grp"),
    )
    return jax.shard_map(
        per_device, mesh=mesh, in_specs=placed, out_specs=P("grp", "slab", None), check_vma=False
    )
```

time: 98 us -> 74.5 us (0.76)
  waiting for transfers between devices: 40.9 us -> 28.1 us
  starting transfers between devices: 46.9 us -> 36.4 us
    ppermute x18, waiting for transfers between devices: 40.9 us -> 28.1 us  [permute(): return lax.ppermute(x, ('slab', 'grp'), pairs)]
    ppermute x18, starting transfers between devices: 46.9 us -> 36.4 us  [permute(): return lax.ppermute(x, ('slab', 'grp'), pairs)]
    pallas_call x10 -> x16, Pallas kernels: 6.56 us -> 7.53 us  [call(): pl.pallas_call(kernel, out_shape=[jax.ShapeDtypeStruct(s, t) for s, t in...]
    unnamed x15 -> x12, local copies, waits for them, and re-layouts: 1.98 us -> 2.23 us
  transfers between devices with their start and end apart: 18 -> 18, of which waited for: 13 -> 9; matrix products, arithmetic and copies ran while one was open for 0% -> 0% of each run, Pallas kernels for 5% -> 7%
where the time goes in v1:
time: 74.5 us; the launch traced here: 74.4 us
  starting transfers between devices  36.4 us (49%)
  waiting for transfers between devices  28.1 us (38%)
  Pallas kernels  7.53 us (10%)
  local copies, waits for them, and re-layouts  2.23 us (3%)
    ppermute x18, starting transfers between devices, permute(): return lax.ppermute(x, ('slab', 'grp'), pairs)  36.4 us
    ppermute x18, waiting for transfers between devices, permute(): return lax.ppermute(x, ('slab', 'grp'), pairs)  28.1 us
    pallas_call x16, Pallas kernels, call(): pl.pallas_call(kernel, out_shape=[jax.ShapeDtypeStruct(s, t) for s, t in...  7.53 us
    unnamed x12, local copies, waits for them, and re-layouts  2.23 us
  transfers between devices with their start and end apart: 18, of which 9 were waited for; matrix products, arithmetic and copies ran while one was open for 0% of the time, Pallas kernels for 7%

profile of v1, /device:TPU:4, one launch (start us, length us, event | category | flops | bytes accessed | tf_op | source)
XLA Modules:
  0.0 74.4 jit_solution(9400591917779263677)
XLA Ops:
  0.0 1.0 %copy-done.2 = f32[64,4,4,128]{3,2,1,0:T(4,128)S(1)} copy-done((f32[64,4,4,128]{3,2,1,0:T(4,128)S(1)}, f32[64,4,4,128]{3,2,1,0:T(4,128)}, u32[]{:S(2)}) %copy-start.2) | copy-done | bytes 524312
  1.0 0.1 edges.1
  1.1 1.3 %collective-permute-start = (f32[256,128]{1,0:T(8,128)S(1)}, f32[256,128]{1,0:T(8,128)S(1)}, u32[]{:S(2)}, u32[]{:S(2)}) collective-permute-start(f32[256,128]{1,0:T(8,128)S(1)} %get-tuple-element.28), channel_id=1, source_target_pairs={{0,1},{1,0},{2,3},{3,2},{4,5},{5,4},{6,7},{7,6},{8,9},{9,8},{10,11... | collective-permute-start | bytes 393224 | tf_op jit(solution)/shard_map/ppermute | solution.py:322
  2.4 1.6 %collective-permute-start.1 = (f32[256,128]{1,0:T(8,128)S(1)}, f32[256,128]{1,0:T(8,128)S(1)}, u32[]{:S(2)}, u32[]{:S(2)}) collective-permute-start(f32[256,128]{1,0:T(8,128)S(1)} %get-tuple-element.29), channel_id=1, source_target_pairs={{0,199},{1,2},{2,1},{3,4},{4,3},{5,6},{6,5},{7,192},{8,207},{9,10}... | collective-permute-start | bytes 393224 | tf_op jit(solution)/shard_map/ppermute | solution.py:322
  4.0 1.2 %copy-done.5 = f32[3,3,3,64,64]{4,3,2,1,0:T(8,128)S(1)} copy-done((f32[3,3,3,64,64]{4,3,2,1,0:T(8,128)S(1)}, f32[3,3,3,64,64]{4,3,2,1,0:T(8,128)}, u32[]{:S(2)}) %copy-start.5) | copy-done | bytes 442392
  5.2 2.0 %fine_own.1 = (f32[1536,128]{1,0:T(8,128)S(1)}, bf16[384,768]{1,0:T(8,128)(2,1)S(1)}) custom-call(f32[1024,128]{1,0:T(8,128)S(1)} %bitcast.13, f32[1728,64]{1,0:T(8,128)S(1)} %bitcast.16), custom_call_target="tpu_custom_call" | custom-call | flops 1000000000 | bytes 966656 | tf_op jit(solution)/shard_map/fine_own/pallas_call | solution.py:35
  7.2 0.0 copy-start.3
  7.2 5.7 %collective-permute-start.8 = (f32[128,128]{1,0:T(8,128)S(1)}, f32[128,128]{1,0:T(8,128)S(1)}, u32[]{:S(2)}, u32[]{:S(2)}) collective-permute-start(f32[128,128]{1,0:T(8,128)S(1)} %own_half.1.first), channel_id=1, source_target_pairs={{0,4},{1,5},{2,6},{3,7},{4,0},{5,1},{6,2},{7,3},{8,12},{9,13},{10,... | collective-permute-start | bytes 196616 | tf_op jit(solution)/shard_map/ppermute | solution.py:322
  12.9 0.0 collective-permute-done.near
  12.9 0.0 collective-permute-done.1.far
  12.9 0.0 copy-start.1
  12.9 0.6 fine_rim.1
  13.6 0.1 collective-permute-start.2
  13.7 2.9 %collective-permute-start.3 = (f32[256,128]{1,0:T(8,128)S(1)}, f32[256,128]{1,0:T(8,128)S(1)}, u32[]{:S(2)}, u32[]{:S(2)}) collective-permute-start(f32[256,128]{1,0:T(8,128)S(1)} %get-tuple-element.32), channel_id=1, source_target_pairs={{0,252},{1,253},{2,254},{3,255},{4,248},{5,249},{6,250},{7,251},{8... | collective-permute-start | bytes 393224 | tf_op jit(solution)/shard_map/ppermute | solution.py:322
  16.5 0.0 collective-permute-done.8.second
  16.6 8.4 %collective-permute-start.9 = (f32[256,128]{1,0:T(8,128)S(1)}, f32[256,128]{1,0:T(8,128)S(1)}, u32[]{:S(2)}, u32[]{:S(2)}) collective-permute-start(f32[256,128]{1,0:T(8,128)S(1)} %joined.4.first), channel_id=1, source_target_pairs={{0,1},{1,0},{2,3},{3,2},{4,5},{5,4},{6,7},{7,6},{8,9},{9,8},{10,11... | collective-permute-start | bytes 393224 | tf_op jit(solution)/shard_map/ppermute | solution.py:322
  25.0 0.0 collective-permute-done.2.near
  25.0 0.0 collective-permute-done.3.far
  25.0 0.5 first_down.1
  25.5 3.1 %collective-permute-done.9.second = f32[256,128]{1,0:T(8,128)S(1)} collective-permute-done((f32[256,128]{1,0:T(8,128)S(1)}, f32[256,128]{1,0:T(8,128)S(1)}, u32[]{:S(2)}, u32[]{:S(2)}) %collective-permute-start.9) | collective-permute-done | bytes 131104 | tf_op jit(solution)/shard_map/ppermute | solution.py:322
  28.7 0.8 %collective-permute-start.10 = (f32[512,128]{1,0:T(8,128)S(1)}, f32[512,128]{1,0:T(8,128)S(1)}, u32[]{:S(2)}, u32[]{:S(2)}) collective-permute-start(f32[512,128]{1,0:T(8,128)S(1)} %joined.5.first), channel_id=1, source_target_pairs={{0,3},{1,2},{2,1},{3,0},{4,7},{5,6},{6,5},{7,4},{8,11},{9,10},{10,... | collective-permute-start | bytes 786440 | tf_op jit(solution)/shard_map/ppermute | solution.py:322
  29.5 2.6 %collective-permute-start.4 = (f32[128,128]{1,0:T(8,128)S(1)}, f32[128,128]{1,0:T(8,128)S(1)}, u32[]{:S(2)}, u32[]{:S(2)}) collective-permute-start(f32[128,128]{1,0:T(8,128)S(1)} %get-tuple-element.36), channel_id=1, source_target_pairs={{0,1},{1,0},{2,3},{3,2},{4,5},{5,4},{6,7},{7,6},{8,9},{9,8},{10,11... | collective-permute-start | bytes 196616 | tf_op jit(solution)/shard_map/ppermute | solution.py:322
  32.1 1.1 %collective-permute-start.5 = (f32[128,128]{1,0:T(8,128)S(1)}, f32[128,128]{1,0:T(8,128)S(1)}, u32[]{:S(2)}, u32[]{:S(2)}) collective-permute-start(f32[128,128]{1,0:T(8,128)S(1)} %get-tuple-element.37), channel_id=1, source_target_pairs={{0,199},{1,2},{2,1},{3,4},{4,3},{5,6},{6,5},{7,192},{8,207},{9,10}... | collective-permute-start | bytes 196616 | tf_op jit(solution)/shard_map/ppermute | solution.py:322
  33.3 0.5 filters.1
  33.8 0.9 %middle_own.1.own = f32[256,384]{1,0:T(8,128)S(1)} custom-call(f32[128,128]{1,0:T(8,128)S(1)} %get-tuple-element.33.d_low.after, f32[128,128]{1,0:T(8,128)S(1)} %get-tuple-element.34.d_high, bf16[2304,384]{1,0:T(8,128)(2,1)S(1)} %get-tuple-element.35.w), custom_call_target="tpu_custom_call" | custom-call | flops 100000000 | bytes 1900544 | tf_op jit(solution)/shard_map/middle_own/pallas_call | solution.py:35
  34.7 1.7 %collective-permute-done.5.far = f32[128,128]{1,0:T(8,128)S(1)} collective-permute-done((f32[128,128]{1,0:T(8,128)S(1)}, f32[128,128]{1,0:T(8,128)S(1)}, u32[]{:S(2)}, u32[]{:S(2)}) %collective-permute-start.5) | collective-permute-done | bytes 65568 | tf_op jit(solution)/shard_map/ppermute | solution.py:322
  36.4 0.5 middle_rim.1
  37.0 0.1 collective-permute-start.11
  37.1 0.5 collective-permute-start.6
  37.6 0.9 %collective-permute-start.7 = (f32[128,128]{1,0:T(8,128)S(1)}, f32[128,128]{1,0:T(8,128)S(1)}, u32[]{:S(2)}, u32[]{:S(2)}) collective-permute-start(f32[128,128]{1,0:T(8,128)S(1)} %get-tuple-element.40), channel_id=1, source_target_pairs={{0,252},{1,253},{2,254},{3,255},{4,248},{5,249},{6,250},{7,251},{8... | collective-permute-start | bytes 196616 | tf_op jit(solution)/shard_map/ppermute | solution.py:322
  38.5 0.5 collective-permute-done.11.other
  39.0 0.2 gathered_filters.1
  39.2 5.4 %collective-permute-done.7.far = f32[128,128]{1,0:T(8,128)S(1)} collective-permute-done((f32[128,128]{1,0:T(8,128)S(1)}, f32[128,128]{1,0:T(8,128)S(1)}, u32[]{:S(2)}, u32[]{:S(2)}) %collective-permute-start.7) | collective-permute-done | bytes 65568 | tf_op jit(solution)/shard_map/ppermute | solution.py:322
  44.6 0.4 second_down.1.first.after
  45.0 1.9 %collective-permute-start.12 = (f32[32,256]{1,0:T(8,128)S(1)}, f32[32,256]{1,0:T(8,128)S(1)}, u32[]{:S(2)}, u32[]{:S(2)}) collective-permute-start(f32[32,256]{1,0:T(8,128)S(1)} %second_down.1.first.after), channel_id=1, source_target_pairs={{0,4},{1,5},{2,6},{3,7},{4,0},{5,1},{6,2},{7,3},{8,12},{9,13},{10,... | collective-permute-start | bytes 98312 | tf_op jit(solution)/shard_map/ppermute | solution.py:322
  46.9 6.0 %collective-permute-done.12.second = f32[32,256]{1,0:T(8,128)S(1)} collective-permute-done((f32[32,256]{1,0:T(8,128)S(1)}, f32[32,256]{1,0:T(8,128)S(1)}, u32[]{:S(2)}, u32[]{:S(2)}) %collective-permute-start.12) | collective-permute-done | bytes 32800 | tf_op jit(solution)/shard_map/ppermute | solution.py:322
  52.9 1.1 %collective-permute-start.15 = (f32[64,256]{1,0:T(8,128)S(1)}, f32[64,256]{1,0:T(8,128)S(1)}, u32[]{:S(2)}, u32[]{:S(2)}) collective-permute-start(f32[64,256]{1,0:T(8,128)S(1)} %joined.7.own), channel_id=1, source_target_pairs={{0,3},{1,2},{2,1},{3,0},{4,7},{5,6},{6,5},{7,4},{8,11},{9,10},{10,... | collective-permute-start | bytes 196616 | tf_op jit(solution)/shard_map/ppermute | solution.py:322
  54.0 7.2 %collective-permute-start.14 = (f32[64,256]{1,0:T(8,128)S(1)}, f32[64,256]{1,0:T(8,128)S(1)}, u32[]{:S(2)}, u32[]{:S(2)}) collective-permute-start(f32[64,256]{1,0:T(8,128)S(1)} %joined.7.own), channel_id=1, source_target_pairs={{0,2},{1,3},{2,0},{3,1},{4,6},{5,7},{6,4},{7,5},{8,10},{9,11},{10,... | collective-permute-start | bytes 196616 | tf_op jit(solution)/shard_map/ppermute | solution.py:322
  61.2 0.0 collective-permute-start.13
  61.2 0.0 collective-permute-done.15.three
  61.2 2.2 %collective-permute-done.14.two = f32[64,256]{1,0:T(8,128)S(1)} collective-permute-done((f32[64,256]{1,0:T(8,128)S(1)}, f32[64,256]{1,0:T(8,128)S(1)}, u32[]{:S(2)}, u32[]{:S(2)}) %collective-permute-start.14) | collective-permute-done | bytes 65568 | tf_op jit(solution)/shard_map/ppermute | solution.py:322
  63.5 2.0 %collective-permute-done.13.one = f32[64,256]{1,0:T(8,128)S(1)} collective-permute-done((f32[64,256]{1,0:T(8,128)S(1)}, f32[64,256]{1,0:T(8,128)S(1)}, u32[]{:S(2)}, u32[]{:S(2)}) %collective-permute-start.13) | collective-permute-done | bytes 65568 | tf_op jit(solution)/shard_map/ppermute | solution.py:322
  65.5 1.0 %coarse_conv.1 = (f32[64,256]{1,0:T(8,128)S(1)}, f32[64,256]{1,0:T(8,128)S(1)}, f32[64,256]{1,0:T(8,128)S(1)}) custom-call(f32[64,256]{1,0:T(8,128)S(1)} %joined.7.own, f32[64,256]{1,0:T(8,128)S(1)} %collective-permute-done.13.one, f32[64,256]{1,0:T(8,128)S(1)} %collective-permute-done.14.two, f32[64,256]{1,0:T(8,128)S(1)} %collective-permute-done.15.three, ...), custom_call_target="tpu_custom_call" | custom-call | flops 100000000 | bytes 2031616 | tf_op jit(solution)/shard_map/coarse_conv/pallas_call | solution.py:35
  66.5 0.1 collective-permute-start.16
  66.6 0.1 collective-permute-start.17
  66.7 1.1 %collective-permute-done.16.near = f32[64,256]{1,0:T(8,128)S(1)} collective-permute-done((f32[64,256]{1,0:T(8,128)S(1)}, f32[64,256]{1,0:T(8,128)S(1)}, u32[]{:S(2)}, u32[]{:S(2)}) %collective-permute-start.16) | collective-permute-done | bytes 65568 | tf_op jit(solution)/shard_map/ppermute | solution.py:322
  67.8 5.9 %collective-permute-done.17.far = f32[64,256]{1,0:T(8,128)S(1)} collective-permute-done((f32[64,256]{1,0:T(8,128)S(1)}, f32[64,256]{1,0:T(8,128)S(1)}, u32[]{:S(2)}, u32[]{:S(2)}) %collective-permute-start.17) | collective-permute-done | bytes 65568 | tf_op jit(solution)/shard_map/ppermute | solution.py:322
  73.7 0.7 finish.1
  (16 shorter events, 0.1 us)
Async XLA Ops:
  0.0 1.0 %copy-start.2 = (f32[64,4,4,128]{3,2,1,0:T(4,128)S(1)}, f32[64,4,4,128]{3,2,1,0:T(4,128)}, u32[]{:S(2)}) copy-start(f32[64,4,4,128]{3,2,1,0:T(4,128)} %param.6) | copy-start | bytes 1572868
  1.1 11.8 %collective-permute-start = (f32[256,128]{1,0:T(8,128)S(1)}, f32[256,128]{1,0:T(8,128)S(1)}, u32[]{:S(2)}, u32[]{:S(2)}) collective-permute-start(f32[256,128]{1,0:T(8,128)S(1)} %get-tuple-element.28), channel_id=1, source_target_pairs={{0,1},{1,0},{2,3},{3,2},{4,5},{5,4},{6,7},{7,6},{8,9},{9,8},{10,11... | collective-permute-start | bytes 393224 | tf_op jit(solution)/shard_map/ppermute | solution.py:322
  2.4 10.5 %collective-permute-start.1 = (f32[256,128]{1,0:T(8,128)S(1)}, f32[256,128]{1,0:T(8,128)S(1)}, u32[]{:S(2)}, u32[]{:S(2)}) collective-permute-start(f32[256,128]{1,0:T(8,128)S(1)} %get-tuple-element.29), channel_id=1, source_target_pairs={{0,199},{1,2},{2,1},{3,4},{4,3},{5,6},{6,5},{7,192},{8,207},{9,10}... | collective-permute-start | bytes 393224 | tf_op jit(solution)/shard_map/ppermute | solution.py:322
  4.0 1.2 %copy-start.5 = (f32[3,3,3,64,64]{4,3,2,1,0:T(8,128)S(1)}, f32[3,3,3,64,64]{4,3,2,1,0:T(8,128)}, u32[]{:S(2)}) copy-start(f32[3,3,3,64,64]{4,3,2,1,0:T(8,128)} %param.7) | copy-start | bytes 1327108
  5.2 2.0 %copy-start.4 = (f32[2,2,2,128,32]{3,4,2,1,0:T(8,128)S(1)}, f32[2,2,2,128,32]{3,4,2,1,0:T(8,128)}, u32[]{:S(2)}) copy-start(f32[2,2,2,128,32]{3,4,2,1,0:T(8,128)} %param.10) | copy-start | bytes 393220
  7.2 17.8 %copy-start.3 = (f32[2,2,2,64,128]{4,3,2,1,0:T(8,128)S(1)}, f32[2,2,2,64,128]{4,3,2,1,0:T(8,128)}, u32[]{:S(2)}) copy-start(f32[2,2,2,64,128]{4,3,2,1,0:T(8,128)} %param.8) | copy-start | bytes 786436
  7.2 9.3 %collective-permute-start.8 = (f32[128,128]{1,0:T(8,128)S(1)}, f32[128,128]{1,0:T(8,128)S(1)}, u32[]{:S(2)}, u32[]{:S(2)}) collective-permute-start(f32[128,128]{1,0:T(8,128)S(1)} %own_half.1.first), channel_id=1, source_target_pairs={{0,4},{1,5},{2,6},{3,7},{4,0},{5,1},{6,2},{7,3},{8,12},{9,13},{10,... | collective-permute-start | bytes 196616 | tf_op jit(solution)/shard_map/ppermute | solution.py:322
  12.9 20.4 %copy-start = (f32[3,3,3,128,128]{4,3,2,1,0:T(8,128)S(1)}, f32[3,3,3,128,128]{4,3,2,1,0:T(8,128)}, u32[]{:S(2)}) copy-start(f32[3,3,3,128,128]{4,3,2,1,0:T(8,128)} %param.9) | copy-start | bytes 5308420
  12.9 20.3 %copy-start.1 = (f32[3,3,3,256,64]{3,4,2,1,0:T(8,128)S(1)}, f32[3,3,3,256,64]{3,4,2,1,0:T(8,128)}, u32[]{:S(2)}) copy-start(f32[3,3,3,256,64]{3,4,2,1,0:T(8,128)} %param.11) | copy-start | bytes 5308420
  13.6 11.4 %collective-permute-start.2 = (f32[256,128]{1,0:T(8,128)S(1)}, f32[256,128]{1,0:T(8,128)S(1)}, u32[]{:S(2)}, u32[]{:S(2)}) collective-permute-start(f32[256,128]{1,0:T(8,128)S(1)} %get-tuple-element.31), channel_id=1, source_target_pairs={{0,8},{1,9},{2,10},{3,11},{4,12},{5,13},{6,14},{7,15},{8,0},{9,1},... | collective-permute-start | bytes 393224 | tf_op jit(solution)/shard_map/ppermute | solution.py:322
  13.7 11.3 %collective-permute-start.3 = (f32[256,128]{1,0:T(8,128)S(1)}, f32[256,128]{1,0:T(8,128)S(1)}, u32[]{:S(2)}, u32[]{:S(2)}) collective-permute-start(f32[256,128]{1,0:T(8,128)S(1)} %get-tuple-element.32), channel_id=1, source_target_pairs={{0,252},{1,253},{2,254},{3,255},{4,248},{5,249},{6,250},{7,251},{8... | collective-permute-start | bytes 393224 | tf_op jit(solution)/shard_map/ppermute | solution.py:322
  16.6 12.1 %collective-permute-start.9 = (f32[256,128]{1,0:T(8,128)S(1)}, f32[256,128]{1,0:T(8,128)S(1)}, u32[]{:S(2)}, u32[]{:S(2)}) collective-permute-start(f32[256,128]{1,0:T(8,128)S(1)} %joined.4.first), channel_id=1, source_target_pairs={{0,1},{1,0},{2,3},{3,2},{4,5},{5,4},{6,7},{7,6},{8,9},{9,8},{10,11... | collective-permute-start | bytes 393224 | tf_op jit(solution)/shard_map/ppermute | solution.py:322
  28.7 8.3 %collective-permute-start.10 = (f32[512,128]{1,0:T(8,128)S(1)}, f32[512,128]{1,0:T(8,128)S(1)}, u32[]{:S(2)}, u32[]{:S(2)}) collective-permute-start(f32[512,128]{1,0:T(8,128)S(1)} %joined.5.first), channel_id=1, source_target_pairs={{0,3},{1,2},{2,1},{3,0},{4,7},{5,6},{6,5},{7,4},{8,11},{9,10},{10,... | collective-permute-start | bytes 786440 | tf_op jit(solution)/shard_map/ppermute | solution.py:322
  29.5 5.2 %collective-permute-start.4 = (f32[128,128]{1,0:T(8,128)S(1)}, f32[128,128]{1,0:T(8,128)S(1)}, u32[]{:S(2)}, u32[]{:S(2)}) collective-permute-start(f32[128,128]{1,0:T(8,128)S(1)} %get-tuple-element.36), channel_id=1, source_target_pairs={{0,1},{1,0},{2,3},{3,2},{4,5},{5,4},{6,7},{7,6},{8,9},{9,8},{10,11... | collective-permute-start | bytes 196616 | tf_op jit(solution)/shard_map/ppermute | solution.py:322
  32.1 4.3 %collective-permute-start.5 = (f32[128,128]{1,0:T(8,128)S(1)}, f32[128,128]{1,0:T(8,128)S(1)}, u32[]{:S(2)}, u32[]{:S(2)}) collective-permute-start(f32[128,128]{1,0:T(8,128)S(1)} %get-tuple-element.37), channel_id=1, source_target_pairs={{0,199},{1,2},{2,1},{3,4},{4,3},{5,6},{6,5},{7,192},{8,207},{9,10}... | collective-permute-start | bytes 196616 | tf_op jit(solution)/shard_map/ppermute | solution.py:322
  37.0 2.0 %collective-permute-start.11 = (f32[1024,128]{1,0:T(8,128)S(1)}, f32[1024,128]{1,0:T(8,128)S(1)}, u32[]{:S(2)}, u32[]{:S(2)}) collective-permute-start(f32[1024,128]{1,0:T(8,128)S(1)} %joined.6.mine), channel_id=1, source_target_pairs={{0,8},{1,9},{2,10},{3,11},{4,12},{5,13},{6,14},{7,15},{8,0},{9,1},... | collective-permute-start | bytes 1572872 | tf_op jit(solution)/shard_map/ppermute | solution.py:322
  37.1 2.1 %collective-permute-start.6 = (f32[128,128]{1,0:T(8,128)S(1)}, f32[128,128]{1,0:T(8,128)S(1)}, u32[]{:S(2)}, u32[]{:S(2)}) collective-permute-start(f32[128,128]{1,0:T(8,128)S(1)} %get-tuple-element.39), channel_id=1, source_target_pairs={{0,8},{1,9},{2,10},{3,11},{4,12},{5,13},{6,14},{7,15},{8,0},{9,1},... | collective-permute-start | bytes 196616 | tf_op jit(solution)/shard_map/ppermute | solution.py:322
  37.6 7.0 %collective-permute-start.7 = (f32[128,128]{1,0:T(8,128)S(1)}, f32[128,128]{1,0:T(8,128)S(1)}, u32[]{:S(2)}, u32[]{:S(2)}) collective-permute-start(f32[128,128]{1,0:T(8,128)S(1)} %get-tuple-element.40), channel_id=1, source_target_pairs={{0,252},{1,253},{2,254},{3,255},{4,248},{5,249},{6,250},{7,251},{8... | collective-permute-start | bytes 196616 | tf_op jit(solution)/shard_map/ppermute | solution.py:322
  45.0 7.9 %collective-permute-start.12 = (f32[32,256]{1,0:T(8,128)S(1)}, f32[32,256]{1,0:T(8,128)S(1)}, u32[]{:S(2)}, u32[]{:S(2)}) collective-permute-start(f32[32,256]{1,0:T(8,128)S(1)} %second_down.1.first.after), channel_id=1, source_target_pairs={{0,4},{1,5},{2,6},{3,7},{4,0},{5,1},{6,2},{7,3},{8,12},{9,13},{10,... | collective-permute-start | bytes 98312 | tf_op jit(solution)/shard_map/ppermute | solution.py:322
  52.9 8.3 %collective-permute-start.15 = (f32[64,256]{1,0:T(8,128)S(1)}, f32[64,256]{1,0:T(8,128)S(1)}, u32[]{:S(2)}, u32[]{:S(2)}) collective-permute-start(f32[64,256]{1,0:T(8,128)S(1)} %joined.7.own), channel_id=1, source_target_pairs={{0,3},{1,2},{2,1},{3,0},{4,7},{5,6},{6,5},{7,4},{8,11},{9,10},{10,... | collective-permute-start | bytes 196616 | tf_op jit(solution)/shard_map/ppermute | solution.py:322
  54.0 9.4 %collective-permute-start.14 = (f32[64,256]{1,0:T(8,128)S(1)}, f32[64,256]{1,0:T(8,128)S(1)}, u32[]{:S(2)}, u32[]{:S(2)}) collective-permute-start(f32[64,256]{1,0:T(8,128)S(1)} %joined.7.own), channel_id=1, source_target_pairs={{0,2},{1,3},{2,0},{3,1},{4,6},{5,7},{6,4},{7,5},{8,10},{9,11},{10,... | collective-permute-start | bytes 196616 | tf_op jit(solution)/shard_map/ppermute | solution.py:322
  61.2 4.3 %collective-permute-start.13 = (f32[64,256]{1,0:T(8,128)S(1)}, f32[64,256]{1,0:T(8,128)S(1)}, u32[]{:S(2)}, u32[]{:S(2)}) collective-permute-start(f32[64,256]{1,0:T(8,128)S(1)} %joined.7.own), channel_id=1, source_target_pairs={{0,1},{1,0},{2,3},{3,2},{4,5},{5,4},{6,7},{7,6},{8,9},{9,8},{10,11... | collective-permute-start | bytes 196616 | tf_op jit(solution)/shard_map/ppermute | solution.py:322
  66.5 1.3 %collective-permute-start.16 = (f32[64,256]{1,0:T(8,128)S(1)}, f32[64,256]{1,0:T(8,128)S(1)}, u32[]{:S(2)}, u32[]{:S(2)}) collective-permute-start(f32[64,256]{1,0:T(8,128)S(1)} %get-tuple-element.45), channel_id=1, source_target_pairs={{0,8},{1,9},{2,10},{3,11},{4,12},{5,13},{6,14},{7,15},{8,0},{9,1},... | collective-permute-start | bytes 196616 | tf_op jit(solution)/shard_map/ppermute | solution.py:322
  66.6 7.1 %collective-permute-start.17 = (f32[64,256]{1,0:T(8,128)S(1)}, f32[64,256]{1,0:T(8,128)S(1)}, u32[]{:S(2)}, u32[]{:S(2)}) collective-permute-start(f32[64,256]{1,0:T(8,128)S(1)} %get-tuple-element.46), channel_id=1, source_target_pairs={{0,252},{1,253},{2,254},{3,255},{4,248},{5,249},{6,250},{7,251},{8... | collective-permute-start | bytes 196616 | tf_op jit(solution)/shard_map/ppermute | solution.py:322

commit v2 on v1

--- a/solution.py
+++ b/solution.py
@@ -32,8 +32,13 @@
 def call(kernel, outs, args, scratch=(), flops=0, after=()):
     vmem = pl.BlockSpec(memory_space=pltpu.VMEM)
     size = sum(a.size * a.dtype.itemsize for a in args)
+    n = len(args)
+
+    def body(*refs):
+        kernel(*refs[:n], *refs[n + len(after) :])
+
     return pl.pallas_call(
-        kernel,
+        body,
         out_shape=[jax.ShapeDtypeStruct(s, t) for s, t in outs],
         in_specs=[vmem] * len(args) + [pl.BlockSpec(memory_space=pl.ANY)] * len(after),
         out_specs=[vmem] * len(outs),
@@ -64,17 +69,18 @@
 
 
 def edges(vol, near, far):
-    for d in range(4):
-        first = vol[pl.ds(d * 4, 64, stride=16), :]
-        last = vol[pl.ds(d * 4 + 3, 64, stride=16), :]
-        send(near, far, pl.ds(d * 64, 64), last, first, "grp")
-
-
-def own_half(w2, after, half):
+    for i in range(3):
+        for d in range(4):
+            low = vol[pl.ds(d * 4 + i, 64, stride=16), :]
+            high = vol[pl.ds(d * 4 + i + 1, 64, stride=16), :]
+            send(near, far, pl.ds((i * 4 + d) * 64, 64), high, low, "grp")
+
+
+def own_half(w2, half):
     half[...] = w2[pl.ds(pl.multiple_of(parity("slab") * 128, 128), 128), :]
 
 
-def joined(first, second, after, out):
+def joined(first, second, out):
     n = first.shape[0]
     out[:n, :] = first[...]
     out[n:, :] = second[...]
@@ -126,75 +132,92 @@
     for d in range(4):
         for h in range(4):
             put_shifted(vol[pl.ds(d * 4 + h, 64, stride=16), :], high, low, d // 2, h * 256, d % 2 * 128)
-    for h in range(4):
+    for h in range(-1, 5):
         first, last = max(h - 1, 0), min(h + 1, 3)
         rows = slice(first * 256, last * 256 + 256)
         lanes = slice((first - h + 1) * 256, (last - h + 2) * 256)
         weights = wt[:, lanes]
         parts = [taps(weights, high[lead, rows, :], low[lead, rows, :]) for lead in range(2)]
         for i, value in enumerate(planes(*parts)):
-            acc[i * 256 + h * 64 : i * 256 + h * 64 + 64, :] = value
-
-
-def fine_rim(acc, wt, near, far, inner, out_near, out_far, high, low):
-    zeros = jnp.zeros((64, 256), BF16)
+            acc[i * 384 + h * 64 + 64 : i * 384 + h * 64 + 128, :] = value
+
+
+def rim_sums(side, acc, wt, ref, inside, high, low):
+    for i in range(3):
+        for lead in range(2):
+            high[lead, i * 256 + 192 : i * 256 + 256, :] = jnp.zeros((64, 256), BF16)
+            low[lead, i * 256 + 192 : i * 256 + 256, :] = jnp.zeros((64, 256), BF16)
+        for d in range(4):
+            x = jnp.where(inside, ref[(i * 4 + d) * 64 : (i * 4 + d) * 64 + 64, :], 0.0)
+            put_shifted(x, high, low, d // 2, i * 256, d % 2 * 128)
+    found = []
+    for j in range(3):
+        h = (j - 2, j + 3)[side]
+        first, last = (j, 2) if side == 0 else (0, j)
+        rows = slice(first * 256, last * 256 + 256)
+        tap = first - j if side == 0 else 2 - j
+        weights = wt[:, tap * 256 : tap * 256 + (last - first + 1) * 256]
+        sums = planes(*[taps(weights, high[lead, rows, :], low[lead, rows, :]) for lead in range(2)])
+        if -1 <= h <= 4:
+            sums = [v + acc[i * 384 + h * 64 + 64 : i * 384 + h * 64 + 128, :] for i, v in enumerate(sums)]
+        found.append(sums)
+    return found
+
+
+def in_grp(side):
+    place = lax.axis_index("grp")
+    return place > 0 if side == 0 else place < lax.axis_size("grp") - 1
+
+
+def fine_near(acc, wt, ref, out, high, low):
     for side in range(2):
-        for lead in range(2):
-            high[side * 2 + lead, 192:256, :] = zeros
-            low[side * 2 + lead, 192:256, :] = zeros
-    for d in range(4):
-        below, above = received(near, far, pl.ds(d * 64, 64), "grp")
-        put_shifted(below, high, low, d // 2, 0, d % 2 * 128)
-        put_shifted(above, high, low, 2 + d // 2, 0, d % 2 * 128)
+        @pl.when(parity("grp") == 1 - side)
+        def _():
+            for j, sums in enumerate(rim_sums(side, acc, wt, ref, in_grp(side), high, low)):
+                for i, value in enumerate(sums):
+                    out[(i * 3 + j) * 64 : (i * 3 + j) * 64 + 64, :] = value
+
+
+def fine_far(acc, wt, ref, other, inner, out_near, out_far, high, low):
+    def put(h, sums):
+        at = (h + 2) * 64
+        send(out_near, out_far, pl.ds(at, 64), sums[5], sums[0], "slab")
+        for d in range(4):
+            inner[d * 512 + at : d * 512 + at + 64, :] = sums[d + 1]
+
     for side in range(2):
-        h = (0, 3)[side]
-        weights = wt[:, side * 512 : side * 512 + 256]
-        parts = [taps(weights, high[side * 2 + lead], low[side * 2 + lead]) for lead in range(2)]
-        totals = planes(*parts)
-        for i, value in enumerate(totals):
-            totals[i] = value + acc[i * 256 + h * 64 : i * 256 + h * 64 + 64, :]
-            if 0 < i < 5:
-                inner[(i - 1) * 128 + side * 64 : (i - 1) * 128 + side * 64 + 64, :] = totals[i]
-        send(out_near, out_far, pl.ds(h * 64, 64), totals[5], totals[0], "slab")
+        @pl.when(parity("grp") == side)
+        def _():
+            for j, sums in enumerate(rim_sums(side, acc, wt, ref, in_grp(side), high, low)):
+                put((j - 2, j + 3)[side], sums)
+                put((j + 3, j - 2)[side], [other[(i * 3 + j) * 64 : (i * 3 + j) * 64 + 64, :] for i in range(6)])
     for h in (1, 2):
-        at = pl.ds(h * 64, 64)
-        send(out_near, out_far, at, acc[5 * 256 + h * 64 : 5 * 256 + h * 64 + 64, :], acc[at, :], "slab")
-
-
-def first_down(acc, inner, near, far, w, out_low, out_high, out_near, out_far, cells, whi, wlo):
+        put(h, [acc[i * 384 + h * 64 + 64 : i * 384 + h * 64 + 128, :] for i in range(6)])
+
+
+def first_down(inner, near, far, w, out, cells, whi, wlo):
     for a in range(2):
         for bk in range(4):
             hi, lo = split(w[(a * 4 + bk) * 64 : (a * 4 + bk) * 64 + 64, :])
             whi[(bk * 2 + a) * 64 : (bk * 2 + a) * 64 + 64, :] = hi
             wlo[(bk * 2 + a) * 64 : (bk * 2 + a) * 64 + 64, :] = lo
-    for h in range(4):
+    for h in range(8):
         before, after = received(near, far, pl.ds(h * 64, 64), "slab")
-        level = []
-        for d in range(4):
-            if h in (0, 3):
-                at = d * 128 + (h == 3) * 64
-                v = inner[at : at + 64, :]
-            else:
-                at = (d + 1) * 256 + h * 64
-                v = acc[at : at + 64, :]
-            if d == 0:
-                v = v + before
-            if d == 3:
-                v = v + after
-            level.append(gelu(v))
+        level = [inner[d * 512 + h * 64 : d * 512 + h * 64 + 64, :] for d in range(4)]
+        level = [gelu(v) for v in (level[0] + before, level[1], level[2], level[3] + after)]
         for d2 in range(2):
             cells[h * 2 + d2] = jnp.concatenate(level[2 * d2 : 2 * d2 + 2], axis=0).T
-    results = []
-    for h2 in range(2):
+    for h2 in range(4):
         rows = []
         for d2 in range(2):
             rows.append(jnp.concatenate(
                 [cells[(2 * h2 + b) * 2 + d2, pl.ds(k, 64, stride=2), :] for b in range(2) for k in range(2)], axis=1))
         hi, lo = split(jnp.concatenate(rows, axis=0))
         both = mm(jnp.concatenate([hi, lo], axis=0), whi[...])
-        results.append(both[:128] + both[128:] + mm(hi, wlo[...]))
-    out_low[...], out_high[...] = results
-    send(out_near, out_far, slice(None), results[1], results[0], "grp")
+        value = both[:128] + both[128:] + mm(hi, wlo[...])
+        if h2 in (0, 3):
+            value = jnp.where(in_grp(h2 // 3), value, 0.0)
+        out[h2 * 128 : h2 * 128 + 128, :] = value
 
 
 def filters(wm, wc, mid, coarse):
@@ -230,42 +253,25 @@
     return x
 
 
-def put_rows(x, high, low, lead, row):
-    for k in range(3):
-        hi, lo = split(shifted_rows(x, k, 64))
-        high[lead, row : row + 64, k * 128 : k * 128 + 128] = hi
-        low[lead, row : row + 64, k * 128 : k * 128 + 128] = lo
-
-
-def middle_taps(high, low, leads, rows, w, b):
-    hi = [high[lead, rows, :] for lead in leads]
-    lo = [low[lead, rows, :] for lead in leads]
-    n = sum(x.shape[0] for x in hi)
-    both = mm(jnp.concatenate(hi + lo, axis=0), w[b * 384 : b * 384 + 384, :])
-    return both[:n] + both[n:] + mm(jnp.concatenate(hi, axis=0), w[1152 + b * 384 : 1152 + b * 384 + 384, :])
-
-
-def middle_own(d_low, d_high, w, total, high, low):
-    for i, ref in enumerate((d_low, d_high)):
+def middle(cells, w, inner, out_near, out_far, high, low):
+    for h in range(4):
         for d in range(2):
-            put_rows(ref[d * 64 : d * 64 + 64, :], high, low, i, d * 64)
-    every = slice(0, 128)
-    center = middle_taps(high, low, (0, 1), every, w, 1)
-    total[:128, :] = center[:128] + middle_taps(high, low, (1,), every, w, 2)
-    total[128:, :] = center[128:] + middle_taps(high, low, (0,), every, w, 0)
-
-
-def middle_rim(own, near, far, w, inner, out_near, out_far, high, low):
-    for d in range(2):
-        below, above = received(near, far, pl.ds(d * 64, 64), "grp")
-        put_rows(below, high, low, 0, d * 64)
-        put_rows(above, high, low, 1, d * 64)
-    every = slice(0, 128)
-    for h in range(2):
-        total = own[h * 128 : h * 128 + 128, :] + middle_taps(high, low, (h,), every, w, 2 * h)
-        inner[h * 64 : h * 64 + 64, :] = total[:64, 128:256] + total[64:, 256:]
-        inner[128 + h * 64 : 128 + h * 64 + 64, :] = total[:64, :128] + total[64:, 128:256]
-        send(out_near, out_far, pl.ds(h * 64, 64), total[64:, :128], total[:64, 256:], "slab")
+            x = cells[h * 128 + d * 64 : h * 128 + d * 64 + 64, :]
+            for k in range(3):
+                hi, lo = split(shifted_rows(x, k, 64))
+                high[d, h * 64 : h * 64 + 64, k * 128 : k * 128 + 128] = hi
+                low[d, h * 64 : h * 64 + 64, k * 128 : k * 128 + 128] = lo
+    total = jnp.zeros((256, 384), F32)
+    for b in range(3):
+        rows = slice(b * 64, b * 64 + 128)
+        hi = [high[d, rows, :] for d in range(2)]
+        lo = [low[d, rows, :] for d in range(2)]
+        both = mm(jnp.concatenate(hi + lo, axis=0), w[b * 384 : b * 384 + 384, :])
+        rest = mm(jnp.concatenate(hi, axis=0), w[1152 + b * 384 : 1152 + b * 384 + 384, :])
+        total = total + (both[:256] + both[256:] + rest)
+    inner[:128, :] = total[:128, 128:256] + total[128:, 256:]
+    inner[128:, :] = total[:128, :128] + total[128:, 128:256]
+    send(out_near, out_far, slice(None), total[128:, :128], total[:128, 256:], "slab")
 
 
 def second_down(inner, near, far, whi, wlo, out, cells):
@@ -307,7 +313,9 @@
 
 def finish(mid, near, far, out):
     before, after = received(near, far, slice(None), "slab")
-    out[:, 0, :] = gelu(mid[...] + before + after)
+    v = gelu(mid[...] + before + after)
+    for j in range(2):
+        out[pl.ds(j, 64, stride=2), :] = v[:, j * 128 : j * 128 + 128]
 
 
 def per_device(volume, conv_fine, down_first, conv_middle, down_second, conv_coarse):
@@ -354,31 +362,33 @@
     w2 = jnp.swapaxes(down_second, 3, 4).reshape(256, 128)
     wc = jnp.swapaxes(conv_coarse, 3, 4).reshape(1728, 256)
 
-    rim = over_grp(*call(edges, [((256, 128), F32)] * 2, (vol,)))
+    near, far = call(edges, [((768, 128), F32)] * 2, (vol,))
+    (half,) = call(own_half, [((128, 128), F32)], (w2,), after=(near,))
+    near, far = over_grp(near, far)
     taken = [pltpu.VMEM((2, 1024, 256), BF16)] * 2
-    acc, wt = call(fine_own, [((1536, 128), F32), ((384, 768), BF16)], (vol, w1), taken, flops=10**9)
-    (half,) = call(own_half, [((128, 128), F32)], (w2,), after=(acc,))
+    acc, wt = call(
+        fine_own, [((2304, 128), F32), ((384, 768), BF16)], (vol, w1), taken, flops=10**9, after=(half,))
     second = swap(half, "grp", 4)
-
-    taken = [pltpu.VMEM((4, 256, 256), BF16)] * 2
-    inner, *out = call(fine_rim, [((512, 128), F32)] + [((256, 128), F32)] * 2, (acc, wt, *rim), taken, flops=10**8)
+    taken = [pltpu.VMEM((2, 768, 256), BF16)] * 2
+    (near,) = call(fine_near, [((1152, 128), F32)], (acc, wt, near), taken, flops=10**8)
+    two = join(half, second, near)
+    second = swap(two, "grp", 1)
+    mid_w, coarse_w = call(filters, [((2304, 384), BF16), ((384, 2304), BF16)], (wm, wc), flops=10**8, after=(near,))
+    inner, *out = call(
+        fine_far, [((2048, 128), F32)] + [((512, 128), F32)] * 2, (acc, wt, far, near), taken, flops=10**8,
+        after=(two, mid_w))
     rim = over_slab(*out)
-    two = join(half, second, inner)
-    second = swap(two, "grp", 1)
-    mid_w, coarse_w = call(filters, [((2304, 384), BF16), ((384, 2304), BF16)], (wm, wc), flops=10**8)
-
-    taken = [pltpu.VMEM((8, 128, 128), F32), pltpu.VMEM((512, 128), BF16), pltpu.VMEM((512, 128), BF16)]
-    d_low, d_high, *out = call(first_down, [((128, 128), F32)] * 4, (acc, inner, *rim, wd1), taken, flops=10**8)
-    rim = over_grp(*out)
-    four = join(two, second, d_low)
+    four = join(two, second, inner)
     second = swap(four, "grp", 3)
-    taken = [pltpu.VMEM((2, 128, 384), BF16)] * 2
-    (own,) = call(middle_own, [((256, 384), F32)], (d_low, d_high, mid_w), taken, flops=10**8)
+
+    taken = [pltpu.VMEM((16, 128, 128), F32), pltpu.VMEM((512, 128), BF16), pltpu.VMEM((512, 128), BF16)]
+    (cells,) = call(first_down, [((512, 128), F32)], (inner, *rim, wd1), taken, flops=10**8)
+    mine = join(four, second, cells)
+    other = swap(mine, "slab", 1)
+    taken = [pltpu.VMEM((2, 256, 384), BF16)] * 2
     inner, *out = call(
-        middle_rim, [((256, 128), F32)] + [((128, 128), F32)] * 2, (own, *rim, mid_w), taken, flops=10**8)
+        middle, [((256, 128), F32)] + [((128, 128), F32)] * 2, (cells, mid_w), taken, flops=10**8)
     rim = over_slab(*out)
-    mine = join(four, second, inner)
-    other = swap(mine, "slab", 1)
     whi, wlo = call(gathered_filters, [((2, 256, 512), BF16)] * 2, (mine, other))
     (row,) = call(
         second_down, [((32, 256), F32)], (inner, *rim, whi, wlo), [pltpu.VMEM((256, 128), F32)], flops=10**8)
@@ -388,7 +398,7 @@
     taken = [pltpu.VMEM((256, 256), F32), pltpu.VMEM((320, 768), BF16), pltpu.VMEM((320, 768), BF16)]
     mid, *out = call(coarse_conv, [((64, 256), F32)] * 3, (pair, *others, coarse_w), taken, flops=10**8)
     rim = over_slab(*out)
-    return call(finish, [((64, 1, 256), F32)], (mid, *rim))[0]
+    return call(finish, [((128, 128), F32)], (mid, *rim))[0].reshape(64, 1, 256)
 
 
 def solution(mesh):

time: 74.5 us -> 80 us (1.074); the launches traced: 74.4 us -> 78.8 us
  starting transfers between devices: 36.4 us -> 40.6 us
  waiting for transfers between devices: 28.1 us -> 24 us
  Pallas kernels: 7.53 us -> 9.82 us
  local copies, waits for them, and re-layouts: 2.23 us -> 4.17 us
    ppermute x18 -> x16, starting transfers between devices: 36.4 us -> 40.6 us  [permute(): return lax.ppermute(x, ('slab', 'grp'), pairs)]
    ppermute x18 -> x16, waiting for transfers between devices: 28.1 us -> 24 us  [permute(): return lax.ppermute(x, ('slab', 'grp'), pairs)]
    pallas_call x16, Pallas kernels: 7.53 us -> 9.82 us  [call(): pl.pallas_call(body, out_shape=[jax.ShapeDtypeStruct(s, t) for s, t in ou...]
    unnamed x12 -> x14, local copies, waits for them, and re-layouts: 2.23 us -> 4.17 us
  transfers between devices with their start and end apart: 18 -> 16, of which waited for: 9 -> 7; matrix products, arithmetic and copies ran while one was open for 0% -> 0% of each run, Pallas kernels for 7% -> 9%
where the time goes in v2:
time: 80 us; the launch traced here: 78.8 us
  starting transfers between devices  40.6 us (51%)
  waiting for transfers between devices  24 us (30%)
  Pallas kernels  9.82 us (12%)
  local copies, waits for them, and re-layouts  4.17 us (5%)
    ppermute x16, starting transfers between devices, permute(): return lax.ppermute(x, ('slab', 'grp'), pairs)  40.6 us
    ppermute x16, waiting for transfers between devices, permute(): return lax.ppermute(x, ('slab', 'grp'), pairs)  24 us
    pallas_call x16, Pallas kernels, call(): pl.pallas_call(body, out_shape=[jax.ShapeDtypeStruct(s, t) for s, t in ou...  9.82 us
    unnamed x14, local copies, waits for them, and re-layouts  4.17 us
  transfers between devices with their start and end apart: 16, of which 7 were waited for; matrix products, arithmetic and copies ran while one was open for 0% of the time, Pallas kernels for 9%

profile of v2, /device:TPU:4, one launch (start us, length us, event | category | flops | bytes accessed | tf_op | source)
XLA Modules:
  0.0 78.8 jit_solution(14798338881556626599)
XLA Ops:
  0.0 1.0 %copy-done.2 = f32[64,4,4,128]{3,2,1,0:T(4,128)S(1)} copy-done((f32[64,4,4,128]{3,2,1,0:T(4,128)S(1)}, f32[64,4,4,128]{3,2,1,0:T(4,128)}, u32[]{:S(2)}) %copy-start.2) | copy-done | bytes 524312
  1.0 0.2 edges.1
  1.3 1.3 %collective-permute-start.1 = (f32[768,128]{1,0:T(8,128)S(1)}, f32[768,128]{1,0:T(8,128)S(1)}, u32[]{:S(2)}, u32[]{:S(2)}) collective-permute-start(f32[768,128]{1,0:T(8,128)S(1)} %get-tuple-element.22.refs_1_), channel_id=1, source_target_pairs={{0,1},{1,0},{2,3},{3,2},{4,5},{5,4},{6,7},{7,6},{8,9},{9,8},{10,11... | collective-permute-start | bytes 1179656 | tf_op jit(solution)/shard_map/ppermute | solution.py:330
  2.6 1.6 %collective-permute-start = (f32[768,128]{1,0:T(8,128)S(1)}, f32[768,128]{1,0:T(8,128)S(1)}, u32[]{:S(2)}, u32[]{:S(2)}) collective-permute-start(f32[768,128]{1,0:T(8,128)S(1)} %get-tuple-element.25), channel_id=1, source_target_pairs={{0,199},{1,2},{2,1},{3,4},{4,3},{5,6},{6,5},{7,192},{8,207},{9,10}... | collective-permute-start | bytes 1179656 | tf_op jit(solution)/shard_map/ppermute | solution.py:330
  4.2 0.9 %copy-done.5 = f32[2,2,2,128,32]{3,4,2,1,0:T(8,128)S(1)} copy-done((f32[2,2,2,128,32]{3,4,2,1,0:T(8,128)S(1)}, f32[2,2,2,128,32]{3,4,2,1,0:T(8,128)}, u32[]{:S(2)}) %copy-start.5) | copy-done | bytes 131096
  5.1 5.6 %collective-permute-start.2 = (f32[128,128]{1,0:T(8,128)S(1)}, f32[128,128]{1,0:T(8,128)S(1)}, u32[]{:S(2)}, u32[]{:S(2)}) collective-permute-start(f32[128,128]{1,0:T(8,128)S(1)} %own_half.1.refs_2_.refs_0_), channel_id=1, source_target_pairs={{0,4},{1,5},{2,6},{3,7},{4,0},{5,1},{6,2},{7,3},{8,12},{9,13},{10,... | collective-permute-start | bytes 196616 | tf_op jit(solution)/shard_map/ppermute | solution.py:330
  10.7 1.0 %copy-done.3 = f32[64,4,4,128]{3,2,1,0:T(4,128)S(1)} copy-done((f32[64,4,4,128]{3,2,1,0:T(4,128)S(1)}, f32[64,4,4,128]{3,2,1,0:T(4,128)}, u32[]{:S(2)}) %copy-start.3) | copy-done | bytes 524312
  11.7 1.2 %copy-done.6 = f32[3,3,3,64,64]{4,3,2,1,0:T(8,128)S(1)} copy-done((f32[3,3,3,64,64]{4,3,2,1,0:T(8,128)S(1)}, f32[3,3,3,64,64]{4,3,2,1,0:T(8,128)}, u32[]{:S(2)}) %copy-start.6) | copy-done | bytes 442392
  12.9 2.3 %fine_own.1 = (f32[2304,128]{1,0:T(8,128)S(1)}, bf16[384,768]{1,0:T(8,128)(2,1)S(1)}) custom-call(f32[1024,128]{1,0:T(8,128)S(1)} %bitcast.14, f32[1728,64]{1,0:T(8,128)S(1)} %bitcast.17, f32[128,128]{1,0:T(8,128)S(1)} %own_half.1.refs_2_.refs_0_), custom_call_target="tpu_custom_call" | custom-call | flops 1000000000 | bytes 966656 | tf_op jit(solution)/shard_map/fine_own/pallas_call | solution.py:40
  15.1 0.0 collective-permute-done.1.refs_2_
  15.1 0.0 copy-start
  15.2 0.0 copy-start.1
  15.2 1.2 %fine_near.1.refs_2_.refs_3_ = f32[1152,128]{1,0:T(8,128)S(1)} custom-call(f32[2304,128]{1,0:T(8,128)S(1)} %get-tuple-element.23.refs_0_, bf16[384,768]{1,0:T(8,128)(2,1)S(1)} %get-tuple-element.24.refs_1_, f32[768,128]{1,0:T(8,128)S(1)} %collective-permute-done.1.refs_2_), custom_call_target="tpu_custom_call" | custom-call | flops 100000000 | bytes 2162688 | tf_op jit(solution)/shard_map/fine_near/pallas_call | solution.py:40
  16.4 0.0 collective-permute-done.2.refs_1_
  16.5 12.5 %collective-permute-start.7 = (f32[256,128]{1,0:T(8,128)S(1)}, f32[256,128]{1,0:T(8,128)S(1)}, u32[]{:S(2)}, u32[]{:S(2)}) collective-permute-start(f32[256,128]{1,0:T(8,128)S(1)} %joined.4.refs_4_.refs_0_), channel_id=1, source_target_pairs={{0,1},{1,0},{2,3},{3,2},{4,5},{5,4},{6,7},{7,6},{8,9},{9,8},{10,11... | collective-permute-start | bytes 393224 | tf_op jit(solution)/shard_map/ppermute | solution.py:330
  29.0 0.5 filters.1
  29.5 0.0 collective-permute-done.refs_2_
  29.5 0.0 copy-start.4
  29.5 1.3 %fine_far.1 = (f32[2048,128]{1,0:T(8,128)S(1)}, f32[512,128]{1,0:T(8,128)S(1)}, f32[512,128]{1,0:T(8,128)S(1)}) custom-call(f32[2304,128]{1,0:T(8,128)S(1)} %get-tuple-element.23.refs_0_, bf16[384,768]{1,0:T(8,128)(2,1)S(1)} %get-tuple-element.24.refs_1_, f32[768,128]{1,0:T(8,128)S(1)} %collective-permute-done.refs_2_, ...), custom_call_target="tpu_custom_call" | custom-call | flops 100000000 | bytes 2752512 | tf_op jit(solution)/shard_map/fine_far/pallas_call | solution.py:40
  30.8 0.1 collective-permute-start.3
  30.9 8.1 %collective-permute-start.4 = (f32[512,128]{1,0:T(8,128)S(1)}, f32[512,128]{1,0:T(8,128)S(1)}, u32[]{:S(2)}, u32[]{:S(2)}) collective-permute-start(f32[512,128]{1,0:T(8,128)S(1)} %get-tuple-element.29), channel_id=1, source_target_pairs={{0,252},{1,253},{2,254},{3,255},{4,248},{5,249},{6,250},{7,251},{8... | collective-permute-start | bytes 786440 | tf_op jit(solution)/shard_map/ppermute | solution.py:330
  39.0 0.0 collective-permute-done.7.refs_1_
  39.0 0.1 collective-permute-start.8
  39.1 0.0 collective-permute-done.3.refs_1_
  39.1 3.9 %collective-permute-done.4.refs_2_ = f32[512,128]{1,0:T(8,128)S(1)} collective-permute-done((f32[512,128]{1,0:T(8,128)S(1)}, f32[512,128]{1,0:T(8,128)S(1)}, u32[]{:S(2)}, u32[]{:S(2)}) %collective-permute-start.4) | collective-permute-done | bytes 262176 | tf_op jit(solution)/shard_map/ppermute | solution.py:330
  43.1 0.7 first_down.1.refs_0_.refs_2_
  43.8 1.7 %collective-permute-done.8.refs_1_ = f32[512,128]{1,0:T(8,128)S(1)} collective-permute-done((f32[512,128]{1,0:T(8,128)S(1)}, f32[512,128]{1,0:T(8,128)S(1)}, u32[]{:S(2)}, u32[]{:S(2)}) %collective-permute-start.8) | collective-permute-done | bytes 262176 | tf_op jit(solution)/shard_map/ppermute | solution.py:330
  45.5 0.3 collective-permute-start.9
  45.8 1.2 %middle.1 = (f32[256,128]{1,0:T(8,128)S(1)}, f32[128,128]{1,0:T(8,128)S(1)}, f32[128,128]{1,0:T(8,128)S(1)}) custom-call(f32[512,128]{1,0:T(8,128)S(1)} %first_down.1.refs_0_.refs_2_, bf16[2304,384]{1,0:T(8,128)(2,1)S(1)} %get-tuple-element.26.refs_5_.refs_1_), custom_call_target="tpu_custom_call" | custom-call | flops 100000000 | bytes 2031616 | tf_op jit(solution)/shard_map/middle/pallas_call | solution.py:40
  47.1 0.6 collective-permute-start.5
  47.6 3.4 %collective-permute-start.6 = (f32[128,128]{1,0:T(8,128)S(1)}, f32[128,128]{1,0:T(8,128)S(1)}, u32[]{:S(2)}, u32[]{:S(2)}) collective-permute-start(f32[128,128]{1,0:T(8,128)S(1)} %get-tuple-element.32), channel_id=1, source_target_pairs={{0,252},{1,253},{2,254},{3,255},{4,248},{5,249},{6,250},{7,251},{8... | collective-permute-start | bytes 196616 | tf_op jit(solution)/shard_map/ppermute | solution.py:330
  51.0 0.0 collective-permute-done.9.refs_1_
  51.0 0.2 gathered_filters.1
  51.2 3.4 %collective-permute-done.6.refs_2_ = f32[128,128]{1,0:T(8,128)S(1)} collective-permute-done((f32[128,128]{1,0:T(8,128)S(1)}, f32[128,128]{1,0:T(8,128)S(1)}, u32[]{:S(2)}, u32[]{:S(2)}) %collective-permute-start.6) | collective-permute-done | bytes 65568 | tf_op jit(solution)/shard_map/ppermute | solution.py:330
  54.7 0.4 second_down.1.refs_0_.refs_2_
  55.1 2.1 %collective-permute-start.10 = (f32[32,256]{1,0:T(8,128)S(1)}, f32[32,256]{1,0:T(8,128)S(1)}, u32[]{:S(2)}, u32[]{:S(2)}) collective-permute-start(f32[32,256]{1,0:T(8,128)S(1)} %second_down.1.refs_0_.refs_2_), channel_id=1, source_target_pairs={{0,4},{1,5},{2,6},{3,7},{4,0},{5,1},{6,2},{7,3},{8,12},{9,13},{10,... | collective-permute-start | bytes 98312 | tf_op jit(solution)/shard_map/ppermute | solution.py:330
  57.1 5.8 %collective-permute-done.10.refs_1_ = f32[32,256]{1,0:T(8,128)S(1)} collective-permute-done((f32[32,256]{1,0:T(8,128)S(1)}, f32[32,256]{1,0:T(8,128)S(1)}, u32[]{:S(2)}, u32[]{:S(2)}) %collective-permute-start.10) | collective-permute-done | bytes 32800 | tf_op jit(solution)/shard_map/ppermute | solution.py:330
  62.9 1.2 %collective-permute-start.11 = (f32[64,256]{1,0:T(8,128)S(1)}, f32[64,256]{1,0:T(8,128)S(1)}, u32[]{:S(2)}, u32[]{:S(2)}) collective-permute-start(f32[64,256]{1,0:T(8,128)S(1)} %joined.7.refs_0_), channel_id=1, source_target_pairs={{0,1},{1,0},{2,3},{3,2},{4,5},{5,4},{6,7},{7,6},{8,9},{9,8},{10,11... | collective-permute-start | bytes 196616 | tf_op jit(solution)/shard_map/ppermute | solution.py:330
  64.2 0.2 collective-permute-start.12
  64.4 2.0 %collective-permute-start.13 = (f32[64,256]{1,0:T(8,128)S(1)}, f32[64,256]{1,0:T(8,128)S(1)}, u32[]{:S(2)}, u32[]{:S(2)}) collective-permute-start(f32[64,256]{1,0:T(8,128)S(1)} %joined.7.refs_0_), channel_id=1, source_target_pairs={{0,3},{1,2},{2,1},{3,0},{4,7},{5,6},{6,5},{7,4},{8,11},{9,10},{10,... | collective-permute-start | bytes 196616 | tf_op jit(solution)/shard_map/ppermute | solution.py:330
  66.4 0.8 collective-permute-done.11.refs_1_
  67.2 2.7 %collective-permute-done.12.refs_2_ = f32[64,256]{1,0:T(8,128)S(1)} collective-permute-done((f32[64,256]{1,0:T(8,128)S(1)}, f32[64,256]{1,0:T(8,128)S(1)}, u32[]{:S(2)}, u32[]{:S(2)}) %collective-permute-start.12) | collective-permute-done | bytes 65568 | tf_op jit(solution)/shard_map/ppermute | solution.py:330
  69.9 0.0 collective-permute-done.13.refs_3_
  69.9 1.0 %coarse_conv.1 = (f32[64,256]{1,0:T(8,128)S(1)}, f32[64,256]{1,0:T(8,128)S(1)}, f32[64,256]{1,0:T(8,128)S(1)}) custom-call(f32[64,256]{1,0:T(8,128)S(1)} %joined.7.refs_0_, f32[64,256]{1,0:T(8,128)S(1)} %collective-permute-done.11.refs_1_, f32[64,256]{1,0:T(8,128)S(1)} %collective-permute-done.12.refs_2_, f32[64,256]{1,0:T(8,128)S(1)} %collective-permute-done.13.refs_3_, ...), custom_call_target="tpu_custom_call" | custom-call | flops 100000000 | bytes 2031616 | tf_op jit(solution)/shard_map/coarse_conv/pallas_call | solution.py:40
  71.0 0.1 collective-permute-start.14
  71.1 1.5 %collective-permute-start.15 = (f32[64,256]{1,0:T(8,128)S(1)}, f32[64,256]{1,0:T(8,128)S(1)}, u32[]{:S(2)}, u32[]{:S(2)}) collective-permute-start(f32[64,256]{1,0:T(8,128)S(1)} %get-tuple-element.38), channel_id=1, source_target_pairs={{0,252},{1,253},{2,254},{3,255},{4,248},{5,249},{6,250},{7,251},{8... | collective-permute-start | bytes 196616 | tf_op jit(solution)/shard_map/ppermute | solution.py:330
  72.5 5.6 %collective-permute-done.15.refs_2_ = f32[64,256]{1,0:T(8,128)S(1)} collective-permute-done((f32[64,256]{1,0:T(8,128)S(1)}, f32[64,256]{1,0:T(8,128)S(1)}, u32[]{:S(2)}, u32[]{:S(2)}) %collective-permute-start.15) | collective-permute-done | bytes 65568 | tf_op jit(solution)/shard_map/ppermute | solution.py:330
  78.2 0.7 finish.1
  (14 shorter events, 0.1 us)
Async XLA Ops:
  0.0 1.0 %copy-start.2 = (f32[64,4,4,128]{3,2,1,0:T(4,128)S(1)}, f32[64,4,4,128]{3,2,1,0:T(4,128)}, u32[]{:S(2)}) copy-start(f32[64,4,4,128]{3,2,1,0:T(4,128)} %param.6) | copy-start | bytes 1572868
  1.3 13.9 %collective-permute-start.1 = (f32[768,128]{1,0:T(8,128)S(1)}, f32[768,128]{1,0:T(8,128)S(1)}, u32[]{:S(2)}, u32[]{:S(2)}) collective-permute-start(f32[768,128]{1,0:T(8,128)S(1)} %get-tuple-element.22.refs_1_), channel_id=1, source_target_pairs={{0,1},{1,0},{2,3},{3,2},{4,5},{5,4},{6,7},{7,6},{8,9},{9,8},{10,11... | collective-permute-start | bytes 1179656 | tf_op jit(solution)/shard_map/ppermute | solution.py:330
  2.6 26.9 %collective-permute-start = (f32[768,128]{1,0:T(8,128)S(1)}, f32[768,128]{1,0:T(8,128)S(1)}, u32[]{:S(2)}, u32[]{:S(2)}) collective-permute-start(f32[768,128]{1,0:T(8,128)S(1)} %get-tuple-element.25), channel_id=1, source_target_pairs={{0,199},{1,2},{2,1},{3,4},{4,3},{5,6},{6,5},{7,192},{8,207},{9,10}... | collective-permute-start | bytes 1179656 | tf_op jit(solution)/shard_map/ppermute | solution.py:330
  4.2 0.9 %copy-start.5 = (f32[2,2,2,128,32]{3,4,2,1,0:T(8,128)S(1)}, f32[2,2,2,128,32]{3,4,2,1,0:T(8,128)}, u32[]{:S(2)}) copy-start(f32[2,2,2,128,32]{3,4,2,1,0:T(8,128)} %param.10) | copy-start | bytes 393220
  5.1 11.3 %collective-permute-start.2 = (f32[128,128]{1,0:T(8,128)S(1)}, f32[128,128]{1,0:T(8,128)S(1)}, u32[]{:S(2)}, u32[]{:S(2)}) collective-permute-start(f32[128,128]{1,0:T(8,128)S(1)} %own_half.1.refs_2_.refs_0_), channel_id=1, source_target_pairs={{0,4},{1,5},{2,6},{3,7},{4,0},{5,1},{6,2},{7,3},{8,12},{9,13},{10,... | collective-permute-start | bytes 196616 | tf_op jit(solution)/shard_map/ppermute | solution.py:330
  10.7 1.0 %copy-start.3 = (f32[64,4,4,128]{3,2,1,0:T(4,128)S(1)}, f32[64,4,4,128]{3,2,1,0:T(4,128)}, u32[]{:S(2)}) copy-start(f32[64,4,4,128]{3,2,1,0:T(4,128)} %param.6) | copy-start | bytes 1572868
  11.7 1.2 %copy-start.6 = (f32[3,3,3,64,64]{4,3,2,1,0:T(8,128)S(1)}, f32[3,3,3,64,64]{4,3,2,1,0:T(8,128)}, u32[]{:S(2)}) copy-start(f32[3,3,3,64,64]{4,3,2,1,0:T(8,128)} %param.7) | copy-start | bytes 1327108
  15.1 13.8 %copy-start = (f32[3,3,3,128,128]{4,3,2,1,0:T(8,128)S(1)}, f32[3,3,3,128,128]{4,3,2,1,0:T(8,128)}, u32[]{:S(2)}) copy-start(f32[3,3,3,128,128]{4,3,2,1,0:T(8,128)} %param.9) | copy-start | bytes 5308420
  15.2 13.8 %copy-start.1 = (f32[3,3,3,256,64]{3,4,2,1,0:T(8,128)S(1)}, f32[3,3,3,256,64]{3,4,2,1,0:T(8,128)}, u32[]{:S(2)}) copy-start(f32[3,3,3,256,64]{3,4,2,1,0:T(8,128)} %param.11) | copy-start | bytes 5308420
  16.5 22.6 %collective-permute-start.7 = (f32[256,128]{1,0:T(8,128)S(1)}, f32[256,128]{1,0:T(8,128)S(1)}, u32[]{:S(2)}, u32[]{:S(2)}) collective-permute-start(f32[256,128]{1,0:T(8,128)S(1)} %joined.4.refs_4_.refs_0_), channel_id=1, source_target_pairs={{0,1},{1,0},{2,3},{3,2},{4,5},{5,4},{6,7},{7,6},{8,9},{9,8},{10,11... | collective-permute-start | bytes 393224 | tf_op jit(solution)/shard_map/ppermute | solution.py:330
  29.5 13.6 %copy-start.4 = (f32[2,2,2,64,128]{4,3,2,1,0:T(8,128)S(1)}, f32[2,2,2,64,128]{4,3,2,1,0:T(8,128)}, u32[]{:S(2)}) copy-start(f32[2,2,2,64,128]{4,3,2,1,0:T(8,128)} %param.8) | copy-start | bytes 786436
  30.8 8.4 %collective-permute-start.3 = (f32[512,128]{1,0:T(8,128)S(1)}, f32[512,128]{1,0:T(8,128)S(1)}, u32[]{:S(2)}, u32[]{:S(2)}) collective-permute-start(f32[512,128]{1,0:T(8,128)S(1)} %get-tuple-element.28), channel_id=1, source_target_pairs={{0,8},{1,9},{2,10},{3,11},{4,12},{5,13},{6,14},{7,15},{8,0},{9,1},... | collective-permute-start | bytes 786440 | tf_op jit(solution)/shard_map/ppermute | solution.py:330
  30.9 12.2 %collective-permute-start.4 = (f32[512,128]{1,0:T(8,128)S(1)}, f32[512,128]{1,0:T(8,128)S(1)}, u32[]{:S(2)}, u32[]{:S(2)}) collective-permute-start(f32[512,128]{1,0:T(8,128)S(1)} %get-tuple-element.29), channel_id=1, source_target_pairs={{0,252},{1,253},{2,254},{3,255},{4,248},{5,249},{6,250},{7,251},{8... | collective-permute-start | bytes 786440 | tf_op jit(solution)/shard_map/ppermute | solution.py:330
  39.0 6.5 %collective-permute-start.8 = (f32[512,128]{1,0:T(8,128)S(1)}, f32[512,128]{1,0:T(8,128)S(1)}, u32[]{:S(2)}, u32[]{:S(2)}) collective-permute-start(f32[512,128]{1,0:T(8,128)S(1)} %joined.5.refs_0_), channel_id=1, source_target_pairs={{0,3},{1,2},{2,1},{3,0},{4,7},{5,6},{6,5},{7,4},{8,11},{9,10},{10,... | collective-permute-start | bytes 786440 | tf_op jit(solution)/shard_map/ppermute | solution.py:330
  45.5 5.5 %collective-permute-start.9 = (f32[1024,128]{1,0:T(8,128)S(1)}, f32[1024,128]{1,0:T(8,128)S(1)}, u32[]{:S(2)}, u32[]{:S(2)}) collective-permute-start(f32[1024,128]{1,0:T(8,128)S(1)} %joined.6.refs_0_), channel_id=1, source_target_pairs={{0,8},{1,9},{2,10},{3,11},{4,12},{5,13},{6,14},{7,15},{8,0},{9,1},... | collective-permute-start | bytes 1572872 | tf_op jit(solution)/shard_map/ppermute | solution.py:330
  47.1 4.2 %collective-permute-start.5 = (f32[128,128]{1,0:T(8,128)S(1)}, f32[128,128]{1,0:T(8,128)S(1)}, u32[]{:S(2)}, u32[]{:S(2)}) collective-permute-start(f32[128,128]{1,0:T(8,128)S(1)} %get-tuple-element.31), channel_id=1, source_target_pairs={{0,8},{1,9},{2,10},{3,11},{4,12},{5,13},{6,14},{7,15},{8,0},{9,1},... | collective-permute-start | bytes 196616 | tf_op jit(solution)/shard_map/ppermute | solution.py:330
  47.6 7.0 %collective-permute-start.6 = (f32[128,128]{1,0:T(8,128)S(1)}, f32[128,128]{1,0:T(8,128)S(1)}, u32[]{:S(2)}, u32[]{:S(2)}) collective-permute-start(f32[128,128]{1,0:T(8,128)S(1)} %get-tuple-element.32), channel_id=1, source_target_pairs={{0,252},{1,253},{2,254},{3,255},{4,248},{5,249},{6,250},{7,251},{8... | collective-permute-start | bytes 196616 | tf_op jit(solution)/shard_map/ppermute | solution.py:330
  55.1 7.9 %collective-permute-start.10 = (f32[32,256]{1,0:T(8,128)S(1)}, f32[32,256]{1,0:T(8,128)S(1)}, u32[]{:S(2)}, u32[]{:S(2)}) collective-permute-start(f32[32,256]{1,0:T(8,128)S(1)} %second_down.1.refs_0_.refs_2_), channel_id=1, source_target_pairs={{0,4},{1,5},{2,6},{3,7},{4,0},{5,1},{6,2},{7,3},{8,12},{9,13},{10,... | collective-permute-start | bytes 98312 | tf_op jit(solution)/shard_map/ppermute | solution.py:330
  62.9 4.3 %collective-permute-start.11 = (f32[64,256]{1,0:T(8,128)S(1)}, f32[64,256]{1,0:T(8,128)S(1)}, u32[]{:S(2)}, u32[]{:S(2)}) collective-permute-start(f32[64,256]{1,0:T(8,128)S(1)} %joined.7.refs_0_), channel_id=1, source_target_pairs={{0,1},{1,0},{2,3},{3,2},{4,5},{5,4},{6,7},{7,6},{8,9},{9,8},{10,11... | collective-permute-start | bytes 196616 | tf_op jit(solution)/shard_map/ppermute | solution.py:330
  64.2 5.8 %collective-permute-start.12 = (f32[64,256]{1,0:T(8,128)S(1)}, f32[64,256]{1,0:T(8,128)S(1)}, u32[]{:S(2)}, u32[]{:S(2)}) collective-permute-start(f32[64,256]{1,0:T(8,128)S(1)} %joined.7.refs_0_), channel_id=1, source_target_pairs={{0,2},{1,3},{2,0},{3,1},{4,6},{5,7},{6,4},{7,5},{8,10},{9,11},{10,... | collective-permute-start | bytes 196616 | tf_op jit(solution)/shard_map/ppermute | solution.py:330
  64.4 5.5 %collective-permute-start.13 = (f32[64,256]{1,0:T(8,128)S(1)}, f32[64,256]{1,0:T(8,128)S(1)}, u32[]{:S(2)}, u32[]{:S(2)}) collective-permute-start(f32[64,256]{1,0:T(8,128)S(1)} %joined.7.refs_0_), channel_id=1, source_target_pairs={{0,3},{1,2},{2,1},{3,0},{4,7},{5,6},{6,5},{7,4},{8,11},{9,10},{10,... | collective-permute-start | bytes 196616 | tf_op jit(solution)/shard_map/ppermute | solution.py:330
  71.0 1.6 %collective-permute-start.14 = (f32[64,256]{1,0:T(8,128)S(1)}, f32[64,256]{1,0:T(8,128)S(1)}, u32[]{:S(2)}, u32[]{:S(2)}) collective-permute-start(f32[64,256]{1,0:T(8,128)S(1)} %get-tuple-element.37), channel_id=1, source_target_pairs={{0,8},{1,9},{2,10},{3,11},{4,12},{5,13},{6,14},{7,15},{8,0},{9,1},... | collective-permute-start | bytes 196616 | tf_op jit(solution)/shard_map/ppermute | solution.py:330
  71.1 7.1 %collective-permute-start.15 = (f32[64,256]{1,0:T(8,128)S(1)}, f32[64,256]{1,0:T(8,128)S(1)}, u32[]{:S(2)}, u32[]{:S(2)}) collective-permute-start(f32[64,256]{1,0:T(8,128)S(1)} %get-tuple-element.38), channel_id=1, source_target_pairs={{0,252},{1,253},{2,254},{3,255},{4,248},{5,249},{6,250},{7,251},{8... | collective-permute-start | bytes 196616 | tf_op jit(solution)/shard_map/ppermute | solution.py:330

commit v3 on v1

--- a/solution.py
+++ b/solution.py
@@ -29,13 +29,18 @@
     return v * (1.0 + lax.erf(v * 0.7071067811865476)) * 0.5
 
 
-def call(kernel, outs, args, scratch=(), flops=0, after=()):
+def call(kernel, outs, args, scratch=(), flops=0, after=(), spaces=None):
     vmem = pl.BlockSpec(memory_space=pltpu.VMEM)
     size = sum(a.size * a.dtype.itemsize for a in args)
+    n = len(args)
+
+    def body(*refs):
+        kernel(*refs[:n], *refs[n + len(after) :])
+
     return pl.pallas_call(
-        kernel,
+        body,
         out_shape=[jax.ShapeDtypeStruct(s, t) for s, t in outs],
-        in_specs=[vmem] * len(args) + [pl.BlockSpec(memory_space=pl.ANY)] * len(after),
+        in_specs=[pl.BlockSpec(memory_space=space) for space in spaces or (pltpu.VMEM,) * n] + [pl.BlockSpec(memory_space=pl.ANY)] * len(after),
         out_specs=[vmem] * len(outs),
         scratch_shapes=list(scratch),
         compiler_params=pltpu.CompilerParams(vmem_limit_bytes=16 * 2**20),
@@ -70,11 +75,11 @@
         send(near, far, pl.ds(d * 64, 64), last, first, "grp")
 
 
-def own_half(w2, after, half):
-    half[...] = w2[pl.ds(pl.multiple_of(parity("slab") * 128, 128), 128), :]
-
-
-def joined(first, second, after, out):
+def own_half(w2, half):
+    pltpu.sync_copy(w2.at[pl.ds(pl.multiple_of(parity("slab") * 128, 128), 128), :], half)
+
+
+def joined(first, second, out):
     n = first.shape[0]
     out[:n, :] = first[...]
     out[n:, :] = second[...]
@@ -307,7 +312,9 @@
 
 def finish(mid, near, far, out):
     before, after = received(near, far, slice(None), "slab")
-    out[:, 0, :] = gelu(mid[...] + before + after)
+    v = gelu(mid[...] + before + after)
+    for j in range(2):
+        out[pl.ds(j, 64, stride=2), :] = v[:, j * 128 : j * 128 + 128]
 
 
 def per_device(volume, conv_fine, down_first, conv_middle, down_second, conv_coarse):
@@ -323,29 +330,30 @@
 
     def far_slab(s, g):
         if s in (0, slabs - 1):
-            return slabs - 1 - s, g ^ 4
+            return s, g ^ 1
         return (s + 1 if s % 2 else s - 1), g
 
     def far_grp(s, g):
         if g in (0, grps - 1):
-            z, rest = divmod(s, slabs // 4)
-            return (3 - z) * (slabs // 4) + rest, grps - 1 - g
+            return s ^ 1, g
         return s, (g + 1 if g % 2 else g - 1)
 
     def over_grp(near, far):
-        return swap(near, "grp", 1), permute(far, far_grp)
+        far = permute(far, far_grp)
+        return swap(near, "grp", 1), far
 
     def over_slab(near, far):
-        return swap(near, "slab", 1), permute(far, far_slab)
+        far = permute(far, far_slab)
+        return swap(near, "slab", 1), far
 
     def swap(x, axis, mask):
         if axis == "slab":
             return permute(x, lambda s, g: (s ^ mask, g))
         return permute(x, lambda s, g: (s, g ^ mask))
 
-    def join(first, second, after):
+    def join(first, second, *after):
         rows, lanes = first.shape
-        return call(joined, [((2 * rows, lanes), F32)], (first, second), after=(after,))[0]
+        return call(joined, [((2 * rows, lanes), F32)], (first, second), after=after)[0]
 
     vol = volume.reshape(1024, 128)
     w1 = conv_fine.reshape(1728, 64)
@@ -354,24 +362,25 @@
     w2 = jnp.swapaxes(down_second, 3, 4).reshape(256, 128)
     wc = jnp.swapaxes(conv_coarse, 3, 4).reshape(1728, 256)
 
-    rim = over_grp(*call(edges, [((256, 128), F32)] * 2, (vol,)))
+    (half,) = call(own_half, [((128, 128), F32)], (w2,), spaces=(pl.ANY,))
+    second = swap(half, "grp", 4)
+    rim = over_grp(*call(edges, [((256, 128), F32)] * 2, (vol,), after=(half,)))
     taken = [pltpu.VMEM((2, 1024, 256), BF16)] * 2
     acc, wt = call(fine_own, [((1536, 128), F32), ((384, 768), BF16)], (vol, w1), taken, flops=10**9)
-    (half,) = call(own_half, [((128, 128), F32)], (w2,), after=(acc,))
-    second = swap(half, "grp", 4)
-
+    two = join(half, second, acc)
+    second = swap(two, "grp", 1)
     taken = [pltpu.VMEM((4, 256, 256), BF16)] * 2
-    inner, *out = call(fine_rim, [((512, 128), F32)] + [((256, 128), F32)] * 2, (acc, wt, *rim), taken, flops=10**8)
+    inner, *out = call(
+        fine_rim, [((512, 128), F32)] + [((256, 128), F32)] * 2, (acc, wt, *rim), taken, flops=10**8,
+        after=(two,))
     rim = over_slab(*out)
-    two = join(half, second, inner)
-    second = swap(two, "grp", 1)
+    four = join(two, second, *rim)
+    second = swap(four, "grp", 3)
     mid_w, coarse_w = call(filters, [((2304, 384), BF16), ((384, 2304), BF16)], (wm, wc), flops=10**8)
 
     taken = [pltpu.VMEM((8, 128, 128), F32), pltpu.VMEM((512, 128), BF16), pltpu.VMEM((512, 128), BF16)]
     d_low, d_high, *out = call(first_down, [((128, 128), F32)] * 4, (acc, inner, *rim, wd1), taken, flops=10**8)
     rim = over_grp(*out)
-    four = join(two, second, d_low)
-    second = swap(four, "grp", 3)
     taken = [pltpu.VMEM((2, 128, 384), BF16)] * 2
     (own,) = call(middle_own, [((256, 384), F32)], (d_low, d_high, mid_w), taken, flops=10**8)
     inner, *out = call(
@@ -383,12 +392,12 @@
     (row,) = call(
         second_down, [((32, 256), F32)], (inner, *rim, whi, wlo), [pltpu.VMEM((256, 128), F32)], flops=10**8)
 
-    pair = join(row, swap(row, "grp", 4), row)
+    pair = join(row, swap(row, "grp", 4))
     others = [swap(pair, "grp", mask) for mask in (1, 2, 3)]
     taken = [pltpu.VMEM((256, 256), F32), pltpu.VMEM((320, 768), BF16), pltpu.VMEM((320, 768), BF16)]
     mid, *out = call(coarse_conv, [((64, 256), F32)] * 3, (pair, *others, coarse_w), taken, flops=10**8)
     rim = over_slab(*out)
-    return call(finish, [((64, 1, 256), F32)], (mid, *rim))[0]
+    return call(finish, [((128, 128), F32)], (mid, *rim))[0].reshape(64, 1, 256)
 
 
 def solution(mesh):

time: 74.5 us -> 72.3 us (0.970)
  the two profiles are of different devices: /device:TPU:4 before, /device:TPU:38 now
where the time goes in v3:
time: 72.3 us; the launch traced here: 72.2 us
  waiting for transfers between devices  32.2 us (45%)
  starting transfers between devices  29.1 us (40%)
  Pallas kernels  7.52 us (10%)
  local copies, waits for them, and re-layouts  3.12 us (4%)
    ppermute x18, waiting for transfers between devices, permute(): return lax.ppermute(x, ('slab', 'grp'), pairs)  32.2 us
    ppermute x18, starting transfers between devices, permute(): return lax.ppermute(x, ('slab', 'grp'), pairs)  29.1 us
    pallas_call x16, Pallas kernels, call(): pl.pallas_call(body, out_shape=[jax.ShapeDtypeStruct(s, t) for s, t in ou...  7.52 us
    unnamed x12, local copies, waits for them, and re-layouts  3.12 us
  transfers between devices with their start and end apart: 18, of which 10 were waited for; matrix products, arithmetic and copies ran while one was open for 0% of the time, Pallas kernels for 7%

profile of v3, /device:TPU:38, one launch (start us, length us, event | category | flops | bytes accessed | tf_op | source)
XLA Modules:
  0.0 72.2 jit_solution(11564701187789436959)
XLA Ops:
  0.0 0.9 %copy-done.4 = f32[2,2,2,128,32]{3,4,2,1,0:T(8,128)S(1)} copy-done((f32[2,2,2,128,32]{3,4,2,1,0:T(8,128)S(1)}, f32[2,2,2,128,32]{3,4,2,1,0:T(8,128)}, u32[]{:S(2)}) %copy-start.4) | copy-done | bytes 131096
  0.9 0.1 own_half.1.refs_1_.refs_0_
  1.0 0.0 copy-start.2
  1.0 1.0 %copy-done.2 = f32[64,4,4,128]{3,2,1,0:T(4,128)S(1)} copy-done((f32[64,4,4,128]{3,2,1,0:T(4,128)S(1)}, f32[64,4,4,128]{3,2,1,0:T(4,128)}, u32[]{:S(2)}) %copy-start.2) | copy-done | bytes 524312
  2.0 0.1 edges.1
  2.1 0.9 %collective-permute-start = (f32[256,128]{1,0:T(8,128)S(1)}, f32[256,128]{1,0:T(8,128)S(1)}, u32[]{:S(2)}, u32[]{:S(2)}) collective-permute-start(f32[256,128]{1,0:T(8,128)S(1)} %get-tuple-element.28), channel_id=1, source_target_pairs={{0,1},{1,0},{2,3},{3,2},{4,5},{5,4},{6,7},{7,6},{8,9},{9,8},{10,11... | collective-permute-start | bytes 393224 | tf_op jit(solution)/shard_map/ppermute | solution.py:329
  3.0 6.9 %collective-permute-start.1 = (f32[256,128]{1,0:T(8,128)S(1)}, f32[256,128]{1,0:T(8,128)S(1)}, u32[]{:S(2)}, u32[]{:S(2)}) collective-permute-start(f32[256,128]{1,0:T(8,128)S(1)} %get-tuple-element.29), channel_id=1, source_target_pairs={{0,8},{1,2},{2,1},{3,4},{4,3},{5,6},{6,5},{7,15},{8,0},{9,10},{10,... | collective-permute-start | bytes 393224 | tf_op jit(solution)/shard_map/ppermute | solution.py:329
  9.9 0.0 collective-permute-start.2
  9.9 1.2 %copy-done.5 = f32[3,3,3,64,64]{4,3,2,1,0:T(8,128)S(1)} copy-done((f32[3,3,3,64,64]{4,3,2,1,0:T(8,128)S(1)}, f32[3,3,3,64,64]{4,3,2,1,0:T(8,128)}, u32[]{:S(2)}) %copy-start.5) | copy-done | bytes 442392
  11.1 2.0 %fine_own.1 = (f32[1536,128]{1,0:T(8,128)S(1)}, bf16[384,768]{1,0:T(8,128)(2,1)S(1)}) custom-call(f32[1024,128]{1,0:T(8,128)S(1)} %bitcast.14, f32[1728,64]{1,0:T(8,128)S(1)} %bitcast.17), custom_call_target="tpu_custom_call" | custom-call | flops 1000000000 | bytes 966656 | tf_op jit(solution)/shard_map/fine_own/pallas_call | solution.py:40
  13.0 5.0 %collective-permute-done.2.refs_1_ = f32[128,128]{1,0:T(8,128)S(1)} collective-permute-done((f32[128,128]{1,0:T(8,128)S(1)}, f32[128,128]{1,0:T(8,128)S(1)}, u32[]{:S(2)}, u32[]{:S(2)}) %collective-permute-start.2) | collective-permute-done | bytes 65568 | tf_op jit(solution)/shard_map/ppermute | solution.py:329
  18.1 0.1 collective-permute-start.9
  18.2 0.0 collective-permute-done.refs_2_
  18.2 0.0 copy-start
  18.2 0.0 copy-start.1
  18.2 0.6 fine_rim.1
  18.9 0.1 collective-permute-start.3
  19.0 3.6 %collective-permute-start.4 = (f32[256,128]{1,0:T(8,128)S(1)}, f32[256,128]{1,0:T(8,128)S(1)}, u32[]{:S(2)}, u32[]{:S(2)}) collective-permute-start(f32[256,128]{1,0:T(8,128)S(1)} %get-tuple-element.32), channel_id=1, source_target_pairs={{0,1},{1,0},{2,3},{3,2},{4,5},{5,4},{6,7},{7,6},{8,16},{9,17},{10,... | collective-permute-start | bytes 393224 | tf_op jit(solution)/shard_map/ppermute | solution.py:329
  22.5 0.6 collective-permute-done.9.refs_1_
  23.1 2.4 %collective-permute-done.4.refs_3_ = f32[256,128]{1,0:T(8,128)S(1)} collective-permute-done((f32[256,128]{1,0:T(8,128)S(1)}, f32[256,128]{1,0:T(8,128)S(1)}, u32[]{:S(2)}, u32[]{:S(2)}) %collective-permute-start.4) | collective-permute-done | bytes 131104 | tf_op jit(solution)/shard_map/ppermute | solution.py:329
  25.6 1.5 %collective-permute-start.10 = (f32[512,128]{1,0:T(8,128)S(1)}, f32[512,128]{1,0:T(8,128)S(1)}, u32[]{:S(2)}, u32[]{:S(2)}) collective-permute-start(f32[512,128]{1,0:T(8,128)S(1)} %joined.5.refs_0_), channel_id=1, source_target_pairs={{0,3},{1,2},{2,1},{3,0},{4,7},{5,6},{6,5},{7,4},{8,11},{9,10},{10,... | collective-permute-start | bytes 786440 | tf_op jit(solution)/shard_map/ppermute | solution.py:329
  27.1 0.5 first_down.1
  27.6 1.5 %collective-permute-start.5 = (f32[128,128]{1,0:T(8,128)S(1)}, f32[128,128]{1,0:T(8,128)S(1)}, u32[]{:S(2)}, u32[]{:S(2)}) collective-permute-start(f32[128,128]{1,0:T(8,128)S(1)} %get-tuple-element.36), channel_id=1, source_target_pairs={{0,1},{1,0},{2,3},{3,2},{4,5},{5,4},{6,7},{7,6},{8,9},{9,8},{10,11... | collective-permute-start | bytes 196616 | tf_op jit(solution)/shard_map/ppermute | solution.py:329
  29.0 7.6 %collective-permute-start.6 = (f32[128,128]{1,0:T(8,128)S(1)}, f32[128,128]{1,0:T(8,128)S(1)}, u32[]{:S(2)}, u32[]{:S(2)}) collective-permute-start(f32[128,128]{1,0:T(8,128)S(1)} %get-tuple-element.37), channel_id=1, source_target_pairs={{0,8},{1,2},{2,1},{3,4},{4,3},{5,6},{6,5},{7,15},{8,0},{9,10},{10,... | collective-permute-start | bytes 196616 | tf_op jit(solution)/shard_map/ppermute | solution.py:329
  36.6 0.5 filters.1
  37.2 0.9 %middle_own.1.refs_0_ = f32[256,384]{1,0:T(8,128)S(1)} custom-call(f32[128,128]{1,0:T(8,128)S(1)} %get-tuple-element.33.refs_0_, f32[128,128]{1,0:T(8,128)S(1)} %get-tuple-element.34.refs_1_, bf16[2304,384]{1,0:T(8,128)(2,1)S(1)} %get-tuple-element.35.refs_2_.refs_3_), custom_call_target="tpu_custom_call" | custom-call | flops 100000000 | bytes 1900544 | tf_op jit(solution)/shard_map/middle_own/pallas_call | solution.py:40
  38.1 1.3 %collective-permute-done.6.refs_2_ = f32[128,128]{1,0:T(8,128)S(1)} collective-permute-done((f32[128,128]{1,0:T(8,128)S(1)}, f32[128,128]{1,0:T(8,128)S(1)}, u32[]{:S(2)}, u32[]{:S(2)}) %collective-permute-start.6) | collective-permute-done | bytes 65568 | tf_op jit(solution)/shard_map/ppermute | solution.py:329
  39.3 0.5 middle_rim.1
  39.9 0.1 collective-permute-start.11
  40.0 0.5 collective-permute-start.7
  40.5 1.4 %collective-permute-start.8 = (f32[128,128]{1,0:T(8,128)S(1)}, f32[128,128]{1,0:T(8,128)S(1)}, u32[]{:S(2)}, u32[]{:S(2)}) collective-permute-start(f32[128,128]{1,0:T(8,128)S(1)} %get-tuple-element.40), channel_id=1, source_target_pairs={{0,1},{1,0},{2,3},{3,2},{4,5},{5,4},{6,7},{7,6},{8,16},{9,17},{10,... | collective-permute-start | bytes 196616 | tf_op jit(solution)/shard_map/ppermute | solution.py:329
  41.9 0.0 collective-permute-done.11.refs_1_
  41.9 0.2 gathered_filters.1
  42.1 4.2 %collective-permute-done.8.refs_2_ = f32[128,128]{1,0:T(8,128)S(1)} collective-permute-done((f32[128,128]{1,0:T(8,128)S(1)}, f32[128,128]{1,0:T(8,128)S(1)}, u32[]{:S(2)}, u32[]{:S(2)}) %collective-permute-start.8) | collective-permute-done | bytes 65568 | tf_op jit(solution)/shard_map/ppermute | solution.py:329
  46.3 0.4 second_down.1.refs_0_
  46.7 0.1 collective-permute-start.12
  46.9 7.7 %collective-permute-done.12.refs_1_ = f32[32,256]{1,0:T(8,128)S(1)} collective-permute-done((f32[32,256]{1,0:T(8,128)S(1)}, f32[32,256]{1,0:T(8,128)S(1)}, u32[]{:S(2)}, u32[]{:S(2)}) %collective-permute-start.12) | collective-permute-done | bytes 32800 | tf_op jit(solution)/shard_map/ppermute | solution.py:329
  54.6 0.0 collective-permute-start.13
  54.6 4.4 %collective-permute-start.14 = (f32[64,256]{1,0:T(8,128)S(1)}, f32[64,256]{1,0:T(8,128)S(1)}, u32[]{:S(2)}, u32[]{:S(2)}) collective-permute-start(f32[64,256]{1,0:T(8,128)S(1)} %joined.7.refs_0_), channel_id=1, source_target_pairs={{0,2},{1,3},{2,0},{3,1},{4,6},{5,7},{6,4},{7,5},{8,10},{9,11},{10,... | collective-permute-start | bytes 196616 | tf_op jit(solution)/shard_map/ppermute | solution.py:329
  59.0 0.3 collective-permute-start.15
  59.3 2.6 %collective-permute-done.14.refs_2_ = f32[64,256]{1,0:T(8,128)S(1)} collective-permute-done((f32[64,256]{1,0:T(8,128)S(1)}, f32[64,256]{1,0:T(8,128)S(1)}, u32[]{:S(2)}, u32[]{:S(2)}) %collective-permute-start.14) | collective-permute-done | bytes 65568 | tf_op jit(solution)/shard_map/ppermute | solution.py:329
  62.0 2.5 %collective-permute-done.15.refs_3_ = f32[64,256]{1,0:T(8,128)S(1)} collective-permute-done((f32[64,256]{1,0:T(8,128)S(1)}, f32[64,256]{1,0:T(8,128)S(1)}, u32[]{:S(2)}, u32[]{:S(2)}) %collective-permute-start.15) | collective-permute-done | bytes 65568 | tf_op jit(solution)/shard_map/ppermute | solution.py:329
  64.5 1.0 %coarse_conv.1 = (f32[64,256]{1,0:T(8,128)S(1)}, f32[64,256]{1,0:T(8,128)S(1)}, f32[64,256]{1,0:T(8,128)S(1)}) custom-call(f32[64,256]{1,0:T(8,128)S(1)} %joined.7.refs_0_, f32[64,256]{1,0:T(8,128)S(1)} %collective-permute-done.13.refs_1_, f32[64,256]{1,0:T(8,128)S(1)} %collective-permute-done.14.refs_2_, f32[64,256]{1,0:T(8,128)S(1)} %collective-permute-done.15.refs_3_, ...), custom_call_target="tpu_custom_call" | custom-call | flops 100000000 | bytes 2031616 | tf_op jit(solution)/shard_map/coarse_conv/pallas_call | solution.py:40
  65.5 0.1 collective-permute-start.16
  65.6 0.1 collective-permute-start.17
  65.7 1.1 %collective-permute-done.16.refs_1_ = f32[64,256]{1,0:T(8,128)S(1)} collective-permute-done((f32[64,256]{1,0:T(8,128)S(1)}, f32[64,256]{1,0:T(8,128)S(1)}, u32[]{:S(2)}, u32[]{:S(2)}) %collective-permute-start.16) | collective-permute-done | bytes 65568 | tf_op jit(solution)/shard_map/ppermute | solution.py:329
  66.8 4.6 %collective-permute-done.17.refs_2_ = f32[64,256]{1,0:T(8,128)S(1)} collective-permute-done((f32[64,256]{1,0:T(8,128)S(1)}, f32[64,256]{1,0:T(8,128)S(1)}, u32[]{:S(2)}, u32[]{:S(2)}) %collective-permute-start.17) | collective-permute-done | bytes 65568 | tf_op jit(solution)/shard_map/ppermute | solution.py:329
  71.5 0.7 finish.1
  (16 shorter events, 0.1 us)
Async XLA Ops:
  0.0 0.9 %copy-start.4 = (f32[2,2,2,128,32]{3,4,2,1,0:T(8,128)S(1)}, f32[2,2,2,128,32]{3,4,2,1,0:T(8,128)}, u32[]{:S(2)}) copy-start(f32[2,2,2,128,32]{3,4,2,1,0:T(8,128)} %param.10) | copy-start | bytes 393220
  1.0 1.0 %copy-start.2 = (f32[64,4,4,128]{3,2,1,0:T(4,128)S(1)}, f32[64,4,4,128]{3,2,1,0:T(4,128)}, u32[]{:S(2)}) copy-start(f32[64,4,4,128]{3,2,1,0:T(4,128)} %param.6) | copy-start | bytes 1572868
  2.1 16.1 %collective-permute-start = (f32[256,128]{1,0:T(8,128)S(1)}, f32[256,128]{1,0:T(8,128)S(1)}, u32[]{:S(2)}, u32[]{:S(2)}) collective-permute-start(f32[256,128]{1,0:T(8,128)S(1)} %get-tuple-element.28), channel_id=1, source_target_pairs={{0,1},{1,0},{2,3},{3,2},{4,5},{5,4},{6,7},{7,6},{8,9},{9,8},{10,11... | collective-permute-start | bytes 393224 | tf_op jit(solution)/shard_map/ppermute | solution.py:329
  3.0 15.2 %collective-permute-start.1 = (f32[256,128]{1,0:T(8,128)S(1)}, f32[256,128]{1,0:T(8,128)S(1)}, u32[]{:S(2)}, u32[]{:S(2)}) collective-permute-start(f32[256,128]{1,0:T(8,128)S(1)} %get-tuple-element.29), channel_id=1, source_target_pairs={{0,8},{1,2},{2,1},{3,4},{4,3},{5,6},{6,5},{7,15},{8,0},{9,10},{10,... | collective-permute-start | bytes 393224 | tf_op jit(solution)/shard_map/ppermute | solution.py:329
  9.9 8.2 %collective-permute-start.2 = (f32[128,128]{1,0:T(8,128)S(1)}, f32[128,128]{1,0:T(8,128)S(1)}, u32[]{:S(2)}, u32[]{:S(2)}) collective-permute-start(f32[128,128]{1,0:T(8,128)S(1)} %own_half.1.refs_1_.refs_0_), channel_id=1, source_target_pairs={{0,4},{1,5},{2,6},{3,7},{4,0},{5,1},{6,2},{7,3},{8,12},{9,13},{10,... | collective-permute-start | bytes 196616 | tf_op jit(solution)/shard_map/ppermute | solution.py:329
  9.9 1.2 %copy-start.5 = (f32[3,3,3,64,64]{4,3,2,1,0:T(8,128)S(1)}, f32[3,3,3,64,64]{4,3,2,1,0:T(8,128)}, u32[]{:S(2)}) copy-start(f32[3,3,3,64,64]{4,3,2,1,0:T(8,128)} %param.7) | copy-start | bytes 1327108
  18.1 9.0 %copy-start.3 = (f32[2,2,2,64,128]{4,3,2,1,0:T(8,128)S(1)}, f32[2,2,2,64,128]{4,3,2,1,0:T(8,128)}, u32[]{:S(2)}) copy-start(f32[2,2,2,64,128]{4,3,2,1,0:T(8,128)} %param.8) | copy-start | bytes 786436
  18.1 5.1 %collective-permute-start.9 = (f32[256,128]{1,0:T(8,128)S(1)}, f32[256,128]{1,0:T(8,128)S(1)}, u32[]{:S(2)}, u32[]{:S(2)}) collective-permute-start(f32[256,128]{1,0:T(8,128)S(1)} %joined.4.refs_4_.refs_0_), channel_id=1, source_target_pairs={{0,1},{1,0},{2,3},{3,2},{4,5},{5,4},{6,7},{7,6},{8,9},{9,8},{10,11... | collective-permute-start | bytes 393224 | tf_op jit(solution)/shard_map/ppermute | solution.py:329
  18.2 18.5 %copy-start = (f32[3,3,3,128,128]{4,3,2,1,0:T(8,128)S(1)}, f32[3,3,3,128,128]{4,3,2,1,0:T(8,128)}, u32[]{:S(2)}) copy-start(f32[3,3,3,128,128]{4,3,2,1,0:T(8,128)} %param.9) | copy-start | bytes 5308420
  18.2 18.4 %copy-start.1 = (f32[3,3,3,256,64]{3,4,2,1,0:T(8,128)S(1)}, f32[3,3,3,256,64]{3,4,2,1,0:T(8,128)}, u32[]{:S(2)}) copy-start(f32[3,3,3,256,64]{3,4,2,1,0:T(8,128)} %param.11) | copy-start | bytes 5308420
  18.9 4.3 %collective-permute-start.3 = (f32[256,128]{1,0:T(8,128)S(1)}, f32[256,128]{1,0:T(8,128)S(1)}, u32[]{:S(2)}, u32[]{:S(2)}) collective-permute-start(f32[256,128]{1,0:T(8,128)S(1)} %get-tuple-element.31), channel_id=1, source_target_pairs={{0,8},{1,9},{2,10},{3,11},{4,12},{5,13},{6,14},{7,15},{8,0},{9,1},... | collective-permute-start | bytes 393224 | tf_op jit(solution)/shard_map/ppermute | solution.py:329
  19.0 6.6 %collective-permute-start.4 = (f32[256,128]{1,0:T(8,128)S(1)}, f32[256,128]{1,0:T(8,128)S(1)}, u32[]{:S(2)}, u32[]{:S(2)}) collective-permute-start(f32[256,128]{1,0:T(8,128)S(1)} %get-tuple-element.32), channel_id=1, source_target_pairs={{0,1},{1,0},{2,3},{3,2},{4,5},{5,4},{6,7},{7,6},{8,16},{9,17},{10,... | collective-permute-start | bytes 393224 | tf_op jit(solution)/shard_map/ppermute | solution.py:329
  25.6 14.3 %collective-permute-start.10 = (f32[512,128]{1,0:T(8,128)S(1)}, f32[512,128]{1,0:T(8,128)S(1)}, u32[]{:S(2)}, u32[]{:S(2)}) collective-permute-start(f32[512,128]{1,0:T(8,128)S(1)} %joined.5.refs_0_), channel_id=1, source_target_pairs={{0,3},{1,2},{2,1},{3,0},{4,7},{5,6},{6,5},{7,4},{8,11},{9,10},{10,... | collective-permute-start | bytes 786440 | tf_op jit(solution)/shard_map/ppermute | solution.py:329
  27.6 10.5 %collective-permute-start.5 = (f32[128,128]{1,0:T(8,128)S(1)}, f32[128,128]{1,0:T(8,128)S(1)}, u32[]{:S(2)}, u32[]{:S(2)}) collective-permute-start(f32[128,128]{1,0:T(8,128)S(1)} %get-tuple-element.36), channel_id=1, source_target_pairs={{0,1},{1,0},{2,3},{3,2},{4,5},{5,4},{6,7},{7,6},{8,9},{9,8},{10,11... | collective-permute-start | bytes 196616 | tf_op jit(solution)/shard_map/ppermute | solution.py:329
  29.0 10.3 %collective-permute-start.6 = (f32[128,128]{1,0:T(8,128)S(1)}, f32[128,128]{1,0:T(8,128)S(1)}, u32[]{:S(2)}, u32[]{:S(2)}) collective-permute-start(f32[128,128]{1,0:T(8,128)S(1)} %get-tuple-element.37), channel_id=1, source_target_pairs={{0,8},{1,2},{2,1},{3,4},{4,3},{5,6},{6,5},{7,15},{8,0},{9,10},{10,... | collective-permute-start | bytes 196616 | tf_op jit(solution)/shard_map/ppermute | solution.py:329
  39.9 2.0 %collective-permute-start.11 = (f32[1024,128]{1,0:T(8,128)S(1)}, f32[1024,128]{1,0:T(8,128)S(1)}, u32[]{:S(2)}, u32[]{:S(2)}) collective-permute-start(f32[1024,128]{1,0:T(8,128)S(1)} %joined.6.refs_0_), channel_id=1, source_target_pairs={{0,8},{1,9},{2,10},{3,11},{4,12},{5,13},{6,14},{7,15},{8,0},{9,1},... | collective-permute-start | bytes 1572872 | tf_op jit(solution)/shard_map/ppermute | solution.py:329
  40.0 2.1 %collective-permute-start.7 = (f32[128,128]{1,0:T(8,128)S(1)}, f32[128,128]{1,0:T(8,128)S(1)}, u32[]{:S(2)}, u32[]{:S(2)}) collective-permute-start(f32[128,128]{1,0:T(8,128)S(1)} %get-tuple-element.39), channel_id=1, source_target_pairs={{0,8},{1,9},{2,10},{3,11},{4,12},{5,13},{6,14},{7,15},{8,0},{9,1},... | collective-permute-start | bytes 196616 | tf_op jit(solution)/shard_map/ppermute | solution.py:329
  40.5 5.8 %collective-permute-start.8 = (f32[128,128]{1,0:T(8,128)S(1)}, f32[128,128]{1,0:T(8,128)S(1)}, u32[]{:S(2)}, u32[]{:S(2)}) collective-permute-start(f32[128,128]{1,0:T(8,128)S(1)} %get-tuple-element.40), channel_id=1, source_target_pairs={{0,1},{1,0},{2,3},{3,2},{4,5},{5,4},{6,7},{7,6},{8,16},{9,17},{10,... | collective-permute-start | bytes 196616 | tf_op jit(solution)/shard_map/ppermute | solution.py:329
  46.7 7.9 %collective-permute-start.12 = (f32[32,256]{1,0:T(8,128)S(1)}, f32[32,256]{1,0:T(8,128)S(1)}, u32[]{:S(2)}, u32[]{:S(2)}) collective-permute-start(f32[32,256]{1,0:T(8,128)S(1)} %second_down.1.refs_0_), channel_id=1, source_target_pairs={{0,4},{1,5},{2,6},{3,7},{4,0},{5,1},{6,2},{7,3},{8,12},{9,13},{10,... | collective-permute-start | bytes 98312 | tf_op jit(solution)/shard_map/ppermute | solution.py:329
  54.6 4.7 %collective-permute-start.13 = (f32[64,256]{1,0:T(8,128)S(1)}, f32[64,256]{1,0:T(8,128)S(1)}, u32[]{:S(2)}, u32[]{:S(2)}) collective-permute-start(f32[64,256]{1,0:T(8,128)S(1)} %joined.7.refs_0_), channel_id=1, source_target_pairs={{0,1},{1,0},{2,3},{3,2},{4,5},{5,4},{6,7},{7,6},{8,9},{9,8},{10,11... | collective-permute-start | bytes 196616 | tf_op jit(solution)/shard_map/ppermute | solution.py:329
  54.6 7.3 %collective-permute-start.14 = (f32[64,256]{1,0:T(8,128)S(1)}, f32[64,256]{1,0:T(8,128)S(1)}, u32[]{:S(2)}, u32[]{:S(2)}) collective-permute-start(f32[64,256]{1,0:T(8,128)S(1)} %joined.7.refs_0_), channel_id=1, source_target_pairs={{0,2},{1,3},{2,0},{3,1},{4,6},{5,7},{6,4},{7,5},{8,10},{9,11},{10,... | collective-permute-start | bytes 196616 | tf_op jit(solution)/shard_map/ppermute | solution.py:329
  59.0 5.5 %collective-permute-start.15 = (f32[64,256]{1,0:T(8,128)S(1)}, f32[64,256]{1,0:T(8,128)S(1)}, u32[]{:S(2)}, u32[]{:S(2)}) collective-permute-start(f32[64,256]{1,0:T(8,128)S(1)} %joined.7.refs_0_), channel_id=1, source_target_pairs={{0,3},{1,2},{2,1},{3,0},{4,7},{5,6},{6,5},{7,4},{8,11},{9,10},{10,... | collective-permute-start | bytes 196616 | tf_op jit(solution)/shard_map/ppermute | solution.py:329
  65.5 1.3 %collective-permute-start.16 = (f32[64,256]{1,0:T(8,128)S(1)}, f32[64,256]{1,0:T(8,128)S(1)}, u32[]{:S(2)}, u32[]{:S(2)}) collective-permute-start(f32[64,256]{1,0:T(8,128)S(1)} %get-tuple-element.45), channel_id=1, source_target_pairs={{0,8},{1,9},{2,10},{3,11},{4,12},{5,13},{6,14},{7,15},{8,0},{9,1},... | collective-permute-start | bytes 196616 | tf_op jit(solution)/shard_map/ppermute | solution.py:329
  65.6 5.9 %collective-permute-start.17 = (f32[64,256]{1,0:T(8,128)S(1)}, f32[64,256]{1,0:T(8,128)S(1)}, u32[]{:S(2)}, u32[]{:S(2)}) collective-permute-start(f32[64,256]{1,0:T(8,128)S(1)} %get-tuple-element.46), channel_id=1, source_target_pairs={{0,1},{1,0},{2,3},{3,2},{4,5},{5,4},{6,7},{7,6},{8,16},{9,17},{10,... | collective-permute-start | bytes 196616 | tf_op jit(solution)/shard_map/ppermute | solution.py:329

commit v4 on v3

--- a/solution.py
+++ b/solution.py
@@ -76,7 +76,7 @@
 
 
 def own_half(w2, half):
-    pltpu.sync_copy(w2.at[pl.ds(pl.multiple_of(parity("slab") * 128, 128), 128), :], half)
+    half[...] = w2[pl.ds(pl.multiple_of(parity("slab") * 128, 128), 128), :]
 
 
 def joined(first, second, out):
@@ -362,18 +362,19 @@
     w2 = jnp.swapaxes(down_second, 3, 4).reshape(256, 128)
     wc = jnp.swapaxes(conv_coarse, 3, 4).reshape(1728, 256)
 
-    (half,) = call(own_half, [((128, 128), F32)], (w2,), spaces=(pl.ANY,))
+    out = call(edges, [((256, 128), F32)] * 2, (vol,))
+    (half,) = call(own_half, [((128, 128), F32)], (w2,), after=(out[0],))
+    rim = over_grp(*out)
     second = swap(half, "grp", 4)
-    rim = over_grp(*call(edges, [((256, 128), F32)] * 2, (vol,), after=(half,)))
     taken = [pltpu.VMEM((2, 1024, 256), BF16)] * 2
-    acc, wt = call(fine_own, [((1536, 128), F32), ((384, 768), BF16)], (vol, w1), taken, flops=10**9)
-    two = join(half, second, acc)
-    second = swap(two, "grp", 1)
+    acc, wt = call(
+        fine_own, [((1536, 128), F32), ((384, 768), BF16)], (vol, w1), taken, flops=10**9, after=(half,))
     taken = [pltpu.VMEM((4, 256, 256), BF16)] * 2
     inner, *out = call(
-        fine_rim, [((512, 128), F32)] + [((256, 128), F32)] * 2, (acc, wt, *rim), taken, flops=10**8,
-        after=(two,))
+        fine_rim, [((512, 128), F32)] + [((256, 128), F32)] * 2, (acc, wt, *rim), taken, flops=10**8)
     rim = over_slab(*out)
+    two = join(half, second, inner)
+    second = swap(two, "grp", 1)
     four = join(two, second, *rim)
     second = swap(four, "grp", 3)
     mid_w, coarse_w = call(filters, [((2304, 384), BF16), ((384, 2304), BF16)], (wm, wc), flops=10**8)

time: 72.3 us -> 68.7 us (0.950)
  the two profiles are of different devices: /device:TPU:38 before, /device:TPU:64 now
where the time goes in v4:
time: 68.7 us; the launch traced here: 68.5 us
  starting transfers between devices  35.1 us (51%)
  waiting for transfers between devices  21.5 us (31%)
  Pallas kernels  7.49 us (11%)
  local copies, waits for them, and re-layouts  4.17 us (6%)
    ppermute x18, starting transfers between devices, permute(): return lax.ppermute(x, ('slab', 'grp'), pairs)  35.1 us
    ppermute x18, waiting for transfers between devices, permute(): return lax.ppermute(x, ('slab', 'grp'), pairs)  21.5 us
    pallas_call x16, Pallas kernels, call(): pl.pallas_call(body, out_shape=[jax.ShapeDtypeStruct(s, t) for s, t in ou...  7.49 us
    unnamed x14, local copies, waits for them, and re-layouts  4.17 us
  transfers between devices with their start and end apart: 18, of which 9 were waited for; matrix products, arithmetic and copies ran while one was open for 0% of the time, Pallas kernels for 8%

profile of v4, /device:TPU:64, one launch (start us, length us, event | category | flops | bytes accessed | tf_op | source)
XLA Modules:
  0.0 68.5 jit_solution(13081645169074750758)
XLA Ops:
  0.0 1.0 %copy-done.2 = f32[64,4,4,128]{3,2,1,0:T(4,128)S(1)} copy-done((f32[64,4,4,128]{3,2,1,0:T(4,128)S(1)}, f32[64,4,4,128]{3,2,1,0:T(4,128)}, u32[]{:S(2)}) %copy-start.2) | copy-done | bytes 524312
  1.0 0.1 edges.1
  1.1 0.1 collective-permute-start.1
  1.2 3.0 %collective-permute-start = (f32[256,128]{1,0:T(8,128)S(1)}, f32[256,128]{1,0:T(8,128)S(1)}, u32[]{:S(2)}, u32[]{:S(2)}) collective-permute-start(f32[256,128]{1,0:T(8,128)S(1)} %get-tuple-element.26.refs_1_), channel_id=1, source_target_pairs={{0,1},{1,0},{2,3},{3,2},{4,5},{5,4},{6,7},{7,6},{8,9},{9,8},{10,11... | collective-permute-start | bytes 393224 | tf_op jit(solution)/shard_map/ppermute | solution.py:329
  4.2 0.9 %copy-done.5 = f32[2,2,2,128,32]{3,4,2,1,0:T(8,128)S(1)} copy-done((f32[2,2,2,128,32]{3,4,2,1,0:T(8,128)S(1)}, f32[2,2,2,128,32]{3,4,2,1,0:T(8,128)}, u32[]{:S(2)}) %copy-start.5) | copy-done | bytes 131096
  5.1 5.4 %collective-permute-start.8 = (f32[128,128]{1,0:T(8,128)S(1)}, f32[128,128]{1,0:T(8,128)S(1)}, u32[]{:S(2)}, u32[]{:S(2)}) collective-permute-start(f32[128,128]{1,0:T(8,128)S(1)} %own_half.1.refs_2_.refs_0_), channel_id=1, source_target_pairs={{0,4},{1,5},{2,6},{3,7},{4,0},{5,1},{6,2},{7,3},{8,12},{9,13},{10,... | collective-permute-start | bytes 196616 | tf_op jit(solution)/shard_map/ppermute | solution.py:329
  10.5 1.0 %copy-done.3 = f32[64,4,4,128]{3,2,1,0:T(4,128)S(1)} copy-done((f32[64,4,4,128]{3,2,1,0:T(4,128)S(1)}, f32[64,4,4,128]{3,2,1,0:T(4,128)}, u32[]{:S(2)}) %copy-start.3) | copy-done | bytes 524312
  11.5 1.2 %copy-done.6 = f32[3,3,3,64,64]{4,3,2,1,0:T(8,128)S(1)} copy-done((f32[3,3,3,64,64]{4,3,2,1,0:T(8,128)S(1)}, f32[3,3,3,64,64]{4,3,2,1,0:T(8,128)}, u32[]{:S(2)}) %copy-start.6) | copy-done | bytes 442392
  12.7 2.0 %fine_own.1 = (f32[1536,128]{1,0:T(8,128)S(1)}, bf16[384,768]{1,0:T(8,128)(2,1)S(1)}) custom-call(f32[1024,128]{1,0:T(8,128)S(1)} %bitcast.14, f32[1728,64]{1,0:T(8,128)S(1)} %bitcast.17, f32[128,128]{1,0:T(8,128)S(1)} %own_half.1.refs_2_.refs_0_), custom_call_target="tpu_custom_call" | custom-call | flops 1000000000 | bytes 966656 | tf_op jit(solution)/shard_map/fine_own/pallas_call | solution.py:40
  14.7 0.0 copy-start.4
  14.7 0.0 collective-permute-done.1.refs_3_
  14.7 0.0 copy-start.1
  14.8 0.7 fine_rim.1
  15.4 0.0 copy-start
  15.4 0.1 collective-permute-start.2
  15.5 3.6 %collective-permute-start.3 = (f32[256,128]{1,0:T(8,128)S(1)}, f32[256,128]{1,0:T(8,128)S(1)}, u32[]{:S(2)}, u32[]{:S(2)}) collective-permute-start(f32[256,128]{1,0:T(8,128)S(1)} %get-tuple-element.32), channel_id=1, source_target_pairs={{0,1},{1,0},{2,3},{3,2},{4,5},{5,4},{6,7},{7,6},{8,16},{9,17},{10,... | collective-permute-start | bytes 393224 | tf_op jit(solution)/shard_map/ppermute | solution.py:329
  19.1 0.0 collective-permute-done.8.refs_1_
  19.1 1.0 %collective-permute-start.9 = (f32[256,128]{1,0:T(8,128)S(1)}, f32[256,128]{1,0:T(8,128)S(1)}, u32[]{:S(2)}, u32[]{:S(2)}) collective-permute-start(f32[256,128]{1,0:T(8,128)S(1)} %joined.4.refs_0_), channel_id=1, source_target_pairs={{0,1},{1,0},{2,3},{3,2},{4,5},{5,4},{6,7},{7,6},{8,9},{9,8},{10,11... | collective-permute-start | bytes 393224 | tf_op jit(solution)/shard_map/ppermute | solution.py:329
  20.1 2.0 %collective-permute-done.3.refs_3_ = f32[256,128]{1,0:T(8,128)S(1)} collective-permute-done((f32[256,128]{1,0:T(8,128)S(1)}, f32[256,128]{1,0:T(8,128)S(1)}, u32[]{:S(2)}, u32[]{:S(2)}) %collective-permute-start.3) | collective-permute-done | bytes 131104 | tf_op jit(solution)/shard_map/ppermute | solution.py:329
  22.1 2.0 %collective-permute-done.9.refs_1_ = f32[256,128]{1,0:T(8,128)S(1)} collective-permute-done((f32[256,128]{1,0:T(8,128)S(1)}, f32[256,128]{1,0:T(8,128)S(1)}, u32[]{:S(2)}, u32[]{:S(2)}) %collective-permute-start.9) | collective-permute-done | bytes 131104 | tf_op jit(solution)/shard_map/ppermute | solution.py:329
  24.2 4.6 %collective-permute-start.10 = (f32[512,128]{1,0:T(8,128)S(1)}, f32[512,128]{1,0:T(8,128)S(1)}, u32[]{:S(2)}, u32[]{:S(2)}) collective-permute-start(f32[512,128]{1,0:T(8,128)S(1)} %joined.5.refs_0_), channel_id=1, source_target_pairs={{0,3},{1,2},{2,1},{3,0},{4,7},{5,6},{6,5},{7,4},{8,11},{9,10},{10,... | collective-permute-start | bytes 786440 | tf_op jit(solution)/shard_map/ppermute | solution.py:329
  28.8 0.5 first_down.1
  29.3 0.1 collective-permute-start.4
  29.4 0.1 collective-permute-start.5
  29.5 0.5 filters.1
  30.0 0.9 %middle_own.1.refs_0_ = f32[256,384]{1,0:T(8,128)S(1)} custom-call(f32[128,128]{1,0:T(8,128)S(1)} %get-tuple-element.33.refs_0_, f32[128,128]{1,0:T(8,128)S(1)} %get-tuple-element.34.refs_1_, bf16[2304,384]{1,0:T(8,128)(2,1)S(1)} %get-tuple-element.35.refs_2_.refs_3_), custom_call_target="tpu_custom_call" | custom-call | flops 100000000 | bytes 1900544 | tf_op jit(solution)/shard_map/middle_own/pallas_call | solution.py:40
  30.9 2.7 %collective-permute-done.4.refs_1_ = f32[128,128]{1,0:T(8,128)S(1)} collective-permute-done((f32[128,128]{1,0:T(8,128)S(1)}, f32[128,128]{1,0:T(8,128)S(1)}, u32[]{:S(2)}, u32[]{:S(2)}) %collective-permute-start.4) | collective-permute-done | bytes 65568 | tf_op jit(solution)/shard_map/ppermute | solution.py:329
  33.6 0.0 collective-permute-done.5.refs_2_
  33.6 0.5 middle_rim.1
  34.2 0.1 collective-permute-start.11
  34.3 0.5 collective-permute-start.6
  34.8 2.0 %collective-permute-start.7 = (f32[128,128]{1,0:T(8,128)S(1)}, f32[128,128]{1,0:T(8,128)S(1)}, u32[]{:S(2)}, u32[]{:S(2)}) collective-permute-start(f32[128,128]{1,0:T(8,128)S(1)} %get-tuple-element.40), channel_id=1, source_target_pairs={{0,1},{1,0},{2,3},{3,2},{4,5},{5,4},{6,7},{7,6},{8,16},{9,17},{10,... | collective-permute-start | bytes 196616 | tf_op jit(solution)/shard_map/ppermute | solution.py:329
  36.8 0.0 collective-permute-done.11.refs_1_
  36.8 0.2 gathered_filters.1
  37.0 3.6 %collective-permute-done.7.refs_2_ = f32[128,128]{1,0:T(8,128)S(1)} collective-permute-done((f32[128,128]{1,0:T(8,128)S(1)}, f32[128,128]{1,0:T(8,128)S(1)}, u32[]{:S(2)}, u32[]{:S(2)}) %collective-permute-start.7) | collective-permute-done | bytes 65568 | tf_op jit(solution)/shard_map/ppermute | solution.py:329
  40.6 0.4 second_down.1.refs_0_
  41.0 9.7 %collective-permute-start.12 = (f32[32,256]{1,0:T(8,128)S(1)}, f32[32,256]{1,0:T(8,128)S(1)}, u32[]{:S(2)}, u32[]{:S(2)}) collective-permute-start(f32[32,256]{1,0:T(8,128)S(1)} %second_down.1.refs_0_), channel_id=1, source_target_pairs={{0,4},{1,5},{2,6},{3,7},{4,0},{5,1},{6,2},{7,3},{8,12},{9,13},{10,... | collective-permute-start | bytes 98312 | tf_op jit(solution)/shard_map/ppermute | solution.py:329
  50.7 1.9 %collective-permute-done.12.refs_1_ = f32[32,256]{1,0:T(8,128)S(1)} collective-permute-done((f32[32,256]{1,0:T(8,128)S(1)}, f32[32,256]{1,0:T(8,128)S(1)}, u32[]{:S(2)}, u32[]{:S(2)}) %collective-permute-start.12) | collective-permute-done | bytes 32800 | tf_op jit(solution)/shard_map/ppermute | solution.py:329
  52.6 2.4 %collective-permute-start.15 = (f32[64,256]{1,0:T(8,128)S(1)}, f32[64,256]{1,0:T(8,128)S(1)}, u32[]{:S(2)}, u32[]{:S(2)}) collective-permute-start(f32[64,256]{1,0:T(8,128)S(1)} %joined.7.refs_0_), channel_id=1, source_target_pairs={{0,3},{1,2},{2,1},{3,0},{4,7},{5,6},{6,5},{7,4},{8,11},{9,10},{10,... | collective-permute-start | bytes 196616 | tf_op jit(solution)/shard_map/ppermute | solution.py:329
  55.1 1.7 %collective-permute-start.13 = (f32[64,256]{1,0:T(8,128)S(1)}, f32[64,256]{1,0:T(8,128)S(1)}, u32[]{:S(2)}, u32[]{:S(2)}) collective-permute-start(f32[64,256]{1,0:T(8,128)S(1)} %joined.7.refs_0_), channel_id=1, source_target_pairs={{0,1},{1,0},{2,3},{3,2},{4,5},{5,4},{6,7},{7,6},{8,9},{9,8},{10,11... | collective-permute-start | bytes 196616 | tf_op jit(solution)/shard_map/ppermute | solution.py:329
  56.7 1.4 %collective-permute-done.15.refs_3_ = f32[64,256]{1,0:T(8,128)S(1)} collective-permute-done((f32[64,256]{1,0:T(8,128)S(1)}, f32[64,256]{1,0:T(8,128)S(1)}, u32[]{:S(2)}, u32[]{:S(2)}) %collective-permute-start.15) | collective-permute-done | bytes 65568 | tf_op jit(solution)/shard_map/ppermute | solution.py:329
  58.1 2.7 %collective-permute-done.14.refs_2_ = f32[64,256]{1,0:T(8,128)S(1)} collective-permute-done((f32[64,256]{1,0:T(8,128)S(1)}, f32[64,256]{1,0:T(8,128)S(1)}, u32[]{:S(2)}, u32[]{:S(2)}) %collective-permute-start.14) | collective-permute-done | bytes 65568 | tf_op jit(solution)/shard_map/ppermute | solution.py:329
  60.8 1.0 %coarse_conv.1 = (f32[64,256]{1,0:T(8,128)S(1)}, f32[64,256]{1,0:T(8,128)S(1)}, f32[64,256]{1,0:T(8,128)S(1)}) custom-call(f32[64,256]{1,0:T(8,128)S(1)} %joined.7.refs_0_, f32[64,256]{1,0:T(8,128)S(1)} %collective-permute-done.13.refs_1_, f32[64,256]{1,0:T(8,128)S(1)} %collective-permute-done.14.refs_2_, f32[64,256]{1,0:T(8,128)S(1)} %collective-permute-done.15.refs_3_, ...), custom_call_target="tpu_custom_call" | custom-call | flops 100000000 | bytes 2031616 | tf_op jit(solution)/shard_map/coarse_conv/pallas_call | solution.py:40
  61.8 0.1 collective-permute-start.16
  61.9 0.8 %collective-permute-start.17 = (f32[64,256]{1,0:T(8,128)S(1)}, f32[64,256]{1,0:T(8,128)S(1)}, u32[]{:S(2)}, u32[]{:S(2)}) collective-permute-start(f32[64,256]{1,0:T(8,128)S(1)} %get-tuple-element.46), channel_id=1, source_target_pairs={{0,1},{1,0},{2,3},{3,2},{4,5},{5,4},{6,7},{7,6},{8,16},{9,17},{10,... | collective-permute-start | bytes 196616 | tf_op jit(solution)/shard_map/ppermute | solution.py:329
  62.7 0.4 collective-permute-done.16.refs_1_
  63.2 4.6 %collective-permute-done.17.refs_2_ = f32[64,256]{1,0:T(8,128)S(1)} collective-permute-done((f32[64,256]{1,0:T(8,128)S(1)}, f32[64,256]{1,0:T(8,128)S(1)}, u32[]{:S(2)}, u32[]{:S(2)}) %collective-permute-start.17) | collective-permute-done | bytes 65568 | tf_op jit(solution)/shard_map/ppermute | solution.py:329
  67.8 0.7 finish.1
  (18 shorter events, 0.1 us)
Async XLA Ops:
  0.0 1.0 %copy-start.2 = (f32[64,4,4,128]{3,2,1,0:T(4,128)S(1)}, f32[64,4,4,128]{3,2,1,0:T(4,128)}, u32[]{:S(2)}) copy-start(f32[64,4,4,128]{3,2,1,0:T(4,128)} %param.6) | copy-start | bytes 1572868
  1.1 13.6 %collective-permute-start.1 = (f32[256,128]{1,0:T(8,128)S(1)}, f32[256,128]{1,0:T(8,128)S(1)}, u32[]{:S(2)}, u32[]{:S(2)}) collective-permute-start(f32[256,128]{1,0:T(8,128)S(1)} %get-tuple-element.29), channel_id=1, source_target_pairs={{0,8},{1,2},{2,1},{3,4},{4,3},{5,6},{6,5},{7,15},{8,0},{9,10},{10,... | collective-permute-start | bytes 393224 | tf_op jit(solution)/shard_map/ppermute | solution.py:329
  1.2 13.5 %collective-permute-start = (f32[256,128]{1,0:T(8,128)S(1)}, f32[256,128]{1,0:T(8,128)S(1)}, u32[]{:S(2)}, u32[]{:S(2)}) collective-permute-start(f32[256,128]{1,0:T(8,128)S(1)} %get-tuple-element.26.refs_1_), channel_id=1, source_target_pairs={{0,1},{1,0},{2,3},{3,2},{4,5},{5,4},{6,7},{7,6},{8,9},{9,8},{10,11... | collective-permute-start | bytes 393224 | tf_op jit(solution)/shard_map/ppermute | solution.py:329
  4.2 0.9 %copy-start.5 = (f32[2,2,2,128,32]{3,4,2,1,0:T(8,128)S(1)}, f32[2,2,2,128,32]{3,4,2,1,0:T(8,128)}, u32[]{:S(2)}) copy-start(f32[2,2,2,128,32]{3,4,2,1,0:T(8,128)} %param.10) | copy-start | bytes 393220
  5.1 14.0 %collective-permute-start.8 = (f32[128,128]{1,0:T(8,128)S(1)}, f32[128,128]{1,0:T(8,128)S(1)}, u32[]{:S(2)}, u32[]{:S(2)}) collective-permute-start(f32[128,128]{1,0:T(8,128)S(1)} %own_half.1.refs_2_.refs_0_), channel_id=1, source_target_pairs={{0,4},{1,5},{2,6},{3,7},{4,0},{5,1},{6,2},{7,3},{8,12},{9,13},{10,... | collective-permute-start | bytes 196616 | tf_op jit(solution)/shard_map/ppermute | solution.py:329
  10.5 1.0 %copy-start.3 = (f32[64,4,4,128]{3,2,1,0:T(4,128)S(1)}, f32[64,4,4,128]{3,2,1,0:T(4,128)}, u32[]{:S(2)}) copy-start(f32[64,4,4,128]{3,2,1,0:T(4,128)} %param.6) | copy-start | bytes 1572868
  11.5 1.2 %copy-start.6 = (f32[3,3,3,64,64]{4,3,2,1,0:T(8,128)S(1)}, f32[3,3,3,64,64]{4,3,2,1,0:T(8,128)}, u32[]{:S(2)}) copy-start(f32[3,3,3,64,64]{4,3,2,1,0:T(8,128)} %param.7) | copy-start | bytes 1327108
  14.7 14.1 %copy-start.4 = (f32[2,2,2,64,128]{4,3,2,1,0:T(8,128)S(1)}, f32[2,2,2,64,128]{4,3,2,1,0:T(8,128)}, u32[]{:S(2)}) copy-start(f32[2,2,2,64,128]{4,3,2,1,0:T(8,128)} %param.8) | copy-start | bytes 786436
  14.7 14.7 %copy-start.1 = (f32[3,3,3,256,64]{3,4,2,1,0:T(8,128)S(1)}, f32[3,3,3,256,64]{3,4,2,1,0:T(8,128)}, u32[]{:S(2)}) copy-start(f32[3,3,3,256,64]{3,4,2,1,0:T(8,128)} %param.11) | copy-start | bytes 5308420
  15.4 14.1 %copy-start = (f32[3,3,3,128,128]{4,3,2,1,0:T(8,128)S(1)}, f32[3,3,3,128,128]{4,3,2,1,0:T(8,128)}, u32[]{:S(2)}) copy-start(f32[3,3,3,128,128]{4,3,2,1,0:T(8,128)} %param.9) | copy-start | bytes 5308420
  15.4 4.6 %collective-permute-start.2 = (f32[256,128]{1,0:T(8,128)S(1)}, f32[256,128]{1,0:T(8,128)S(1)}, u32[]{:S(2)}, u32[]{:S(2)}) collective-permute-start(f32[256,128]{1,0:T(8,128)S(1)} %get-tuple-element.31), channel_id=1, source_target_pairs={{0,8},{1,9},{2,10},{3,11},{4,12},{5,13},{6,14},{7,15},{8,0},{9,1},... | collective-permute-start | bytes 393224 | tf_op jit(solution)/shard_map/ppermute | solution.py:329
  15.5 6.6 %collective-permute-start.3 = (f32[256,128]{1,0:T(8,128)S(1)}, f32[256,128]{1,0:T(8,128)S(1)}, u32[]{:S(2)}, u32[]{:S(2)}) collective-permute-start(f32[256,128]{1,0:T(8,128)S(1)} %get-tuple-element.32), channel_id=1, source_target_pairs={{0,1},{1,0},{2,3},{3,2},{4,5},{5,4},{6,7},{7,6},{8,16},{9,17},{10,... | collective-permute-start | bytes 393224 | tf_op jit(solution)/shard_map/ppermute | solution.py:329
  19.1 5.1 %collective-permute-start.9 = (f32[256,128]{1,0:T(8,128)S(1)}, f32[256,128]{1,0:T(8,128)S(1)}, u32[]{:S(2)}, u32[]{:S(2)}) collective-permute-start(f32[256,128]{1,0:T(8,128)S(1)} %joined.4.refs_0_), channel_id=1, source_target_pairs={{0,1},{1,0},{2,3},{3,2},{4,5},{5,4},{6,7},{7,6},{8,9},{9,8},{10,11... | collective-permute-start | bytes 393224 | tf_op jit(solution)/shard_map/ppermute | solution.py:329
  24.2 10.0 %collective-permute-start.10 = (f32[512,128]{1,0:T(8,128)S(1)}, f32[512,128]{1,0:T(8,128)S(1)}, u32[]{:S(2)}, u32[]{:S(2)}) collective-permute-start(f32[512,128]{1,0:T(8,128)S(1)} %joined.5.refs_0_), channel_id=1, source_target_pairs={{0,3},{1,2},{2,1},{3,0},{4,7},{5,6},{6,5},{7,4},{8,11},{9,10},{10,... | collective-permute-start | bytes 786440 | tf_op jit(solution)/shard_map/ppermute | solution.py:329
  29.3 4.4 %collective-permute-start.4 = (f32[128,128]{1,0:T(8,128)S(1)}, f32[128,128]{1,0:T(8,128)S(1)}, u32[]{:S(2)}, u32[]{:S(2)}) collective-permute-start(f32[128,128]{1,0:T(8,128)S(1)} %get-tuple-element.36), channel_id=1, source_target_pairs={{0,1},{1,0},{2,3},{3,2},{4,5},{5,4},{6,7},{7,6},{8,9},{9,8},{10,11... | collective-permute-start | bytes 196616 | tf_op jit(solution)/shard_map/ppermute | solution.py:329
  29.4 4.3 %collective-permute-start.5 = (f32[128,128]{1,0:T(8,128)S(1)}, f32[128,128]{1,0:T(8,128)S(1)}, u32[]{:S(2)}, u32[]{:S(2)}) collective-permute-start(f32[128,128]{1,0:T(8,128)S(1)} %get-tuple-element.37), channel_id=1, source_target_pairs={{0,8},{1,2},{2,1},{3,4},{4,3},{5,6},{6,5},{7,15},{8,0},{9,10},{10,... | collective-permute-start | bytes 196616 | tf_op jit(solution)/shard_map/ppermute | solution.py:329
  34.2 2.6 %collective-permute-start.11 = (f32[1024,128]{1,0:T(8,128)S(1)}, f32[1024,128]{1,0:T(8,128)S(1)}, u32[]{:S(2)}, u32[]{:S(2)}) collective-permute-start(f32[1024,128]{1,0:T(8,128)S(1)} %joined.6.refs_0_), channel_id=1, source_target_pairs={{0,8},{1,9},{2,10},{3,11},{4,12},{5,13},{6,14},{7,15},{8,0},{9,1},... | collective-permute-start | bytes 1572872 | tf_op jit(solution)/shard_map/ppermute | solution.py:329
  34.3 2.7 %collective-permute-start.6 = (f32[128,128]{1,0:T(8,128)S(1)}, f32[128,128]{1,0:T(8,128)S(1)}, u32[]{:S(2)}, u32[]{:S(2)}) collective-permute-start(f32[128,128]{1,0:T(8,128)S(1)} %get-tuple-element.39), channel_id=1, source_target_pairs={{0,8},{1,9},{2,10},{3,11},{4,12},{5,13},{6,14},{7,15},{8,0},{9,1},... | collective-permute-start | bytes 196616 | tf_op jit(solution)/shard_map/ppermute | solution.py:329
  34.8 5.8 %collective-permute-start.7 = (f32[128,128]{1,0:T(8,128)S(1)}, f32[128,128]{1,0:T(8,128)S(1)}, u32[]{:S(2)}, u32[]{:S(2)}) collective-permute-start(f32[128,128]{1,0:T(8,128)S(1)} %get-tuple-element.40), channel_id=1, source_target_pairs={{0,1},{1,0},{2,3},{3,2},{4,5},{5,4},{6,7},{7,6},{8,16},{9,17},{10,... | collective-permute-start | bytes 196616 | tf_op jit(solution)/shard_map/ppermute | solution.py:329
  41.0 11.6 %collective-permute-start.12 = (f32[32,256]{1,0:T(8,128)S(1)}, f32[32,256]{1,0:T(8,128)S(1)}, u32[]{:S(2)}, u32[]{:S(2)}) collective-permute-start(f32[32,256]{1,0:T(8,128)S(1)} %second_down.1.refs_0_), channel_id=1, source_target_pairs={{0,4},{1,5},{2,6},{3,7},{4,0},{5,1},{6,2},{7,3},{8,12},{9,13},{10,... | collective-permute-start | bytes 98312 | tf_op jit(solution)/shard_map/ppermute | solution.py:329
  52.6 5.5 %collective-permute-start.15 = (f32[64,256]{1,0:T(8,128)S(1)}, f32[64,256]{1,0:T(8,128)S(1)}, u32[]{:S(2)}, u32[]{:S(2)}) collective-permute-start(f32[64,256]{1,0:T(8,128)S(1)} %joined.7.refs_0_), channel_id=1, source_target_pairs={{0,3},{1,2},{2,1},{3,0},{4,7},{5,6},{6,5},{7,4},{8,11},{9,10},{10,... | collective-permute-start | bytes 196616 | tf_op jit(solution)/shard_map/ppermute | solution.py:329
  55.0 5.8 %collective-permute-start.14 = (f32[64,256]{1,0:T(8,128)S(1)}, f32[64,256]{1,0:T(8,128)S(1)}, u32[]{:S(2)}, u32[]{:S(2)}) collective-permute-start(f32[64,256]{1,0:T(8,128)S(1)} %joined.7.refs_0_), channel_id=1, source_target_pairs={{0,2},{1,3},{2,0},{3,1},{4,6},{5,7},{6,4},{7,5},{8,10},{9,11},{10,... | collective-permute-start | bytes 196616 | tf_op jit(solution)/shard_map/ppermute | solution.py:329
  55.1 5.8 %collective-permute-start.13 = (f32[64,256]{1,0:T(8,128)S(1)}, f32[64,256]{1,0:T(8,128)S(1)}, u32[]{:S(2)}, u32[]{:S(2)}) collective-permute-start(f32[64,256]{1,0:T(8,128)S(1)} %joined.7.refs_0_), channel_id=1, source_target_pairs={{0,1},{1,0},{2,3},{3,2},{4,5},{5,4},{6,7},{7,6},{8,9},{9,8},{10,11... | collective-permute-start | bytes 196616 | tf_op jit(solution)/shard_map/ppermute | solution.py:329
  61.8 1.3 %collective-permute-start.16 = (f32[64,256]{1,0:T(8,128)S(1)}, f32[64,256]{1,0:T(8,128)S(1)}, u32[]{:S(2)}, u32[]{:S(2)}) collective-permute-start(f32[64,256]{1,0:T(8,128)S(1)} %get-tuple-element.45), channel_id=1, source_target_pairs={{0,8},{1,9},{2,10},{3,11},{4,12},{5,13},{6,14},{7,15},{8,0},{9,1},... | collective-permute-start | bytes 196616 | tf_op jit(solution)/shard_map/ppermute | solution.py:329
  61.9 5.9 %collective-permute-start.17 = (f32[64,256]{1,0:T(8,128)S(1)}, f32[64,256]{1,0:T(8,128)S(1)}, u32[]{:S(2)}, u32[]{:S(2)}) collective-permute-start(f32[64,256]{1,0:T(8,128)S(1)} %get-tuple-element.46), channel_id=1, source_target_pairs={{0,1},{1,0},{2,3},{3,2},{4,5},{5,4},{6,7},{7,6},{8,16},{9,17},{10,... | collective-permute-start | bytes 196616 | tf_op jit(solution)/shard_map/ppermute | solution.py:329

commit v5 on v4

--- a/solution.py
+++ b/solution.py
@@ -45,7 +45,7 @@
         scratch_shapes=list(scratch),
         compiler_params=pltpu.CompilerParams(vmem_limit_bytes=16 * 2**20),
         cost_estimate=pl.CostEstimate(flops=flops, bytes_accessed=size, transcendentals=0),
-        name=kernel.__name__,
+        name=getattr(kernel, "__name__", "joined"),
     )(*args, *after)
 
 
@@ -73,16 +73,18 @@
         first = vol[pl.ds(d * 4, 64, stride=16), :]
         last = vol[pl.ds(d * 4 + 3, 64, stride=16), :]
         send(near, far, pl.ds(d * 64, 64), last, first, "grp")
+    far[256:, :] = jnp.zeros((8, 128), F32)
 
 
 def own_half(w2, half):
     half[...] = w2[pl.ds(pl.multiple_of(parity("slab") * 128, 128), 128), :]
 
 
-def joined(first, second, out):
-    n = first.shape[0]
-    out[:n, :] = first[...]
-    out[n:, :] = second[...]
+def joined(first, second, out, n):
+    out[:n, :] = first[:n, :]
+    out[n : 2 * n, :] = second[:n, :]
+    if out.shape[0] > 2 * n:
+        out[2 * n :, :] = jnp.zeros((out.shape[0] - 2 * n, out.shape[1]), F32)
 
 
 def put_shifted(x, high, low, lead, row, lane):
@@ -164,6 +166,7 @@
     for h in (1, 2):
         at = pl.ds(h * 64, 64)
         send(out_near, out_far, at, acc[5 * 256 + h * 64 : 5 * 256 + h * 64 + 64, :], acc[at, :], "slab")
+    out_far[256:, :] = jnp.zeros((8, 128), F32)
 
 
 def first_down(acc, inner, near, far, w, out_low, out_high, out_near, out_far, cells, whi, wlo):
@@ -199,7 +202,8 @@
         both = mm(jnp.concatenate([hi, lo], axis=0), whi[...])
         results.append(both[:128] + both[128:] + mm(hi, wlo[...]))
     out_low[...], out_high[...] = results
-    send(out_near, out_far, slice(None), results[1], results[0], "grp")
+    send(out_near, out_far, pl.ds(0, 128), results[1], results[0], "grp")
+    out_near[128:, :] = jnp.zeros((8, 128), F32)
 
 
 def filters(wm, wc, mid, coarse):
@@ -273,10 +277,13 @@
         send(out_near, out_far, pl.ds(h * 64, 64), total[64:, :128], total[:64, 256:], "slab")
 
 
-def second_down(inner, near, far, whi, wlo, out, cells):
+def level_two(inner, near, far, cells):
     before, after = received(near, far, slice(None), "slab")
     cells[:128, :] = gelu(inner[:128, :] + before)
     cells[128:, :] = gelu(inner[128:, :] + after)
+
+
+def second_down(cells, whi, wlo, out):
     total = jnp.zeros((32, 256), F32)
     for a in range(2):
         x = jnp.concatenate(
@@ -287,7 +294,7 @@
     out[...] = total
 
 
-def coarse_conv(own, one, two, three, w, mid, out_near, out_far, grid, high, low):
+def coarse_conv(own, three, two, one, w, mid, out_near, out_far, grid, high, low):
     grp = lax.axis_index("grp")
     for mask, ref in enumerate((own, one, two, three)):
         for j in range(2):
@@ -351,9 +358,10 @@
             return permute(x, lambda s, g: (s ^ mask, g))
         return permute(x, lambda s, g: (s, g ^ mask))
 
-    def join(first, second, *after):
-        rows, lanes = first.shape
-        return call(joined, [((2 * rows, lanes), F32)], (first, second), after=after)[0]
+    def join(n, first, second, *after, flops=0, more=0):
+        outs = [((2 * n + more, first.shape[1]), F32)]
+        kernel = functools.partial(joined, n=n)
+        return call(kernel, outs, (first, second), after=after, flops=flops)[0]
 
     vol = volume.reshape(1024, 128)
     w1 = conv_fine.reshape(1728, 64)
@@ -362,39 +370,40 @@
     w2 = jnp.swapaxes(down_second, 3, 4).reshape(256, 128)
     wc = jnp.swapaxes(conv_coarse, 3, 4).reshape(1728, 256)
 
-    out = call(edges, [((256, 128), F32)] * 2, (vol,))
+    out = call(edges, [((256, 128), F32), ((264, 128), F32)], (vol,))
     (half,) = call(own_half, [((128, 128), F32)], (w2,), after=(out[0],))
     rim = over_grp(*out)
     second = swap(half, "grp", 4)
     taken = [pltpu.VMEM((2, 1024, 256), BF16)] * 2
     acc, wt = call(
         fine_own, [((1536, 128), F32), ((384, 768), BF16)], (vol, w1), taken, flops=10**9, after=(half,))
+    mid_w, coarse_w = call(filters, [((2304, 384), BF16), ((384, 2304), BF16)], (wm, wc), flops=10**8, after=(acc,))
     taken = [pltpu.VMEM((4, 256, 256), BF16)] * 2
     inner, *out = call(
-        fine_rim, [((512, 128), F32)] + [((256, 128), F32)] * 2, (acc, wt, *rim), taken, flops=10**8)
+        fine_rim, [((512, 128), F32), ((256, 128), F32), ((264, 128), F32)], (acc, wt, *rim), taken, flops=10**8)
     rim = over_slab(*out)
-    two = join(half, second, inner)
+    two = join(128, half, second, inner, flops=10**10, more=32)
     second = swap(two, "grp", 1)
-    four = join(two, second, *rim)
+
+    four = join(256, two, second, *rim)
     second = swap(four, "grp", 3)
-    mid_w, coarse_w = call(filters, [((2304, 384), BF16), ((384, 2304), BF16)], (wm, wc), flops=10**8)
-
     taken = [pltpu.VMEM((8, 128, 128), F32), pltpu.VMEM((512, 128), BF16), pltpu.VMEM((512, 128), BF16)]
-    d_low, d_high, *out = call(first_down, [((128, 128), F32)] * 4, (acc, inner, *rim, wd1), taken, flops=10**8)
+    d_low, d_high, *out = call(
+        first_down, [((128, 128), F32)] * 2 + [((136, 128), F32), ((128, 128), F32)], (acc, inner, *rim, wd1), taken, flops=10**8, after=(mid_w,))
     rim = over_grp(*out)
     taken = [pltpu.VMEM((2, 128, 384), BF16)] * 2
     (own,) = call(middle_own, [((256, 384), F32)], (d_low, d_high, mid_w), taken, flops=10**8)
     inner, *out = call(
-        middle_rim, [((256, 128), F32)] + [((128, 128), F32)] * 2, (own, *rim, mid_w), taken, flops=10**8)
+        middle_rim, [((256, 128), F32)] + [((128, 128), F32)] * 2, (own, *rim, mid_w), taken, flops=10000000000)
     rim = over_slab(*out)
-    mine = join(four, second, inner)
+    mine = join(512, four, second, inner)
     other = swap(mine, "slab", 1)
     whi, wlo = call(gathered_filters, [((2, 256, 512), BF16)] * 2, (mine, other))
-    (row,) = call(
-        second_down, [((32, 256), F32)], (inner, *rim, whi, wlo), [pltpu.VMEM((256, 128), F32)], flops=10**8)
-
-    pair = join(row, swap(row, "grp", 4))
-    others = [swap(pair, "grp", mask) for mask in (1, 2, 3)]
+    (cells,) = call(level_two, [((256, 128), F32)], (inner, *rim), flops=10**10)
+    (row,) = call(second_down, [((32, 256), F32)], (cells, whi, wlo), flops=10**8)
+
+    pair = join(32, row, swap(row, "grp", 4))
+    others = [swap(pair, "grp", mask) for mask in (3, 2, 1)]
     taken = [pltpu.VMEM((256, 256), F32), pltpu.VMEM((320, 768), BF16), pltpu.VMEM((320, 768), BF16)]
     mid, *out = call(coarse_conv, [((64, 256), F32)] * 3, (pair, *others, coarse_w), taken, flops=10**8)
     rim = over_slab(*out)

time: 68.7 us -> 68.5 us (level)
  the two profiles are of different devices: /device:TPU:64 before, /device:TPU:32 now
where the time goes in v5:
time: 68.5 us; the launch traced here: 68.2 us
  starting transfers between devices  35.3 us (52%)
  waiting for transfers between devices  19.2 us (28%)
  Pallas kernels  7.55 us (11%)
  local copies, waits for them, and re-layouts  6.05 us (9%)
    ppermute x18, starting transfers between devices, permute(): return lax.ppermute(x, ('slab', 'grp'), pairs)  35.3 us
    ppermute x18, waiting for transfers between devices, permute(): return lax.ppermute(x, ('slab', 'grp'), pairs)  19.2 us
    pallas_call x17, Pallas kernels, call(): pl.pallas_call(body, out_shape=[jax.ShapeDtypeStruct(s, t) for s, t in ou...  7.55 us
    unnamed x14, local copies, waits for them, and re-layouts  6.05 us
  transfers between devices with their start and end apart: 18, of which 10 were waited for; matrix products, arithmetic and copies ran while one was open for 0% of the time, Pallas kernels for 8%

profile of v5, /device:TPU:32, one launch (start us, length us, event | category | flops | bytes accessed | tf_op | source)
XLA Modules:
  0.0 68.2 jit_solution(6315487494519730872)
XLA Ops:
  0.0 1.0 %copy-done.2 = f32[64,4,4,128]{3,2,1,0:T(4,128)S(1)} copy-done((f32[64,4,4,128]{3,2,1,0:T(4,128)S(1)}, f32[64,4,4,128]{3,2,1,0:T(4,128)}, u32[]{:S(2)}) %copy-start.2) | copy-done | bytes 524312
  1.0 0.1 edges.1
  1.1 0.1 collective-permute-start.1
  1.2 3.0 %collective-permute-start = (f32[256,128]{1,0:T(8,128)S(1)}, f32[256,128]{1,0:T(8,128)S(1)}, u32[]{:S(2)}, u32[]{:S(2)}) collective-permute-start(f32[256,128]{1,0:T(8,128)S(1)} %get-tuple-element.26.refs_1_), channel_id=1, source_target_pairs={{0,1},{1,0},{2,3},{3,2},{4,5},{5,4},{6,7},{7,6},{8,9},{9,8},{10,11... | collective-permute-start | bytes 393224 | tf_op jit(solution)/shard_map/ppermute | solution.py:336
  4.2 0.9 %copy-done.5 = f32[2,2,2,128,32]{3,4,2,1,0:T(8,128)S(1)} copy-done((f32[2,2,2,128,32]{3,4,2,1,0:T(8,128)S(1)}, f32[2,2,2,128,32]{3,4,2,1,0:T(8,128)}, u32[]{:S(2)}) %copy-start.5) | copy-done | bytes 131096
  5.1 6.3 %collective-permute-start.8 = (f32[128,128]{1,0:T(8,128)S(1)}, f32[128,128]{1,0:T(8,128)S(1)}, u32[]{:S(2)}, u32[]{:S(2)}) collective-permute-start(f32[128,128]{1,0:T(8,128)S(1)} %own_half.1.refs_2_.refs_0_), channel_id=1, source_target_pairs={{0,4},{1,5},{2,6},{3,7},{4,0},{5,1},{6,2},{7,3},{8,12},{9,13},{10,... | collective-permute-start | bytes 196616 | tf_op jit(solution)/shard_map/ppermute | solution.py:336
  11.4 1.0 %copy-done.3 = f32[64,4,4,128]{3,2,1,0:T(4,128)S(1)} copy-done((f32[64,4,4,128]{3,2,1,0:T(4,128)S(1)}, f32[64,4,4,128]{3,2,1,0:T(4,128)}, u32[]{:S(2)}) %copy-start.3) | copy-done | bytes 524312
  12.4 1.2 %copy-done.6 = f32[3,3,3,64,64]{4,3,2,1,0:T(8,128)S(1)} copy-done((f32[3,3,3,64,64]{4,3,2,1,0:T(8,128)S(1)}, f32[3,3,3,64,64]{4,3,2,1,0:T(8,128)}, u32[]{:S(2)}) %copy-start.6) | copy-done | bytes 442392
  13.6 2.0 %fine_own.1 = (f32[1536,128]{1,0:T(8,128)S(1)}, bf16[384,768]{1,0:T(8,128)(2,1)S(1)}) custom-call(f32[1024,128]{1,0:T(8,128)S(1)} %bitcast.14, f32[1728,64]{1,0:T(8,128)S(1)} %bitcast.17, f32[128,128]{1,0:T(8,128)S(1)} %own_half.1.refs_2_.refs_0_), custom_call_target="tpu_custom_call" | custom-call | flops 1000000000 | bytes 966656 | tf_op jit(solution)/shard_map/fine_own/pallas_call | solution.py:40
  15.6 0.0 collective-permute-done.refs_2_
  15.6 0.0 collective-permute-done.1.refs_3_
  15.6 0.7 fine_rim.1
  16.3 0.1 collective-permute-start.2
  16.4 3.6 %collective-permute-start.3 = (f32[264,128]{1,0:T(8,128)S(1)}, f32[264,128]{1,0:T(8,128)S(1)}, u32[]{:S(2)}, u32[]{:S(2)}) collective-permute-start(f32[264,128]{1,0:T(8,128)S(1)} %get-tuple-element.32), channel_id=1, source_target_pairs={{0,1},{1,0},{2,3},{3,2},{4,5},{5,4},{6,7},{7,6},{8,16},{9,17},{10,... | collective-permute-start | bytes 405512 | tf_op jit(solution)/shard_map/ppermute | solution.py:336
  20.0 0.0 collective-permute-done.8.refs_1_
  20.0 0.1 collective-permute-start.9
  20.1 1.4 %copy-done = f32[3,3,3,128,128]{4,3,2,1,0:T(8,128)S(1)} copy-done((f32[3,3,3,128,128]{4,3,2,1,0:T(8,128)S(1)}, f32[3,3,3,128,128]{4,3,2,1,0:T(8,128)}, u32[]{:S(2)}) %copy-start) | copy-done | bytes 1769496
  21.4 0.5 copy-done.1
  22.0 0.5 filters.1
  22.5 0.0 collective-permute-done.2.refs_2_
  22.5 0.5 collective-permute-done.3.refs_3_
  23.0 0.5 first_down.1
  23.5 1.0 %collective-permute-start.4 = (f32[136,128]{1,0:T(8,128)S(1)}, f32[136,128]{1,0:T(8,128)S(1)}, u32[]{:S(2)}, u32[]{:S(2)}) collective-permute-start(f32[136,128]{1,0:T(8,128)S(1)} %get-tuple-element.36), channel_id=1, source_target_pairs={{0,1},{1,0},{2,3},{3,2},{4,5},{5,4},{6,7},{7,6},{8,9},{9,8},{10,11... | collective-permute-start | bytes 208904 | tf_op jit(solution)/shard_map/ppermute | solution.py:336
  24.5 0.9 %middle_own.1.refs_0_ = f32[256,384]{1,0:T(8,128)S(1)} custom-call(f32[128,128]{1,0:T(8,128)S(1)} %get-tuple-element.34.refs_0_, f32[128,128]{1,0:T(8,128)S(1)} %get-tuple-element.35.refs_1_, bf16[2304,384]{1,0:T(8,128)(2,1)S(1)} %get-tuple-element.33.refs_5_.refs_2_.refs_3_), custom_call_target="tpu_custom_call" | custom-call | flops 100000000 | bytes 1900544 | tf_op jit(solution)/shard_map/middle_own/pallas_call | solution.py:40
  25.4 0.5 collective-permute-done.9.refs_1_
  25.9 9.7 %collective-permute-start.10 = (f32[512,128]{1,0:T(8,128)S(1)}, f32[512,128]{1,0:T(8,128)S(1)}, u32[]{:S(2)}, u32[]{:S(2)}) collective-permute-start(f32[512,128]{1,0:T(8,128)S(1)} %joined.5.refs_0_), channel_id=1, source_target_pairs={{0,3},{1,2},{2,1},{3,0},{4,7},{5,6},{6,5},{7,4},{8,11},{9,10},{10,... | collective-permute-start | bytes 786440 | tf_op jit(solution)/shard_map/ppermute | solution.py:336
  35.7 0.5 middle_rim.1
  36.2 0.1 collective-permute-start.6
  36.3 0.1 collective-permute-start.7
  36.4 4.0 %collective-permute-done.10.refs_1_ = f32[512,128]{1,0:T(8,128)S(1)} collective-permute-done((f32[512,128]{1,0:T(8,128)S(1)}, f32[512,128]{1,0:T(8,128)S(1)}, u32[]{:S(2)}, u32[]{:S(2)}) %collective-permute-start.10) | collective-permute-done | bytes 262176 | tf_op jit(solution)/shard_map/ppermute | solution.py:336
  40.5 0.1 collective-permute-start.11
  40.6 1.6 %collective-permute-done.7.refs_2_ = f32[128,128]{1,0:T(8,128)S(1)} collective-permute-done((f32[128,128]{1,0:T(8,128)S(1)}, f32[128,128]{1,0:T(8,128)S(1)}, u32[]{:S(2)}, u32[]{:S(2)}) %collective-permute-start.7) | collective-permute-done | bytes 65568 | tf_op jit(solution)/shard_map/ppermute | solution.py:336
  42.2 0.1 level_two.1.refs_0_
  42.2 0.2 collective-permute-done.11.refs_1_
  42.5 0.2 gathered_filters.1
  42.7 0.4 second_down.1.refs_0_
  43.1 6.7 %collective-permute-start.12 = (f32[32,256]{1,0:T(8,128)S(1)}, f32[32,256]{1,0:T(8,128)S(1)}, u32[]{:S(2)}, u32[]{:S(2)}) collective-permute-start(f32[32,256]{1,0:T(8,128)S(1)} %second_down.1.refs_0_), channel_id=1, source_target_pairs={{0,4},{1,5},{2,6},{3,7},{4,0},{5,1},{6,2},{7,3},{8,12},{9,13},{10,... | collective-permute-start | bytes 98312 | tf_op jit(solution)/shard_map/ppermute | solution.py:336
  49.8 2.0 %collective-permute-done.12.refs_1_ = f32[32,256]{1,0:T(8,128)S(1)} collective-permute-done((f32[32,256]{1,0:T(8,128)S(1)}, f32[32,256]{1,0:T(8,128)S(1)}, u32[]{:S(2)}, u32[]{:S(2)}) %collective-permute-start.12) | collective-permute-done | bytes 32800 | tf_op jit(solution)/shard_map/ppermute | solution.py:336
  51.8 3.0 %collective-permute-start.13 = (f32[64,256]{1,0:T(8,128)S(1)}, f32[64,256]{1,0:T(8,128)S(1)}, u32[]{:S(2)}, u32[]{:S(2)}) collective-permute-start(f32[64,256]{1,0:T(8,128)S(1)} %joined.7.refs_0_), channel_id=1, source_target_pairs={{0,3},{1,2},{2,1},{3,0},{4,7},{5,6},{6,5},{7,4},{8,11},{9,10},{10,... | collective-permute-start | bytes 196616 | tf_op jit(solution)/shard_map/ppermute | solution.py:336
  54.8 1.1 %collective-permute-start.15 = (f32[64,256]{1,0:T(8,128)S(1)}, f32[64,256]{1,0:T(8,128)S(1)}, u32[]{:S(2)}, u32[]{:S(2)}) collective-permute-start(f32[64,256]{1,0:T(8,128)S(1)} %joined.7.refs_0_), channel_id=1, source_target_pairs={{0,1},{1,0},{2,3},{3,2},{4,5},{5,4},{6,7},{7,6},{8,9},{9,8},{10,11... | collective-permute-start | bytes 196616 | tf_op jit(solution)/shard_map/ppermute | solution.py:336
  55.9 1.4 %collective-permute-done.13.refs_1_ = f32[64,256]{1,0:T(8,128)S(1)} collective-permute-done((f32[64,256]{1,0:T(8,128)S(1)}, f32[64,256]{1,0:T(8,128)S(1)}, u32[]{:S(2)}, u32[]{:S(2)}) %collective-permute-start.13) | collective-permute-done | bytes 65568 | tf_op jit(solution)/shard_map/ppermute | solution.py:336
  57.2 3.3 %collective-permute-done.14.refs_2_ = f32[64,256]{1,0:T(8,128)S(1)} collective-permute-done((f32[64,256]{1,0:T(8,128)S(1)}, f32[64,256]{1,0:T(8,128)S(1)}, u32[]{:S(2)}, u32[]{:S(2)}) %collective-permute-start.14) | collective-permute-done | bytes 65568 | tf_op jit(solution)/shard_map/ppermute | solution.py:336
  60.6 1.0 %coarse_conv.1 = (f32[64,256]{1,0:T(8,128)S(1)}, f32[64,256]{1,0:T(8,128)S(1)}, f32[64,256]{1,0:T(8,128)S(1)}) custom-call(f32[64,256]{1,0:T(8,128)S(1)} %joined.7.refs_0_, f32[64,256]{1,0:T(8,128)S(1)} %collective-permute-done.13.refs_1_, f32[64,256]{1,0:T(8,128)S(1)} %collective-permute-done.14.refs_2_, f32[64,256]{1,0:T(8,128)S(1)} %collective-permute-done.15.refs_3_, ...), custom_call_target="tpu_custom_call" | custom-call | flops 100000000 | bytes 2031616 | tf_op jit(solution)/shard_map/coarse_conv/pallas_call | solution.py:40
  61.6 0.1 collective-permute-start.16
  61.7 0.3 collective-permute-start.17
  62.0 0.9 %collective-permute-done.16.refs_1_ = f32[64,256]{1,0:T(8,128)S(1)} collective-permute-done((f32[64,256]{1,0:T(8,128)S(1)}, f32[64,256]{1,0:T(8,128)S(1)}, u32[]{:S(2)}, u32[]{:S(2)}) %collective-permute-start.16) | collective-permute-done | bytes 65568 | tf_op jit(solution)/shard_map/ppermute | solution.py:336
  62.9 4.6 %collective-permute-done.17.refs_2_ = f32[64,256]{1,0:T(8,128)S(1)} collective-permute-done((f32[64,256]{1,0:T(8,128)S(1)}, f32[64,256]{1,0:T(8,128)S(1)}, u32[]{:S(2)}, u32[]{:S(2)}) %collective-permute-start.17) | collective-permute-done | bytes 65568 | tf_op jit(solution)/shard_map/ppermute | solution.py:336
  67.6 0.7 finish.1
  (19 shorter events, 0.1 us)
Async XLA Ops:
  0.0 1.0 %copy-start.2 = (f32[64,4,4,128]{3,2,1,0:T(4,128)S(1)}, f32[64,4,4,128]{3,2,1,0:T(4,128)}, u32[]{:S(2)}) copy-start(f32[64,4,4,128]{3,2,1,0:T(4,128)} %param.6) | copy-start | bytes 1572868
  1.1 14.5 %collective-permute-start.1 = (f32[264,128]{1,0:T(8,128)S(1)}, f32[264,128]{1,0:T(8,128)S(1)}, u32[]{:S(2)}, u32[]{:S(2)}) collective-permute-start(f32[264,128]{1,0:T(8,128)S(1)} %get-tuple-element.29), channel_id=1, source_target_pairs={{0,8},{1,2},{2,1},{3,4},{4,3},{5,6},{6,5},{7,15},{8,0},{9,10},{10,... | collective-permute-start | bytes 405512 | tf_op jit(solution)/shard_map/ppermute | solution.py:336
  1.2 14.4 %collective-permute-start = (f32[256,128]{1,0:T(8,128)S(1)}, f32[256,128]{1,0:T(8,128)S(1)}, u32[]{:S(2)}, u32[]{:S(2)}) collective-permute-start(f32[256,128]{1,0:T(8,128)S(1)} %get-tuple-element.26.refs_1_), channel_id=1, source_target_pairs={{0,1},{1,0},{2,3},{3,2},{4,5},{5,4},{6,7},{7,6},{8,9},{9,8},{10,11... | collective-permute-start | bytes 393224 | tf_op jit(solution)/shard_map/ppermute | solution.py:336
  4.2 0.9 %copy-start.5 = (f32[2,2,2,128,32]{3,4,2,1,0:T(8,128)S(1)}, f32[2,2,2,128,32]{3,4,2,1,0:T(8,128)}, u32[]{:S(2)}) copy-start(f32[2,2,2,128,32]{3,4,2,1,0:T(8,128)} %param.10) | copy-start | bytes 393220
  5.1 14.9 %collective-permute-start.8 = (f32[128,128]{1,0:T(8,128)S(1)}, f32[128,128]{1,0:T(8,128)S(1)}, u32[]{:S(2)}, u32[]{:S(2)}) collective-permute-start(f32[128,128]{1,0:T(8,128)S(1)} %own_half.1.refs_2_.refs_0_), channel_id=1, source_target_pairs={{0,4},{1,5},{2,6},{3,7},{4,0},{5,1},{6,2},{7,3},{8,12},{9,13},{10,... | collective-permute-start | bytes 196616 | tf_op jit(solution)/shard_map/ppermute | solution.py:336
  11.4 1.0 %copy-start.3 = (f32[64,4,4,128]{3,2,1,0:T(4,128)S(1)}, f32[64,4,4,128]{3,2,1,0:T(4,128)}, u32[]{:S(2)}) copy-start(f32[64,4,4,128]{3,2,1,0:T(4,128)} %param.6) | copy-start | bytes 1572868
  12.4 1.2 %copy-start.6 = (f32[3,3,3,64,64]{4,3,2,1,0:T(8,128)S(1)}, f32[3,3,3,64,64]{4,3,2,1,0:T(8,128)}, u32[]{:S(2)}) copy-start(f32[3,3,3,64,64]{4,3,2,1,0:T(8,128)} %param.7) | copy-start | bytes 1327108
  16.3 6.2 %collective-permute-start.2 = (f32[256,128]{1,0:T(8,128)S(1)}, f32[256,128]{1,0:T(8,128)S(1)}, u32[]{:S(2)}, u32[]{:S(2)}) collective-permute-start(f32[256,128]{1,0:T(8,128)S(1)} %get-tuple-element.31), channel_id=1, source_target_pairs={{0,8},{1,9},{2,10},{3,11},{4,12},{5,13},{6,14},{7,15},{8,0},{9,1},... | collective-permute-start | bytes 393224 | tf_op jit(solution)/shard_map/ppermute | solution.py:336
  16.4 6.6 %collective-permute-start.3 = (f32[264,128]{1,0:T(8,128)S(1)}, f32[264,128]{1,0:T(8,128)S(1)}, u32[]{:S(2)}, u32[]{:S(2)}) collective-permute-start(f32[264,128]{1,0:T(8,128)S(1)} %get-tuple-element.32), channel_id=1, source_target_pairs={{0,1},{1,0},{2,3},{3,2},{4,5},{5,4},{6,7},{7,6},{8,16},{9,17},{10,... | collective-permute-start | bytes 405512 | tf_op jit(solution)/shard_map/ppermute | solution.py:336
  20.0 1.5 %copy-start = (f32[3,3,3,128,128]{4,3,2,1,0:T(8,128)S(1)}, f32[3,3,3,128,128]{4,3,2,1,0:T(8,128)}, u32[]{:S(2)}) copy-start(f32[3,3,3,128,128]{4,3,2,1,0:T(8,128)} %param.9) | copy-start | bytes 5308420
  20.0 2.0 %copy-start.1 = (f32[3,3,3,256,64]{3,4,2,1,0:T(8,128)S(1)}, f32[3,3,3,256,64]{3,4,2,1,0:T(8,128)}, u32[]{:S(2)}) copy-start(f32[3,3,3,256,64]{3,4,2,1,0:T(8,128)} %param.11) | copy-start | bytes 5308420
  20.0 5.9 %collective-permute-start.9 = (f32[288,128]{1,0:T(8,128)S(1)}, f32[288,128]{1,0:T(8,128)S(1)}, u32[]{:S(2)}, u32[]{:S(2)}) collective-permute-start(f32[288,128]{1,0:T(8,128)S(1)} %joined.4.refs_0_), channel_id=1, source_target_pairs={{0,1},{1,0},{2,3},{3,2},{4,5},{5,4},{6,7},{7,6},{8,9},{9,8},{10,11... | collective-permute-start | bytes 442376 | tf_op jit(solution)/shard_map/ppermute | solution.py:336
  22.0 1.1 %copy-start.4 = (f32[2,2,2,64,128]{4,3,2,1,0:T(8,128)S(1)}, f32[2,2,2,64,128]{4,3,2,1,0:T(8,128)}, u32[]{:S(2)}) copy-start(f32[2,2,2,64,128]{4,3,2,1,0:T(8,128)} %param.8) | copy-start | bytes 786436
  23.5 12.1 %collective-permute-start.4 = (f32[136,128]{1,0:T(8,128)S(1)}, f32[136,128]{1,0:T(8,128)S(1)}, u32[]{:S(2)}, u32[]{:S(2)}) collective-permute-start(f32[136,128]{1,0:T(8,128)S(1)} %get-tuple-element.36), channel_id=1, source_target_pairs={{0,1},{1,0},{2,3},{3,2},{4,5},{5,4},{6,7},{7,6},{8,9},{9,8},{10,11... | collective-permute-start | bytes 208904 | tf_op jit(solution)/shard_map/ppermute | solution.py:336
  24.5 11.1 %collective-permute-start.5 = (f32[128,128]{1,0:T(8,128)S(1)}, f32[128,128]{1,0:T(8,128)S(1)}, u32[]{:S(2)}, u32[]{:S(2)}) collective-permute-start(f32[128,128]{1,0:T(8,128)S(1)} %get-tuple-element.37), channel_id=1, source_target_pairs={{0,8},{1,2},{2,1},{3,4},{4,3},{5,6},{6,5},{7,15},{8,0},{9,10},{10,... | collective-permute-start | bytes 196616 | tf_op jit(solution)/shard_map/ppermute | solution.py:336
  25.9 14.5 %collective-permute-start.10 = (f32[512,128]{1,0:T(8,128)S(1)}, f32[512,128]{1,0:T(8,128)S(1)}, u32[]{:S(2)}, u32[]{:S(2)}) collective-permute-start(f32[512,128]{1,0:T(8,128)S(1)} %joined.5.refs_0_), channel_id=1, source_target_pairs={{0,3},{1,2},{2,1},{3,0},{4,7},{5,6},{6,5},{7,4},{8,11},{9,10},{10,... | collective-permute-start | bytes 786440 | tf_op jit(solution)/shard_map/ppermute | solution.py:336
  36.2 4.4 %collective-permute-start.6 = (f32[128,128]{1,0:T(8,128)S(1)}, f32[128,128]{1,0:T(8,128)S(1)}, u32[]{:S(2)}, u32[]{:S(2)}) collective-permute-start(f32[128,128]{1,0:T(8,128)S(1)} %get-tuple-element.39), channel_id=1, source_target_pairs={{0,8},{1,9},{2,10},{3,11},{4,12},{5,13},{6,14},{7,15},{8,0},{9,1},... | collective-permute-start | bytes 196616 | tf_op jit(solution)/shard_map/ppermute | solution.py:336
  36.3 5.9 %collective-permute-start.7 = (f32[128,128]{1,0:T(8,128)S(1)}, f32[128,128]{1,0:T(8,128)S(1)}, u32[]{:S(2)}, u32[]{:S(2)}) collective-permute-start(f32[128,128]{1,0:T(8,128)S(1)} %get-tuple-element.40), channel_id=1, source_target_pairs={{0,1},{1,0},{2,3},{3,2},{4,5},{5,4},{6,7},{7,6},{8,16},{9,17},{10,... | collective-permute-start | bytes 196616 | tf_op jit(solution)/shard_map/ppermute | solution.py:336
  40.5 2.0 %collective-permute-start.11 = (f32[1024,128]{1,0:T(8,128)S(1)}, f32[1024,128]{1,0:T(8,128)S(1)}, u32[]{:S(2)}, u32[]{:S(2)}) collective-permute-start(f32[1024,128]{1,0:T(8,128)S(1)} %joined.6.refs_0_), channel_id=1, source_target_pairs={{0,8},{1,9},{2,10},{3,11},{4,12},{5,13},{6,14},{7,15},{8,0},{9,1},... | collective-permute-start | bytes 1572872 | tf_op jit(solution)/shard_map/ppermute | solution.py:336
  43.1 8.7 %collective-permute-start.12 = (f32[32,256]{1,0:T(8,128)S(1)}, f32[32,256]{1,0:T(8,128)S(1)}, u32[]{:S(2)}, u32[]{:S(2)}) collective-permute-start(f32[32,256]{1,0:T(8,128)S(1)} %second_down.1.refs_0_), channel_id=1, source_target_pairs={{0,4},{1,5},{2,6},{3,7},{4,0},{5,1},{6,2},{7,3},{8,12},{9,13},{10,... | collective-permute-start | bytes 98312 | tf_op jit(solution)/shard_map/ppermute | solution.py:336
  51.8 5.5 %collective-permute-start.13 = (f32[64,256]{1,0:T(8,128)S(1)}, f32[64,256]{1,0:T(8,128)S(1)}, u32[]{:S(2)}, u32[]{:S(2)}) collective-permute-start(f32[64,256]{1,0:T(8,128)S(1)} %joined.7.refs_0_), channel_id=1, source_target_pairs={{0,3},{1,2},{2,1},{3,0},{4,7},{5,6},{6,5},{7,4},{8,11},{9,10},{10,... | collective-permute-start | bytes 196616 | tf_op jit(solution)/shard_map/ppermute | solution.py:336
  54.8 5.8 %collective-permute-start.14 = (f32[64,256]{1,0:T(8,128)S(1)}, f32[64,256]{1,0:T(8,128)S(1)}, u32[]{:S(2)}, u32[]{:S(2)}) collective-permute-start(f32[64,256]{1,0:T(8,128)S(1)} %joined.7.refs_0_), channel_id=1, source_target_pairs={{0,2},{1,3},{2,0},{3,1},{4,6},{5,7},{6,4},{7,5},{8,10},{9,11},{10,... | collective-permute-start | bytes 196616 | tf_op jit(solution)/shard_map/ppermute | solution.py:336
  54.8 5.8 %collective-permute-start.15 = (f32[64,256]{1,0:T(8,128)S(1)}, f32[64,256]{1,0:T(8,128)S(1)}, u32[]{:S(2)}, u32[]{:S(2)}) collective-permute-start(f32[64,256]{1,0:T(8,128)S(1)} %joined.7.refs_0_), channel_id=1, source_target_pairs={{0,1},{1,0},{2,3},{3,2},{4,5},{5,4},{6,7},{7,6},{8,9},{9,8},{10,11... | collective-permute-start | bytes 196616 | tf_op jit(solution)/shard_map/ppermute | solution.py:336
  61.6 1.3 %collective-permute-start.16 = (f32[64,256]{1,0:T(8,128)S(1)}, f32[64,256]{1,0:T(8,128)S(1)}, u32[]{:S(2)}, u32[]{:S(2)}) collective-permute-start(f32[64,256]{1,0:T(8,128)S(1)} %get-tuple-element.45), channel_id=1, source_target_pairs={{0,8},{1,9},{2,10},{3,11},{4,12},{5,13},{6,14},{7,15},{8,0},{9,1},... | collective-permute-start | bytes 196616 | tf_op jit(solution)/shard_map/ppermute | solution.py:336
  61.7 5.9 %collective-permute-start.17 = (f32[64,256]{1,0:T(8,128)S(1)}, f32[64,256]{1,0:T(8,128)S(1)}, u32[]{:S(2)}, u32[]{:S(2)}) collective-permute-start(f32[64,256]{1,0:T(8,128)S(1)} %get-tuple-element.46), channel_id=1, source_target_pairs={{0,1},{1,0},{2,3},{3,2},{4,5},{5,4},{6,7},{7,6},{8,16},{9,17},{10,... | collective-permute-start | bytes 196616 | tf_op jit(solution)/shard_map/ppermute | solution.py:336
